TPU v7x, 32 devices: a whole 2x2x4 slice. The times are simulated.
32 devices in a mesh: dp: 8 (over z, y), seq: 4 (over x, core).
Axes of the slice: x: 2, y: 2, z: 4, core: 2. Of those that a mesh axis runs over, the one named last changes fastest.
Arguments:
- tokens: bfloat16 [8, 1152, 1024], P('dp', 'seq'), may hold values from -6 to 6
- segment_ids: int32 [8, 1152], P('dp'), may hold values from 0 to 3, never falling along the last dimension, each value on 1 to 640 neighbouring positions
- qkv_weight: bfloat16 [1024, 3072], P(('dp', 'seq')), may hold values from -0.1875 to 0.1875
- query_bias: bfloat16 [1024], P(('dp', 'seq')), may hold values from -1.75 to 1.75
- value_bias: bfloat16 [1024], P(('dp', 'seq')), may hold values from -0.625 to 0.625
- out_weight: bfloat16 [1024, 1024], P(('dp', 'seq')), may hold values from -1 to 1
- out_bias: bfloat16 [1024], P(('dp', 'seq')), may hold values from -3 to 3
- first_gain: bfloat16 [1024], P(('dp', 'seq')), may hold values from 0.25 to 1.75
- first_shift: bfloat16 [1024], P(('dp', 'seq')), may hold values from -3 to 3
- up_weight: bfloat16 [1024, 4096], P(('dp', 'seq')), may hold values from -0.1875 to 0.1875
- up_bias: bfloat16 [4096], P(('dp', 'seq')), may hold values from -3 to 3
- down_weight: bfloat16 [4096, 1024], P(('dp', 'seq')), may hold values from -0.09375 to 0.09375
- down_bias: bfloat16 [1024], P(('dp', 'seq')), may hold values from -3 to 3
- second_gain: bfloat16 [1024], P(('dp', 'seq')), may hold values from 0.25 to 1.75
- second_shift: bfloat16 [1024], P(('dp', 'seq')), may hold values from -3 to 3
- cotangent: bfloat16 [8, 1152, 1024], P('dp', 'seq'), may hold values from -6 to 6
Outputs:
- output: bfloat16 [8, 1152, 1024], P('dp', 'seq')
- tokens_grad: bfloat16 [8, 1152, 1024], P('dp', 'seq')
- qkv_weight_grad: float32 [1024, 3072], P(('dp', 'seq'))
- query_bias_grad: float32 [1024], P(('dp', 'seq'))
- value_bias_grad: float32 [1024], P(('dp', 'seq'))
- out_weight_grad: float32 [1024, 1024], P(('dp', 'seq'))
- out_bias_grad: float32 [1024], P(('dp', 'seq'))
- first_gain_grad: float32 [1024], P(('dp', 'seq'))
- first_shift_grad: float32 [1024], P(('dp', 'seq'))
- up_weight_grad: float32 [1024, 4096], P(('dp', 'seq'))
- up_bias_grad: float32 [4096], P(('dp', 'seq'))
- down_weight_grad: float32 [4096, 1024], P(('dp', 'seq'))
- down_bias_grad: float32 [1024], P(('dp', 'seq'))
- second_gain_grad: float32 [1024], P(('dp', 'seq'))
- second_shift_grad: float32 [1024], P(('dp', 'seq'))
Inputs may be any that keep to these rules, and one draw needn't show every extreme that they name: `segment_ids`: in each sequence the document numbers never fall along the tokens; a document spans 1 to 640 tokens, and some document spans exactly 640.
All inputs are finite; a program needn't handle non-finite values.
Results may differ from a plain program's by a relative error of at most 0.014.
Values may be sent and summed in bfloat16 or wider, within the bound.
No kernel may reach another device: no remote copies, remote signals or barrier semaphores. Data moves between devices by JAX's collectives and lax.ppermute only.
A program may use at most 192 MiB of HBM per device.

v0:
```python
from functools import partial

import jax
import jax.numpy as jnp
from jax import lax
from jax.sharding import PartitionSpec as P

HEADS = 16
HEAD_DIM = 64


EPSILON = 1e-06
MASKED = -1e30
heads_per_group = 4


def matmul(left, right):
    return jnp.dot(left, right, preferred_element_type=jnp.float32)


def left_product(left, right):
    return lax.dot_general(
        left, right, (((0,), (0,)), ((), ())), preferred_element_type=jnp.float32
    )


def right_product(left, right):
    return lax.dot_general(
        left, right, (((1,), (1,)), ((), ())), preferred_element_type=jnp.float32
    )


def norm_forward(value, gain, shift):
    mean = jnp.mean(value, axis=-1, keepdims=True)
    centered = value - mean
    variance = jnp.mean(centered * centered, axis=-1, keepdims=True)
    factor = lax.rsqrt(variance + EPSILON)
    normed = centered * factor
    return (normed * gain.astype(jnp.float32) + shift.astype(jnp.float32), normed, factor)


def norm_backward(grad, normed, factor, gain):
    scaled = grad * gain.astype(jnp.float32)
    inner = jnp.mean(scaled, axis=-1, keepdims=True)
    along = jnp.mean(scaled * normed, axis=-1, keepdims=True)
    return (
        factor * (scaled - inner - normed * along),
        jnp.sum(grad * normed, axis=0),
        jnp.sum(grad, axis=0),
    )


def heads_to_rows(groups_out, count, width):
    return jnp.moveaxis(groups_out, 0, 2).reshape(count, width)


def body(
    tokens,
    segment_ids,
    qkv_weight,
    query_bias,
    value_bias,
    out_weight,
    out_bias,
    first_gain,
    first_shift,
    up_weight,
    up_bias,
    down_weight,
    down_bias,
    second_gain,
    second_shift,
    cotangent,
):
    (
        full_joint,
        full_query_bias,
        full_value_bias,
        full_out,
        full_out_bias,
        full_gain_one,
        full_shift_one,
    ) = (
        lax.all_gather(qkv_weight, ("dp", "seq"), axis=0, tiled=True),
        lax.all_gather(query_bias, ("dp", "seq"), axis=0, tiled=True),
        lax.all_gather(value_bias, ("dp", "seq"), axis=0, tiled=True),
        lax.all_gather(out_weight, ("dp", "seq"), axis=0, tiled=True),
        lax.all_gather(out_bias, ("dp", "seq"), axis=0, tiled=True),
        lax.all_gather(first_gain, ("dp", "seq"), axis=0, tiled=True),
        lax.all_gather(first_shift, ("dp", "seq"), axis=0, tiled=True),
    )
    seqs_here, local_len, width = tokens.shape
    count = seqs_here * local_len
    full_len = segment_ids.shape[1]
    rows = tokens.reshape(count, width)
    bias = jnp.concatenate(
        [full_query_bias, jnp.zeros_like(full_query_bias), full_value_bias]
    ).astype(jnp.float32)
    projected = (matmul(rows, full_joint) + bias).astype(jnp.bfloat16)
    queries = projected[:, :width].reshape(seqs_here, local_len, width)
    pairs = projected[:, width:].reshape(seqs_here, local_len, 2 * width)
    whole_pairs = lax.all_gather(pairs, "seq", axis=1, tiled=True)
    local_segments = lax.dynamic_slice_in_dim(
        segment_ids, lax.axis_index("seq") * local_len, local_len, 1
    )
    same = local_segments[:, :, None] == segment_ids[:, None, :]
    group_cols = heads_per_group * HEAD_DIM
    groups = HEADS // heads_per_group
    score_scale = HEAD_DIM ** (-0.5)

    def split_heads(source, start, length):
        return lax.dynamic_slice_in_dim(source, start, group_cols, 2).reshape(
            seqs_here, length, heads_per_group, HEAD_DIM
        )

    def head_slices(start):
        return (
            split_heads(queries, start, local_len),
            split_heads(whole_pairs, start, full_len),
            split_heads(whole_pairs, width + start, full_len),
        )

    def masked_scores(query_part, key_part, mask):
        scores = (
            jnp.einsum("sqhd,skhd->shqk", query_part, key_part, preferred_element_type=jnp.float32)
            * score_scale
        )
        return jnp.where(mask[:, None], scores, MASKED)

    def attend(index):
        query_part, key_part, value_part = head_slices(index * group_cols)
        scores = masked_scores(query_part, key_part, same)
        highest = jnp.max(scores, axis=-1, keepdims=True)
        weights = jnp.exp(scores - highest)
        total = jnp.sum(weights, axis=-1, keepdims=True)
        shares_low = (weights / total).astype(jnp.bfloat16)
        mixed_part = jnp.einsum(
            "shqk,skhd->sqhd", shares_low, value_part, preferred_element_type=jnp.float32
        )
        return (mixed_part.astype(jnp.bfloat16), highest[..., 0] + jnp.log(total[..., 0]))

    mixed_groups, log_totals = lax.map(attend, jnp.arange(groups))
    mixed = heads_to_rows(mixed_groups, count, width)
    branch = matmul(mixed, full_out) + full_out_bias.astype(jnp.float32)
    first, normed_one, factor_one = norm_forward(
        rows.astype(jnp.float32) + branch, full_gain_one, full_shift_one
    )
    first_low = first.astype(jnp.bfloat16)
    full_up, full_up_bias, full_down, full_down_bias, full_gain_two, full_shift_two = (
        lax.all_gather(up_weight, ("dp", "seq"), axis=0, tiled=True),
        lax.all_gather(up_bias, ("dp", "seq"), axis=0, tiled=True),
        lax.all_gather(down_weight, ("dp", "seq"), axis=0, tiled=True),
        lax.all_gather(down_bias, ("dp", "seq"), axis=0, tiled=True),
        lax.all_gather(second_gain, ("dp", "seq"), axis=0, tiled=True),
        lax.all_gather(second_shift, ("dp", "seq"), axis=0, tiled=True),
    )
    preact = matmul(first_low, full_up) + full_up_bias.astype(jnp.float32)
    activated, gelu_pull = jax.vjp(partial(jax.nn.gelu, approximate=False), preact)
    hidden = activated.astype(jnp.bfloat16)
    second = matmul(hidden, full_down) + full_down_bias.astype(jnp.float32)
    result, normed_two, factor_two = norm_forward(first + second, full_gain_two, full_shift_two)
    output = result.astype(jnp.bfloat16).reshape(tokens.shape)
    full_joint, full_out, full_gain_one = (
        lax.all_gather(qkv_weight, ("dp", "seq"), axis=0, tiled=True),
        lax.all_gather(out_weight, ("dp", "seq"), axis=0, tiled=True),
        lax.all_gather(first_gain, ("dp", "seq"), axis=0, tiled=True),
    )
    full_up, full_down, full_gain_two = (
        lax.all_gather(up_weight, ("dp", "seq"), axis=0, tiled=True),
        lax.all_gather(down_weight, ("dp", "seq"), axis=0, tiled=True),
        lax.all_gather(second_gain, ("dp", "seq"), axis=0, tiled=True),
    )
    grad_out = cotangent.reshape(count, width).astype(jnp.float32)
    second_grad, gain_two_grad, shift_two_grad = norm_backward(
        grad_out, normed_two, factor_two, full_gain_two
    )
    second_low = second_grad.astype(jnp.bfloat16)
    down_bias_grad = jnp.sum(second_low, axis=0, dtype=jnp.float32)
    down_grad = left_product(hidden, second_low)
    (preact_grad,) = gelu_pull(right_product(second_low, full_down))
    preact_low = preact_grad.astype(jnp.bfloat16)
    up_bias_grad = jnp.sum(preact_low, axis=0, dtype=jnp.float32)
    up_grad = left_product(first_low, preact_low)
    up_owned, up_bias_owned, down_owned, down_bias_owned, gain_two_owned, shift_two_owned = (
        lax.psum_scatter(up_grad, ("dp", "seq"), scatter_dimension=0, tiled=True),
        lax.psum_scatter(up_bias_grad, ("dp", "seq"), scatter_dimension=0, tiled=True),
        lax.psum_scatter(down_grad, ("dp", "seq"), scatter_dimension=0, tiled=True),
        lax.psum_scatter(down_bias_grad, ("dp", "seq"), scatter_dimension=0, tiled=True),
        lax.psum_scatter(gain_two_grad, ("dp", "seq"), scatter_dimension=0, tiled=True),
        lax.psum_scatter(shift_two_grad, ("dp", "seq"), scatter_dimension=0, tiled=True),
    )
    first_grad = second_grad + right_product(preact_low, full_up)
    residual_grad, gain_one_grad, shift_one_grad = norm_backward(
        first_grad, normed_one, factor_one, full_gain_one
    )
    branch_low = residual_grad.astype(jnp.bfloat16)
    out_bias_grad = jnp.sum(branch_low, axis=0, dtype=jnp.float32)
    out_grad = left_product(mixed, branch_low)
    mixed_grad = (
        right_product(branch_low, full_out)
        .astype(jnp.bfloat16)
        .reshape(seqs_here, local_len, width)
    )

    def attend_back(index):
        start = index * group_cols
        query_part, key_part, value_part = head_slices(start)
        grad_part = split_heads(mixed_grad, start, local_len)
        shares = jnp.exp(masked_scores(query_part, key_part, same) - log_totals[index][..., None])
        shares_low = shares.astype(jnp.bfloat16)
        shares_grad = jnp.einsum(
            "sqhd,skhd->shqk", grad_part, value_part, preferred_element_type=jnp.float32
        )
        inner = jnp.sum(shares * shares_grad, axis=-1, keepdims=True)
        score_low = (shares * (shares_grad - inner)).astype(jnp.bfloat16)
        query_grad = (
            jnp.einsum("shqk,skhd->sqhd", score_low, key_part, preferred_element_type=jnp.float32)
            * score_scale
        )
        key_grad = (
            jnp.einsum("shqk,sqhd->skhd", score_low, query_part, preferred_element_type=jnp.float32)
            * score_scale
        )
        value_grad = jnp.einsum(
            "shqk,sqhd->skhd", shares_low, grad_part, preferred_element_type=jnp.float32
        )
        key_local, value_local = (
            lax.psum_scatter(
                key_grad.astype(jnp.bfloat16), "seq", scatter_dimension=1, tiled=True
            ).astype(jnp.float32),
            lax.psum_scatter(
                value_grad.astype(jnp.bfloat16), "seq", scatter_dimension=1, tiled=True
            ).astype(jnp.float32),
        )
        return (
            query_grad.astype(jnp.bfloat16),
            key_local.astype(jnp.bfloat16),
            value_local.astype(jnp.bfloat16),
        )

    query_groups, key_groups, value_groups = lax.map(attend_back, jnp.arange(groups))
    query_rows = heads_to_rows(query_groups, count, width)
    value_rows = heads_to_rows(value_groups, count, width)
    projected_grad = jnp.concatenate(
        [query_rows, heads_to_rows(key_groups, count, width), value_rows], axis=1
    )
    query_bias_grad = jnp.sum(query_rows, axis=0, dtype=jnp.float32)
    value_bias_grad = jnp.sum(value_rows, axis=0, dtype=jnp.float32)
    joint_grad = left_product(rows, projected_grad)
    tokens_grad = (
        (residual_grad + right_product(projected_grad, full_joint))
        .astype(jnp.bfloat16)
        .reshape(tokens.shape)
    )
    (
        joint_owned,
        query_bias_owned,
        value_bias_owned,
        out_owned,
        out_bias_owned,
        gain_one_owned,
        shift_one_owned,
    ) = (
        lax.psum_scatter(joint_grad, ("dp", "seq"), scatter_dimension=0, tiled=True),
        lax.psum_scatter(query_bias_grad, ("dp", "seq"), scatter_dimension=0, tiled=True),
        lax.psum_scatter(value_bias_grad, ("dp", "seq"), scatter_dimension=0, tiled=True),
        lax.psum_scatter(out_grad, ("dp", "seq"), scatter_dimension=0, tiled=True),
        lax.psum_scatter(out_bias_grad, ("dp", "seq"), scatter_dimension=0, tiled=True),
        lax.psum_scatter(gain_one_grad, ("dp", "seq"), scatter_dimension=0, tiled=True),
        lax.psum_scatter(shift_one_grad, ("dp", "seq"), scatter_dimension=0, tiled=True),
    )
    return (
        output,
        tokens_grad,
        joint_owned,
        query_bias_owned,
        value_bias_owned,
        out_owned,
        out_bias_owned,
        gain_one_owned,
        shift_one_owned,
        up_owned,
        up_bias_owned,
        down_owned,
        down_bias_owned,
        gain_two_owned,
        shift_two_owned,
    )


def solution(mesh):
    return jax.shard_map(
        body,
        mesh=mesh,
        in_specs=(
            P("dp", "seq", None),
            P("dp", None),
            P(("dp", "seq"), None),
            P(("dp", "seq")),
            P(("dp", "seq")),
            P(("dp", "seq"), None),
            P(("dp", "seq")),
            P(("dp", "seq")),
            P(("dp", "seq")),
            P(("dp", "seq"), None),
            P(("dp", "seq")),
            P(("dp", "seq"), None),
            P(("dp", "seq")),
            P(("dp", "seq")),
            P(("dp", "seq")),
            P("dp", "seq", None),
        ),
        out_specs=(
            P("dp", "seq", None),
            P("dp", "seq", None),
            P(("dp", "seq"), None),
            P(("dp", "seq")),
            P(("dp", "seq")),
            P(("dp", "seq"), None),
            P(("dp", "seq")),
            P(("dp", "seq")),
            P(("dp", "seq")),
            P(("dp", "seq"), None),
            P(("dp", "seq")),
            P(("dp", "seq"), None),
            P(("dp", "seq")),
            P(("dp", "seq")),
            P(("dp", "seq")),
        ),
        check_vma=False,
    )
```

profile of v0, /device:TPU:0, one launch (start us, length us, event | category | flops | bytes accessed | tf_op | source)
XLA Modules:
  0.0 1358.0 jit_solution(12682063940617955000)
XLA Ops:
  14.7 42.6 %all-reduce.18 = (bf16[1024]{0:T(1024)(128)(2,1)S(1)}, bf16[1024]{0:T(1024)(128)(2,1)S(1)}, bf16[1024]{0:T(1024)(128)(2,1)S(1)}, bf16[1024]{0:T(1024)(128)(2,1)S...) all-reduce(bf16[1024]{0:T(1024)(128)(2,1)S(1)} %dynamic-update-slic, ...), channel_id=1, replica_groups=mesh['dp'=8,'seq'=4] {'dp','seq'}, use_global_device_ids=true, to_apply=%add.1 | all-reduce | flops 8192 | bytes 32768
  57.3 26.0 %all-gather.8.cloned.1.call-done = bf16[1024,3072]{1,0:T(8,128)(2,1)} async-done(((bf16[32,3072]{1,0:T(8,128)(2,1)}), bf16[1024,3072]{1,0:T(8,128)(2,1)}) %all-gather.8.cloned.1.call-update) | async-done | bytes 6291472 | tf_op jit(solution)/shard_map/all_gather | solution.py:84
  83.2 5.0 fusion.28
  91.4 39.0 %all-gather.1 = bf16[32,1,128]{2,1,0:T(2,128)(2,1)S(1)} all-gather(bf16[1,1,128]{2,1,0:T(2,128)(2,1)S(1)} %bitcast.226), channel_id=1, replica_groups=mesh['dp'=8,'seq'=4] {'dp','seq'}, dimensions={0}, use_global_device_ids=true | all-gather | bytes 8448 | tf_op jit(solution)/shard_map/all_gather | solution.py:151
  131.8 6.8 copy.37
  138.6 30.5 %while.32 = (s32[]{:T(128)}, bf16[4,1,288,4,64]{2,4,3,1,0:T(8,128)(2,1)S(1)}, f32[4,1,4,288]{3,2,1,0:T(4,128)S(1)}, s32[4]{0:T(128)S(1)}, bf16[1,1152,2048]{1,2,...) while((s32[]{:T(128)}, ...), condition=%wide.region_3.4_spmd.clone, body=%wide.region_0.3_spmd.clone.sunk | while | flops 350759808 | bytes 20817292 | solution.py:142
  169.1 15.8 %all-gather.10.cloned.1.call-done = bf16[1024,1024]{1,0:T(8,128)(2,1)} async-done(((bf16[32,1024]{1,0:T(8,128)(2,1)}), bf16[1024,1024]{1,0:T(8,128)(2,1)}) %all-gather.10.cloned.1.call-update) | async-done | bytes 2097168 | tf_op jit(solution)/shard_map/all_gather | solution.py:87
  187.7 76.2 %all-gather.12.cloned.1.call-done = bf16[1024,4096]{1,0:T(8,128)(2,1)} async-done(((bf16[32,4096]{1,0:T(8,128)(2,1)}), bf16[1024,4096]{1,0:T(8,128)(2,1)}) %all-gather.12.cloned.1.call-update) | async-done | bytes 8388624 | tf_op jit(solution)/shard_map/all_gather | solution.py:150
  263.9 17.1 %multiply_convert_fusion.1 = (bf16[288,4096]{1,0:T(8,128)(2,1)}, f32[288,4096]{1,0:T(8,128)}, f32[288,4096]{1,0:T(8,128)}) fusion(f32[4096]{0:T(1024)S(1)} %bitcast.225, bf16[1024,4096]{1,0:T(8,128)(2,1)} %all-gather.12.cloned.1.call-done, f32[288,1024]{1,0:T(8,128)S(1)} %get-tuple-element.431, f32[1024]{0:T(1024)S(1)} %convert_element_type.161, ...), kind=kOutput, calls=%fused_computation.43 | convolution fusion | flops 2495250432 | bytes 21391616 | tf_op jit(solution)/shard_map/dot_general | solution.py:18
  281.1 61.7 %all-gather.14.cloned.1.call-done = bf16[4096,1024]{1,0:T(8,128)(2,1)} async-done(((bf16[128,1024]{1,0:T(8,128)(2,1)}), bf16[4096,1024]{1,0:T(8,128)(2,1)}) %all-gather.14.cloned.1.call-update) | async-done | bytes 8388624 | tf_op jit(solution)/shard_map/all_gather | solution.py:152
  342.7 6.1 fusion.65
  352.1 12.0 convert_reduce_fusion
  364.2 7.0 multiply_reduce_fusion.1
  372.1 3.2 fusion.49
  375.3 3.2 fusion.38
  381.5 295.2 %while.33 = (s32[]{:T(128)}, bf16[4,1,288,4,64]{2,4,3,1,0:T(8,128)(2,1)}, bf16[4,1,288,4,64]{2,4,3,1,0:T(8,128)(2,1)}, bf16[4,1,288,4,64]{2,4,3,1,0:T(8,128)(2,1...) while((s32[]{:T(128)}, ...), condition=%wide.region_16.17_spmd.clone, body=%wide.region_12.16_spmd.clone.sunk | while | flops 862653312 | bytes 96834232 | solution.py:241
  387.9 3.2 fusion.129
  392.1 4.8 multiply_reduce_fusion.7
  406.9 3.9 fusion.131
  410.8 3.2 copy.56
  418.6 9.0 reduce-scatter.27.cloned.1.call-done
  429.0 23.4 %reduce-scatter.25.cloned.1.call-done = bf16[288,256]{1,0:T(8,128)(2,1)} async-done(((bf16[1152,256]{1,0:T(8,128)(2,1)}), bf16[288,256]{1,0:T(8,128)(2,1)}) %reduce-scatter.25.cloned.1.call-update) | async-done | bytes 147472 | tf_op jit(solution)/shard_map/while
  460.5 3.2 fusion.129
  464.7 4.8 multiply_reduce_fusion.7
  479.5 3.9 fusion.131
  491.2 10.5 reduce-scatter.27.cloned.1.call-done
  503.0 23.5 %reduce-scatter.25.cloned.1.call-done = bf16[288,256]{1,0:T(8,128)(2,1)} async-done(((bf16[1152,256]{1,0:T(8,128)(2,1)}), bf16[288,256]{1,0:T(8,128)(2,1)}) %reduce-scatter.25.cloned.1.call-update) | async-done | bytes 147472 | tf_op jit(solution)/shard_map/while
  534.5 3.2 fusion.129
  538.7 4.8 multiply_reduce_fusion.7
  553.5 3.9 fusion.131
  557.5 3.2 copy.56
  565.2 10.5 reduce-scatter.27.cloned.1.call-done
  577.1 23.5 %reduce-scatter.25.cloned.1.call-done = bf16[288,256]{1,0:T(8,128)(2,1)} async-done(((bf16[1152,256]{1,0:T(8,128)(2,1)}), bf16[288,256]{1,0:T(8,128)(2,1)}) %reduce-scatter.25.cloned.1.call-update) | async-done | bytes 147472 | tf_op jit(solution)/shard_map/while
  608.6 3.2 fusion.129
  612.8 4.8 multiply_reduce_fusion.7
  627.6 3.9 fusion.131
  639.3 10.5 reduce-scatter.27.cloned.1.call-done
  651.1 23.4 %reduce-scatter.25.cloned.1.call-done = bf16[288,256]{1,0:T(8,128)(2,1)} async-done(((bf16[1152,256]{1,0:T(8,128)(2,1)}), bf16[288,256]{1,0:T(8,128)(2,1)}) %reduce-scatter.25.cloned.1.call-update) | async-done | bytes 147472 | tf_op jit(solution)/shard_map/while
  678.3 10.8 convolution_bitcast_fusion
  689.1 12.6 copy.43
  702.9 10.0 fusion.58
  714.2 9.8 fusion.52
  725.9 40.9 %all-reduce.17 = (f32[1024]{0:T(1024)S(1)}, f32[1024]{0:T(1024)S(1)}, f32[1024]{0:T(1024)S(1)}, f32[1024]{0:T(1024)S(1)}, f32[1024]{0:T(1024)S(1)}, /*index=5*/f...) all-reduce(f32[1024]{0:T(1024)S(1)} %reduce_sum.184, ...), channel_id=6, replica_groups=mesh['dp'=8,'seq'=4] {'dp','seq'}, use_global_device_ids=true, to_apply=%region_19.20.clone | all-reduce | flops 12288 | bytes 98304
  772.1 6.6 fusion.37
  778.7 42.6 %reduce-scatter.17.cloned.1.call-done = f32[32,1024]{1,0:T(8,128)} async-done(((f32[1024,1024]{1,0:T(8,128)}), f32[32,1024]{1,0:T(8,128)}) %reduce-scatter.17.cloned.1.call-update) | async-done | bytes 131088 | tf_op jit(solution)/shard_map/reduce_scatter | solution.py:267
  821.3 157.7 %reduce-scatter.23.cloned.1.call-done = f32[32,3072]{1,0:T(8,128)} async-done(((f32[1024,3072]{1,0:T(8,128)}), f32[32,3072]{1,0:T(8,128)}) %reduce-scatter.23.cloned.1.call-update) | async-done | bytes 393232
  979.1 184.7 %reduce-scatter.19.cloned.1.call-done = f32[32,4096]{1,0:T(8,128)} async-done(((f32[1024,4096]{1,0:T(8,128)}), f32[32,4096]{1,0:T(8,128)}) %reduce-scatter.19.cloned.1.call-update) | async-done | bytes 524304 | tf_op jit(solution)/shard_map/reduce_scatter | solution.py:185
  1163.8 187.5 %reduce-scatter.21.cloned.1.call-done = f32[128,1024]{1,0:T(8,128)} async-done(((f32[4096,1024]{1,0:T(8,128)}), f32[128,1024]{1,0:T(8,128)}) %reduce-scatter.21.cloned.1.call-update) | async-done | bytes 524304 | tf_op jit(solution)/shard_map/reduce_scatter | solution.py:187
  (294 shorter events, 155.6 us)
Async XLA Ops:
  7.2 76.1 %all-gather.8.cloned.1.call-start = ((), (), s32[]{:S(2)}) async-start(), calls=%async_computation.6 | async-start | bytes 6488064 | tf_op jit(solution)/shard_map/all_gather | solution.py:84
  7.9 123.8 %all-gather.16.cloned.1.call-start = ((), (), s32[]{:S(2)}) async-start(), calls=%async_computation.13 | async-start | bytes 5898240 | tf_op jit(solution)/shard_map/all_gather | solution.py:102
  57.2 34.0 %copy-start.19 = (s32[1,1152]{1,0:T(1,128)S(1)}, s32[1,1152]{1,0:T(1,128)}, u32[]{:S(2)}) copy-start(s32[1,1152]{1,0:T(1,128)} %param.21) | copy-start | bytes 13828
  57.2 34.1 %copy-start.22 = (bf16[128]{0:T(256)(128)(2,1)S(1)}, bf16[128]{0:T(256)(128)(2,1)}, u32[]{:S(2)}) copy-start(bf16[128]{0:T(256)(128)(2,1)} %param.30) | copy-start | bytes 772
  89.4 95.5 %all-gather.10.cloned.1.call-start = ((), (), s32[]{:S(2)}) async-start(), calls=%async_computation.7 | async-start | bytes 2162688 | tf_op jit(solution)/shard_map/all_gather | solution.py:87
  90.1 173.8 %all-gather.12.cloned.1.call-start = ((), (), s32[]{:S(2)}) async-start(), calls=%async_computation.8 | async-start | bytes 8650752 | tf_op jit(solution)/shard_map/all_gather | solution.py:150
  90.7 252.0 %all-gather.14.cloned.1.call-start = ((), (), s32[]{:S(2)}) async-start(), calls=%async_computation.9 | async-start | bytes 8650752 | tf_op jit(solution)/shard_map/all_gather | solution.py:152
  138.6 46.3 %copy-start.12 = (bf16[1,288,1024]{2,1,0:T(8,128)(2,1)S(1)}, bf16[1,288,1024]{2,1,0:T(8,128)(2,1)}, u32[]{:S(2)}) copy-start(bf16[1,288,1024]{2,1,0:T(8,128)(2,1)} %param.20) | copy-start | bytes 1769476
  187.4 183.7 %copy-start.3 = (f32[288,1024]{1,0:T(8,128)}, f32[288,1024]{1,0:T(8,128)S(1)}, u32[]{:S(2)}) copy-start(f32[288,1024]{1,0:T(8,128)S(1)} %get-tuple-element.431) | copy-start | bytes 3538948
  342.7 9.4 slice-start.2
  342.7 6.4 copy-start.7
  342.7 9.4 slice-start.3
  352.1 12.0 copy-start.10
  364.2 7.0 copy-start.14
  372.1 3.2 copy-start.9
  381.9 45.8 %reduce-scatter.27.cloned.1.call-start = ((), (), s32[]{:S(2)}) async-start(), calls=%async_computation.16 | async-start | bytes 737280 | tf_op jit(solution)/shard_map/while
  385.9 11.0 copy-start.1
  391.8 5.1 slice-start
  392.1 4.9 slice-start.1
  396.9 2.3 copy-start
  397.0 2.3 copy-start.2
  406.9 45.6 %reduce-scatter.25.cloned.1.call-start = ((), (), s32[]{:S(2)}) async-start(), calls=%async_computation.15 | async-start | bytes 737280 | tf_op jit(solution)/shard_map/while
  454.6 47.1 %reduce-scatter.27.cloned.1.call-start = ((), (), s32[]{:S(2)}) async-start(), calls=%async_computation.16 | async-start | bytes 737280 | tf_op jit(solution)/shard_map/while
  458.5 11.0 copy-start.1
  464.4 5.1 slice-start
  464.7 4.9 slice-start.1
  469.6 2.3 copy-start
  469.6 2.3 copy-start.2
  479.5 47.0 %reduce-scatter.25.cloned.1.call-start = ((), (), s32[]{:S(2)}) async-start(), calls=%async_computation.15 | async-start | bytes 737280 | tf_op jit(solution)/shard_map/while
  528.6 47.1 %reduce-scatter.27.cloned.1.call-start = ((), (), s32[]{:S(2)}) async-start(), calls=%async_computation.16 | async-start | bytes 737280 | tf_op jit(solution)/shard_map/while
  532.5 11.0 copy-start.1
  538.5 5.1 slice-start
  538.7 4.9 slice-start.1
  543.6 2.3 copy-start
  543.6 2.3 copy-start.2
  553.5 47.0 %reduce-scatter.25.cloned.1.call-start = ((), (), s32[]{:S(2)}) async-start(), calls=%async_computation.15 | async-start | bytes 737280 | tf_op jit(solution)/shard_map/while
  602.6 47.1 %reduce-scatter.27.cloned.1.call-start = ((), (), s32[]{:S(2)}) async-start(), calls=%async_computation.16 | async-start | bytes 737280 | tf_op jit(solution)/shard_map/while
  606.6 11.0 copy-start.1
  612.5 5.1 slice-start
  612.8 4.9 slice-start.1
  617.6 2.3 copy-start
  617.7 2.3 copy-start.2
  627.6 47.0 %reduce-scatter.25.cloned.1.call-start = ((), (), s32[]{:S(2)}) async-start(), calls=%async_computation.15 | async-start | bytes 737280 | tf_op jit(solution)/shard_map/while
  676.7 144.6 %reduce-scatter.17.cloned.1.call-start = ((), (), s32[]{:S(2)}) async-start(), calls=%async_computation.10 | async-start | bytes 4325376 | tf_op jit(solution)/shard_map/reduce_scatter | solution.py:267
  677.3 301.8 %reduce-scatter.23.cloned.1.call-start = ((), (), s32[]{:S(2)}) async-start(), calls=%async_computation.14 | async-start | bytes 12976128
  701.7 462.1 %reduce-scatter.19.cloned.1.call-start = ((), (), s32[]{:S(2)}) async-start(), calls=%async_computation.11 | async-start | bytes 17301504 | tf_op jit(solution)/shard_map/reduce_scatter | solution.py:185
  713.0 638.3 %reduce-scatter.21.cloned.1.call-start = ((), (), s32[]{:S(2)}) async-start(), calls=%async_computation.12 | async-start | bytes 17301504 | tf_op jit(solution)/shard_map/reduce_scatter | solution.py:187
  724.1 1.8 copy-start.17
  (11 other events, 16.6 us)
Sparse Core Ops, SparseCore 0:
  10.9 72.3 all-gather.7
  89.5 36.0 all-gather.15
  128.5 56.3 all-gather.9
  187.6 76.2 all-gather.11
  266.6 76.0 all-gather.13
  407.0 20.6 reduce-scatter.26
  430.3 22.0 reduce-scatter.24
  479.6 22.0 reduce-scatter.26
  504.3 22.0 reduce-scatter.24
  553.6 22.0 reduce-scatter.26
  578.4 22.0 reduce-scatter.24
  627.7 22.0 reduce-scatter.26
  652.5 22.0 reduce-scatter.24
  680.1 141.2 reduce-scatter.16
  827.8 151.2 reduce-scatter.22
  981.9 181.8 reduce-scatter.18
  1166.6 184.6 reduce-scatter.20
where the time goes:
time: 1360 us
  waiting for transfers between devices  890 us (65%)
  matrix products  165 us (12%)
  local copies, waits for them, and re-layouts  138 us (10%)
  blocking collectives  123 us (9%)
  loops' own time  14.4 us (1%)
  between operations  14.4 us (1%)
  other arithmetic  13.7 us (1%)
    reduce_scatter x1, waiting for transfers between devices, body(): lax.psum_scatter(down_grad, ('dp', 'seq'), scatter_dimension=0, tiled=True)  187 us
    reduce_scatter x1, waiting for transfers between devices, body(): lax.psum_scatter(up_grad, ('dp', 'seq'), scatter_dimension=0, tiled=True)  185 us
    unnamed x10, waiting for transfers between devices  161 us
    while x16, waiting for transfers between devices  134 us
    unnamed x2, blocking collectives  83.5 us
    all_gather x1, waiting for transfers between devices, body(): lax.all_gather(up_weight, ('dp', 'seq'), axis=0, tiled=True)  76.2 us
    while x72, local copies, waits for them, and re-layouts  66.2 us
    all_gather x1, waiting for transfers between devices, body(): lax.all_gather(down_weight, ('dp', 'seq'), axis=0, tiled=True)  61.7 us
  transfers between devices with their start and end apart: 17, of which 16 were waited for; matrix products, arithmetic and copies ran while one was open for 13% of the time, Pallas kernels for 0%

commit v1 on v0

v1 whole, which is shorter than its diff:
```python
from functools import partial

import jax
import jax.numpy as jnp
from jax import lax
from jax.experimental import pallas as pl
from jax.experimental.pallas import tpu as pltpu
from jax.sharding import PartitionSpec as P

HEADS = 16
HEAD_DIM = 64
EPSILON = 1e-06
MASKED = -1e30
CORES = 2
F32 = jnp.float32
BF16 = jnp.bfloat16
DN_T = (((1,), (1,)), ((), ()))
DN_L = (((0,), (0,)), ((), ()))


def matmul(left, right):
    return jnp.dot(left, right, preferred_element_type=F32)


def left_product(left, right):
    return lax.dot_general(left, right, DN_L, preferred_element_type=F32)


def right_product(left, right):
    return lax.dot_general(left, right, DN_T, preferred_element_type=F32)


def norm_forward(value, gain, shift):
    mean = jnp.mean(value, axis=-1, keepdims=True)
    centered = value - mean
    variance = jnp.mean(centered * centered, axis=-1, keepdims=True)
    factor = lax.rsqrt(variance + EPSILON)
    normed = centered * factor
    return (normed * gain + shift, normed, factor)


def norm_backward(grad, normed, factor, gain):
    scaled = grad * gain
    inner = jnp.mean(scaled, axis=-1, keepdims=True)
    along = jnp.mean(scaled * normed, axis=-1, keepdims=True)
    return (
        factor * (scaled - inner - normed * along),
        jnp.sum(grad * normed, axis=0),
        jnp.sum(grad, axis=0),
    )


class Place:
    def __init__(self, dp, seq):
        self.dp, self.seq = dp, seq
        self.nx = seq // CORES
        self.ny = min(self.nx, dp)
        self.nz = dp // self.ny
        d = lax.axis_index("dp")
        s = lax.axis_index("seq")
        self.d, self.s = d, s
        self.z, self.y = d // self.ny, d % self.ny
        self.x, self.c = s // CORES, s % CORES

    def core(self, a):
        return lax.ppermute(a, "seq", [(i, i ^ 1) for i in range(self.seq)])

    def to_x(self, a, k):
        n = self.nx
        return lax.ppermute(
            a,
            "seq",
            [(i, ((i // CORES + k) % n) * CORES + i % CORES) for i in range(self.seq)],
        )

    def to_y(self, a, k):
        n = self.ny
        return lax.ppermute(
            a, "dp", [(i, i // n * n + (i % n + k) % n) for i in range(self.dp)]
        )

    def to_z(self, a, k):
        n, m = self.nz, self.ny
        return lax.ppermute(
            a, "dp", [(i, (i // m + k) % n * m + i % m) for i in range(self.dp)]
        )

    def pair(self, own, other, axis):
        first = jnp.where(self.c == 0, own, other)
        second = jnp.where(self.c == 0, other, own)
        return jnp.concatenate([first, second], axis=axis)


def put(buffer, block, index):
    return lax.dynamic_update_slice_in_dim(buffer, block[None], index, 0)


def take(buffer, index):
    return lax.dynamic_index_in_dim(buffer, index, 0, keepdims=False)


def exchange_seq(place, blocks):
    n = place.nx
    view = blocks.reshape(n, CORES, *blocks.shape[1:])
    out = jnp.zeros((n, CORES, *blocks.shape[1:]), blocks.dtype)
    for k in range(n):
        peer = (place.x + k) % n
        send = take(view, peer)
        if k:
            send = place.to_x(send, k)
        source = (place.x - k) % n
        mine = take(send, place.c)
        other = place.core(take(send, 1 - place.c))
        out = put(out, place.pair(mine[None], other[None], 0), source)
    return out.reshape(blocks.shape)


def gather_dp(place, block):
    ny, nz = place.ny, place.nz
    out = jnp.zeros((nz * ny, *block.shape), block.dtype)
    here = block
    for k in range(nz):
        z = (place.z - k) % nz
        out = put(out, here, z * ny + place.y)
        for j in range(1, ny):
            out = put(out, place.to_y(here, j), z * ny + (place.y - j) % ny)
        if k < nz - 1:
            here = place.to_z(here, 1)
    return out.reshape(nz * ny * block.shape[0], *block.shape[1:])


def scatter_dp(place, grads):
    ny, nz = place.ny, place.nz
    view = grads.astype(BF16).reshape(nz * ny, grads.shape[0] // (nz * ny), *grads.shape[1:])
    total = None
    for k in range(1, nz + 1):
        z = (place.z - k) % nz
        part = take(view, z * ny + place.y).astype(F32)
        for j in range(1, ny):
            sent = place.to_y(take(view, z * ny + (place.y + j) % ny), j)
            part = part + sent.astype(F32)
        if total is not None:
            part = part + place.to_z(total.astype(BF16), 1).astype(F32)
        total = part
    return total


def all_sum(place, value):
    for axis, size in (("seq", place.seq), ("dp", place.dp)):
        bit = 1
        while bit < size:
            value = value + lax.ppermute(value, axis, [(i, i ^ bit) for i in range(size)])
            bit *= 2
    return value


def rows_all(place, rows):
    out = []
    for k in range(place.nx):
        here = rows if k == 0 else place.to_x(rows, (place.nx - k) % place.nx)
        out.append(jnp.concatenate([here, place.core(here)], axis=0))
    return out


def rows_sum(place, parts):
    total = None
    for k in reversed(range(place.nx)):
        low = parts[k].astype(BF16)
        half = low.shape[0] // 2
        both = low[:half].astype(F32) + place.core(low[half:]).astype(F32)
        if k:
            both = place.to_x(both.astype(BF16), k).astype(F32)
        total = both if total is None else total + both
    return total


BLOCK = 384


def attend_kernel(heads, bounds, qkv_ref, seg_row, seg_col, mixed_ref, log_ref):
    length = qkv_ref.shape[0]
    width = heads * HEAD_DIM
    i = pl.program_id(0)
    start = pl.multiple_of(i * BLOCK, BLOCK)
    cols = pl.ds(start, BLOCK)
    seg_q = seg_row[:, cols]
    queries = [
        qkv_ref[cols, h * HEAD_DIM : (h + 1) * HEAD_DIM] * BF16(HEAD_DIM**-0.5)
        for h in range(heads)
    ]

    def step(j, carry):
        rows = pl.ds(pl.multiple_of(j * BLOCK, BLOCK), BLOCK)
        same = seg_col[rows, :] == seg_q
        out = []
        for h in range(heads):
            high, total, acc = carry[h]
            keys = qkv_ref[rows, width + h * HEAD_DIM : width + (h + 1) * HEAD_DIM]
            values = qkv_ref[rows, 2 * width + h * HEAD_DIM : 2 * width + (h + 1) * HEAD_DIM]
            scores = lax.dot_general(keys, queries[h], DN_T, preferred_element_type=F32)
            scores = jnp.where(same, scores, MASKED)
            new = jnp.maximum(high, jnp.max(scores, axis=0, keepdims=True))
            weights = jnp.exp(scores - new)
            fade = jnp.exp(high - new)
            total = total * fade + jnp.sum(weights, axis=0, keepdims=True)
            acc = acc * fade + lax.dot_general(
                values, weights.astype(BF16), DN_L, preferred_element_type=F32
            )
            out.append((new, total, acc))
        return tuple(out)

    first = tuple(
        (
            jnp.full((1, BLOCK), MASKED, F32),
            jnp.zeros((1, BLOCK), F32),
            jnp.zeros((HEAD_DIM, BLOCK), F32),
        )
        for _ in range(heads)
    )
    done = lax.fori_loop(bounds[i], bounds[i + length // BLOCK], step, first)
    mixed = jnp.concatenate([acc / total for _, total, acc in done], axis=0)
    mixed_ref[...] = mixed.T.astype(BF16)
    log_ref[...] = jnp.concatenate([high + jnp.log(total) for high, total, _ in done], axis=0)


def attend_back_kernel(
    heads, bounds, qkv_ref, mixed_ref, grad_ref, log_ref, seg_row, seg_col, out_ref, acc_ref
):
    length = qkv_ref.shape[0]
    width = heads * HEAD_DIM
    scale = HEAD_DIM**-0.5
    i = pl.program_id(0)

    @pl.when(i == 0)
    def _():
        acc_ref[...] = jnp.zeros_like(acc_ref)

    start = pl.multiple_of(i * BLOCK, BLOCK)
    cols = pl.ds(start, BLOCK)
    seg_q = seg_row[:, cols]
    grads_all = grad_ref[cols, :]
    along = (grads_all.astype(F32) * mixed_ref[cols, :].astype(F32)).T
    along = [
        jnp.sum(along[h * HEAD_DIM : (h + 1) * HEAD_DIM], axis=0, keepdims=True)
        for h in range(heads)
    ]
    logs = [log_ref[h : h + 1, cols] for h in range(heads)]
    queries = [
        qkv_ref[cols, h * HEAD_DIM : (h + 1) * HEAD_DIM] * BF16(scale) for h in range(heads)
    ]
    grads = [grads_all[:, h * HEAD_DIM : (h + 1) * HEAD_DIM] for h in range(heads)]

    def step(j, carry):
        rows = pl.ds(pl.multiple_of(j * BLOCK, BLOCK), BLOCK)
        same = seg_col[rows, :] == seg_q
        out, key_parts, value_parts = [], [], []
        for h in range(heads):
            keys = qkv_ref[rows, width + h * HEAD_DIM : width + (h + 1) * HEAD_DIM]
            values = qkv_ref[rows, 2 * width + h * HEAD_DIM : 2 * width + (h + 1) * HEAD_DIM]
            scores = lax.dot_general(keys, queries[h], DN_T, preferred_element_type=F32)
            shares = jnp.exp(jnp.where(same, scores, MASKED) - logs[h])
            shares_grad = lax.dot_general(values, grads[h], DN_T, preferred_element_type=F32)
            score_low = (shares * (shares_grad - along[h])).astype(BF16)
            value_parts.append(matmul(shares.astype(BF16), grads[h]))
            key_parts.append(matmul(score_low, queries[h]))
            out.append(
                carry[h] + lax.dot_general(keys, score_low, DN_L, preferred_element_type=F32)
            )
        acc_ref[rows, :width] += jnp.concatenate(key_parts, axis=1)
        acc_ref[rows, width:] += jnp.concatenate(value_parts, axis=1)
        return tuple(out)

    first = tuple(jnp.zeros((HEAD_DIM, BLOCK), F32) for _ in range(heads))
    done = lax.fori_loop(bounds[i], bounds[i + length // BLOCK], step, first)
    out_ref[cols, :width] = (jnp.concatenate(done, axis=0) * scale).T.astype(BF16)

    @pl.when(i == length // BLOCK - 1)
    def _():
        out_ref[:, width:] = acc_ref[...].astype(BF16)


VMEM = pl.BlockSpec(memory_space=pltpu.VMEM)


def attend(qkv, seg_row, seg_col, bounds, heads):
    length = qkv.shape[0]
    width = heads * HEAD_DIM
    return pl.pallas_call(
        partial(attend_kernel, heads),
        grid_spec=pltpu.PrefetchScalarGridSpec(
            num_scalar_prefetch=1,
            grid=(length // BLOCK,),
            in_specs=[VMEM, VMEM, VMEM],
            out_specs=[
                pl.BlockSpec((BLOCK, width), lambda i, b: (i, 0)),
                pl.BlockSpec((heads, BLOCK), lambda i, b: (0, i)),
            ],
        ),
        out_shape=[
            jax.ShapeDtypeStruct((length, width), BF16),
            jax.ShapeDtypeStruct((heads, length), F32),
        ],
        compiler_params=pltpu.CompilerParams(vmem_limit_bytes=40 << 20),
        cost_estimate=pl.CostEstimate(
            flops=4 * length * length * width,
            bytes_accessed=8 * length * width,
            transcendentals=length * length * heads,
        ),
    )(bounds, qkv, seg_row, seg_col)


def attend_back(qkv, mixed, grad, logs, seg_row, seg_col, bounds, heads):
    length = qkv.shape[0]
    width = heads * HEAD_DIM
    return pl.pallas_call(
        partial(attend_back_kernel, heads),
        grid_spec=pltpu.PrefetchScalarGridSpec(
            num_scalar_prefetch=1,
            grid=(length // BLOCK,),
            in_specs=[VMEM] * 6,
            out_specs=VMEM,
            scratch_shapes=[pltpu.VMEM((length, 2 * width), F32)],
        ),
        out_shape=jax.ShapeDtypeStruct((length, 3 * width), BF16),
        compiler_params=pltpu.CompilerParams(vmem_limit_bytes=40 << 20),
        cost_estimate=pl.CostEstimate(
            flops=10 * length * length * width,
            bytes_accessed=16 * length * width,
            transcendentals=length * length * heads,
        ),
    )(bounds, qkv, mixed, grad, logs, seg_row, seg_col)


def gelu_pair(preact):
    half = 0.5 + 0.5 * lax.erf(preact * (2.0**-0.5))
    slope = half + preact * jnp.exp(-0.5 * preact * preact) * 0.3989422804014327
    return (preact * half).astype(BF16), slope.astype(BF16)


def body(
    dp,
    seq,
    tokens,
    segment_ids,
    qkv_weight,
    query_bias,
    value_bias,
    out_weight,
    out_bias,
    first_gain,
    first_shift,
    up_weight,
    up_bias,
    down_weight,
    down_bias,
    second_gain,
    second_shift,
    cotangent,
):
    place = Place(dp, seq)
    everyone = dp * seq
    me = place.d * seq + place.s
    _, count, width = tokens.shape
    hidden_own = up_weight.shape[1] // seq
    heads = HEADS // seq
    head_cols = heads * HEAD_DIM
    shard = qkv_weight.shape[0]
    ff_shard = down_weight.shape[0]
    length = segment_ids.shape[1]
    rows = tokens.reshape(count, width)

    qkv_blocks = qkv_weight.reshape(shard, 3, seq, head_cols).transpose(2, 0, 1, 3)
    qkv_block = exchange_seq(place, qkv_blocks.reshape(seq, shard, 3 * head_cols))
    full_qkv = gather_dp(place, qkv_block.reshape(seq * shard, 3 * head_cols))

    smalls = (query_bias, value_bias, out_bias, first_gain, first_shift, down_bias, second_gain, second_shift)
    packed = jnp.concatenate([v.reshape(1, shard) for v in smalls] + [up_bias.reshape(-1, shard)], axis=0)
    packed = all_sum(
        place, put(jnp.zeros((everyone, *packed.shape), F32), packed.astype(F32), me)
    )
    vectors = packed[:, : len(smalls)].transpose(1, 0, 2).reshape(len(smalls), 1, width)
    full_query, full_value, bias_out, gain_one, shift_one, bias_down, gain_two, shift_two = vectors
    up_bias_all = packed[:, len(smalls) :].reshape(dp, seq, ff_shard)
    bias_up = lax.dynamic_index_in_dim(up_bias_all, place.s, 1, keepdims=False).reshape(1, hidden_own)

    row_blocks = rows_all(place, rows)
    all_rows = jnp.zeros((place.nx, CORES * count, width), BF16)
    for k, both in enumerate(row_blocks):
        mine, other = both[:count], both[count:]
        all_rows = put(all_rows, place.pair(mine, other, 0), (place.x + k) % place.nx)
    all_rows = all_rows.reshape(length, width)

    out_x = jnp.zeros((place.nx, shard, width), BF16)
    for k in range(place.nx):
        here = out_weight if k == 0 else place.to_x(out_weight, k)
        out_x = put(out_x, here, (place.x - k) % place.nx)
    out_half = gather_dp(place, out_x.reshape(place.nx * shard, width))
    out_half = out_half.reshape(dp * place.nx, 1, shard, width)
    full_out = place.pair(out_half, place.core(out_half), 1).reshape(width, width)

    up_blocks = up_weight.reshape(shard, dp, seq, ff_shard).transpose(2, 0, 1, 3)
    up_block = exchange_seq(place, up_blocks.reshape(seq, shard, hidden_own))
    full_up = gather_dp(place, up_block.reshape(seq * shard, hidden_own))
    full_down = gather_dp(place, down_weight)

    seg_row = segment_ids
    seg_col = segment_ids.reshape(length, 1)
    blocks = length // BLOCK
    ids = segment_ids.reshape(length)
    heads_first = ids[::BLOCK]
    heads_last = ids[BLOCK - 1 :: BLOCK]
    low = jnp.sum(ids[None, :] < heads_first[:, None], axis=1, dtype=jnp.int32)
    high = jnp.sum(ids[None, :] <= heads_last[:, None], axis=1, dtype=jnp.int32)
    bounds = jnp.concatenate([low // BLOCK, (high + BLOCK - 1) // BLOCK])
    own_cols = place.s * head_cols
    query_own = lax.dynamic_slice_in_dim(full_query, own_cols, head_cols, 1)
    value_own = lax.dynamic_slice_in_dim(full_value, own_cols, head_cols, 1)
    qkv_bias = jnp.concatenate([query_own, jnp.zeros_like(query_own), value_own], axis=1)
    qkv = (matmul(all_rows, full_qkv) + qkv_bias).astype(BF16)
    mixed_own, logs = attend(qkv, seg_row, seg_col, bounds, heads)

    mixed = exchange_seq(place, mixed_own.reshape(seq, count, head_cols))
    mixed = mixed.transpose(1, 0, 2).reshape(count, width)
    branch = matmul(mixed, full_out) + bias_out
    first, normed_one, factor_one = norm_forward(rows.astype(F32) + branch, gain_one, shift_one)
    first_low = first.astype(BF16)

    first_all = rows_all(place, first_low)
    hidden_all, slope_all = [], []
    for block in first_all:
        hidden, slope = gelu_pair(matmul(block, full_up) + bias_up)
        hidden_all.append(hidden)
        slope_all.append(slope)
    second = rows_sum(place, [matmul(hidden, full_down) for hidden in hidden_all]) + bias_down
    result, normed_two, factor_two = norm_forward(first + second, gain_two, shift_two)
    output = result.astype(BF16).reshape(tokens.shape)

    grad_out = cotangent.reshape(count, width).astype(F32)
    second_grad, gain_two_grad, shift_two_grad = norm_backward(
        grad_out, normed_two, factor_two, gain_two
    )
    second_low = second_grad.astype(BF16)
    down_bias_grad = jnp.sum(second_low, axis=0, dtype=F32)
    second_all = rows_all(place, second_low)
    preact_all = [
        (right_product(block, full_down) * slope.astype(F32)).astype(BF16)
        for block, slope in zip(second_all, slope_all)
    ]
    first_grad = second_grad + rows_sum(place, [right_product(p, full_up) for p in preact_all])
    down_grad = sum(left_product(h, g) for h, g in zip(hidden_all, second_all))
    up_grad = sum(left_product(f, g) for f, g in zip(first_all, preact_all))
    up_bias_grad = sum(jnp.sum(p, axis=0, dtype=F32) for p in preact_all)
    down_owned = scatter_dp(place, down_grad)
    up_owned = scatter_dp(place, up_grad).astype(BF16)
    up_owned = up_owned.reshape(seq, shard, hidden_own)
    up_owned = exchange_seq(place, up_owned).reshape(seq, shard, dp, ff_shard)
    up_owned = up_owned.transpose(1, 2, 0, 3).reshape(up_weight.shape).astype(F32)

    residual_grad, gain_one_grad, shift_one_grad = norm_backward(
        first_grad, normed_one, factor_one, gain_one
    )
    branch_low = residual_grad.astype(BF16)
    out_bias_grad = jnp.sum(branch_low, axis=0, dtype=F32)
    mixed_grad = right_product(branch_low, full_out).astype(BF16)
    grad_blocks = mixed_grad.reshape(count, seq, head_cols).transpose(1, 0, 2)
    grad_own = exchange_seq(place, grad_blocks).reshape(length, head_cols)

    out_grad = left_product(mixed, branch_low).astype(BF16)
    view = out_grad.reshape(dp * place.nx, CORES, shard, width)
    mine = lax.dynamic_index_in_dim(view, place.c, 1, keepdims=False)
    other = lax.dynamic_index_in_dim(view, 1 - place.c, 1, keepdims=False)
    view = (mine.astype(F32) + place.core(other).astype(F32)).astype(BF16)
    view = view.reshape(dp, place.nx, shard, width)
    summed = lax.dynamic_index_in_dim(view, place.x, 1, keepdims=False).astype(F32)
    for k in range(1, place.nx):
        sent = lax.dynamic_index_in_dim(view, (place.x + k) % place.nx, 1, keepdims=False)
        summed = summed + place.to_x(sent, k).astype(F32)
    out_owned = scatter_dp(place, summed.reshape(dp * shard, width))

    up_bias_wide = lax.dynamic_update_index_in_dim(
        jnp.zeros((dp, seq, ff_shard), F32),
        up_bias_grad.reshape(dp, ff_shard),
        place.s,
        1,
    )
    wide = jnp.concatenate(
        [
            v.reshape(1, width)
            for v in (
                out_bias_grad,
                gain_one_grad,
                shift_one_grad,
                down_bias_grad,
                gain_two_grad,
                shift_two_grad,
            )
        ],
        axis=0,
    ).reshape(6, everyone, shard)
    wide = jnp.concatenate(
        [wide.transpose(1, 0, 2), up_bias_wide.reshape(everyone, ff_shard // shard, shard)], axis=1
    )
    wide = take(all_sum(place, wide), me)
    out_bias_owned, gain_one_owned, shift_one_owned = wide[0], wide[1], wide[2]
    down_bias_owned, gain_two_owned, shift_two_owned = wide[3], wide[4], wide[5]
    up_bias_owned = wide[6:].reshape(ff_shard)

    qkv_grad = attend_back(qkv, mixed_own, grad_own, logs, seg_row, seg_col, bounds, heads)
    joint_grad = left_product(all_rows, qkv_grad)
    joint_owned = scatter_dp(place, joint_grad).astype(BF16)
    joint_owned = exchange_seq(place, joint_owned.reshape(seq, shard, 3 * head_cols))
    joint_owned = joint_owned.reshape(seq, shard, 3, head_cols).transpose(1, 2, 0, 3)
    joint_owned = joint_owned.reshape(qkv_weight.shape).astype(F32)
    sums = jnp.sum(qkv_grad, axis=0, dtype=F32).reshape(3, head_cols)
    ends = jnp.stack([sums[0], sums[2]])[:, None]
    ends = lax.dynamic_update_slice_in_dim(jnp.zeros((2, seq, head_cols), F32), ends, place.s, 1)
    ends = all_sum(place, ends.reshape(2, everyone, shard))
    ends = lax.dynamic_index_in_dim(ends, me, 1, keepdims=False)

    token_parts = right_product(qkv_grad, full_qkv).astype(BF16)
    token_parts = token_parts.reshape(place.nx, CORES, count, width)
    ordered = []
    for k in range(place.nx):
        both = take(token_parts, (place.x + k) % place.nx)
        ordered.append(
            jnp.concatenate([take(both, place.c), take(both, 1 - place.c)], axis=0)
        )
    tokens_grad = (residual_grad + rows_sum(place, ordered)).astype(BF16).reshape(tokens.shape)
    return (
        output,
        tokens_grad,
        joint_owned,
        ends[0],
        ends[1],
        out_owned,
        out_bias_owned,
        gain_one_owned,
        shift_one_owned,
        up_owned,
        up_bias_owned,
        down_owned,
        down_bias_owned,
        gain_two_owned,
        shift_two_owned,
    )


def solution(mesh):
    rows = P("dp", "seq", None)
    matrix = P(("dp", "seq"), None)
    vector = P(("dp", "seq"))
    params = (
        matrix,
        vector,
        vector,
        matrix,
        vector,
        vector,
        vector,
        matrix,
        vector,
        matrix,
        vector,
        vector,
        vector,
    )
    return jax.shard_map(
        partial(body, mesh.shape["dp"], mesh.shape["seq"]),
        mesh=mesh,
        in_specs=(rows, P("dp", None), *params, rows),
        out_specs=(rows, rows, *params),
        check_vma=False,
    )
```

time: 1360 us -> 488 us (0.36)
  waiting for transfers between devices: 890 us -> 239 us
  blocking collectives: 123 us -> 0 us
  matrix products: 165 us -> 46.5 us
  local copies, waits for them, and re-layouts: 138 us -> 47 us
  starting transfers between devices: 0.59 us -> 85.8 us
  Pallas kernels: 0 us -> 28.1 us
  other arithmetic: 13.7 us -> 30.6 us
  loops' own time: 14.4 us -> 0 us
    reduce_scatter x3 -> x0, waiting for transfers between devices: 415 us -> none  [the longest x1 187 us: body(): lax.psum_scatter(down_grad, ('dp', 'seq'), scatter_dimension=0, tiled=True)]
    ppermute x0 -> x111, waiting for transfers between devices: none -> 239 us  [the longest x15 68.7 us: all_sum(): lax.ppermute(value, axis, [(i, i ^ bit) for i in range(size)])]
    all_gather x5 -> x0, waiting for transfers between devices: 180 us -> none  [the longest x1 76.2 us: body(): lax.all_gather(up_weight, ('dp', 'seq'), axis=0, tiled=True)]
    unnamed x10 -> x0, waiting for transfers between devices: 161 us -> none
    while x16 -> x0, waiting for transfers between devices: 134 us -> none
    dot_general x40 -> x18, matrix products: 165 us -> 46.5 us  [the longest x6 17.1 us: right_product(): return lax.dot_general(left, right, DN_T, preferred_element_type=F32)]
    ppermute x0 -> x111, starting transfers between devices: none -> 85.8 us  [the longest x32 43.2 us: to_y(): lax.ppermute(a, 'dp', [(i, i // n * n + (i % n + k) % n) for i in range(s...]
    unnamed x2 -> x0, blocking collectives: 83.5 us -> none
  transfers between devices with their start and end apart: 17 -> 111, of which waited for: 16 -> 56; matrix products, arithmetic and copies ran while one was open for 13% -> 20% of each run, Pallas kernels for 0% -> 6%
where the time goes in v1:
time: 488 us; the launch traced here: 480 us
  waiting for transfers between devices  239 us (49%)
  starting transfers between devices  85.8 us (18%)
  local copies, waits for them, and re-layouts  47 us (10%)
  matrix products  46.5 us (10%)
  other arithmetic  30.6 us (6%)
  Pallas kernels  28.1 us (6%)
    ppermute x15, waiting for transfers between devices, all_sum(): lax.ppermute(value, axis, [(i, i ^ bit) for i in range(size)])  68.7 us
    ppermute x24, waiting for transfers between devices, to_z(): lax.ppermute(a, 'dp', [(i, (i // m + k) % n * m + i % m) for i in range(s...  58.1 us
    ppermute x32, waiting for transfers between devices, to_y(): lax.ppermute(a, 'dp', [(i, i // n * n + (i % n + k) % n) for i in range(s...  55 us
    ppermute x14, waiting for transfers between devices, to_x(): lax.ppermute(a, 'seq', [(i, (i // CORES + k) % n * CORES + i % CORES) for...  51.7 us
    ppermute x32, starting transfers between devices, to_y(): lax.ppermute(a, 'dp', [(i, i // n * n + (i % n + k) % n) for i in range(s...  43.2 us
    dot_general x6, matrix products, right_product(): return lax.dot_general(left, right, DN_T, preferred_element_type=F32)  17.1 us
    ppermute x15, starting transfers between devices, all_sum(): lax.ppermute(value, axis, [(i, i ^ bit) for i in range(size)])  16.8 us
    ppermute x14, starting transfers between devices, to_x(): lax.ppermute(a, 'seq', [(i, (i // CORES + k) % n * CORES + i % CORES) for...  15.8 us
  transfers between devices with their start and end apart: 111, of which 56 were waited for; matrix products, arithmetic and copies ran while one was open for 20% of the time, Pallas kernels for 6%

profile of v1, /device:TPU:0, one launch (start us, length us, event | category | flops | bytes accessed | tf_op | source)
XLA Modules:
  0.0 479.8 jit_solution(10516293765013243900)
XLA Ops:
  15.4 4.2 collective-permute-done.21
  21.9 8.5 %collective-permute-done.14 = f32[32,12,32]{2,1,0:T(8,128)S(1)} collective-permute-done((f32[32,12,32]{2,1,0:T(8,128)}, f32[32,12,32]{2,1,0:T(8,128)S(1)}, u32[]{:S(2)}, u32[]{:S(2)}) %collective-permute-start.14) | collective-permute-done | bytes 49184 | tf_op jit(solution)/shard_map/ppermute | solution.py:152
  36.4 9.6 %collective-permute-done.15 = f32[32,12,32]{2,1,0:T(8,128)S(1)} collective-permute-done((f32[32,12,32]{2,1,0:T(8,128)S(1)}, f32[32,12,32]{2,1,0:T(8,128)S(1)}, u32[]{:S(2)}, u32[]{:S(2)}) %collective-permute-start.15) | collective-permute-done | bytes 49184 | tf_op jit(solution)/shard_map/ppermute | solution.py:152
  50.4 6.8 %collective-permute-done.23 = bf16[64,1024]{1,0:T(8,128)(2,1)S(1)} collective-permute-done((bf16[64,1024]{1,0:T(8,128)(2,1)S(1)}, bf16[64,1024]{1,0:T(8,128)(2,1)S(1)}, u32[]{:S(2)}, u32[]{:S(2)}) %collective-permute-start.23) | collective-permute-done | bytes 131104 | tf_op jit(solution)/shard_map/ppermute | solution.py:84
  57.9 6.7 %collective-permute-done.16 = f32[32,12,32]{2,1,0:T(8,128)S(1)} collective-permute-done((f32[32,12,32]{2,1,0:T(8,128)S(1)}, f32[32,12,32]{2,1,0:T(8,128)S(1)}, u32[]{:S(2)}, u32[]{:S(2)}) %collective-permute-start.16) | collective-permute-done | bytes 49184 | tf_op jit(solution)/shard_map/ppermute | solution.py:152
  67.8 9.8 %collective-permute-done.17 = f32[32,12,32]{2,1,0:T(8,128)S(1)} collective-permute-done((f32[32,12,32]{2,1,0:T(8,128)S(1)}, f32[32,12,32]{2,1,0:T(8,128)S(1)}, u32[]{:S(2)}, u32[]{:S(2)}) %collective-permute-start.17) | collective-permute-done | bytes 49184 | tf_op jit(solution)/shard_map/ppermute | solution.py:152
  85.1 3.5 collective-permute-done.24
  88.6 7.0 %collective-permute-done.25 = bf16[64,1024]{1,0:T(8,128)(2,1)S(1)} collective-permute-done((bf16[64,1024]{1,0:T(8,128)(2,1)}, bf16[64,1024]{1,0:T(8,128)(2,1)S(1)}, u32[]{:S(2)}, u32[]{:S(2)}) %collective-permute-start.25) | collective-permute-done | bytes 131104 | tf_op jit(solution)/shard_map/ppermute | solution.py:84
  99.1 5.7 %collective-permute-done.35 = bf16[128,1024]{1,0:T(8,128)(2,1)S(1)} collective-permute-done((bf16[128,1024]{1,0:T(8,128)(2,1)S(1)}, bf16[128,1024]{1,0:T(8,128)(2,1)S(1)}, u32[]{:S(2)}, u32[]{:S(2)}) %collective-permute-start.35) | collective-permute-done | bytes 262176 | tf_op jit(solution)/shard_map/ppermute | solution.py:78
  110.9 6.7 %collective-permute-done.27 = bf16[64,1024]{1,0:T(8,128)(2,1)S(1)} collective-permute-done((bf16[64,1024]{1,0:T(8,128)(2,1)S(1)}, bf16[64,1024]{1,0:T(8,128)(2,1)S(1)}, u32[]{:S(2)}, u32[]{:S(2)}) %collective-permute-start.27) | collective-permute-done | bytes 131104 | tf_op jit(solution)/shard_map/ppermute | solution.py:84
  119.9 5.5 %collective-permute-done.8 = bf16[128,768]{1,0:T(8,128)(2,1)S(1)} collective-permute-done((bf16[128,768]{1,0:T(8,128)(2,1)S(1)}, bf16[128,768]{1,0:T(8,128)(2,1)S(1)}, u32[]{:S(2)}, u32[]{:S(2)}) %collective-permute-start.8) | collective-permute-done | bytes 196640 | tf_op jit(solution)/shard_map/ppermute | solution.py:78
  130.9 3.8 collective-permute-done.37
  140.4 6.2 %collective-permute-done.11 = bf16[128,768]{1,0:T(8,128)(2,1)S(1)} collective-permute-done((bf16[128,768]{1,0:T(8,128)(2,1)S(1)}, bf16[128,768]{1,0:T(8,128)(2,1)S(1)}, u32[]{:S(2)}, u32[]{:S(2)}) %collective-permute-start.11) | collective-permute-done | bytes 196640 | tf_op jit(solution)/shard_map/ppermute | solution.py:84
  148.8 6.3 %collective-permute-done.12 = bf16[128,768]{1,0:T(8,128)(2,1)S(1)} collective-permute-done((bf16[128,768]{1,0:T(8,128)(2,1)S(1)}, bf16[128,768]{1,0:T(8,128)(2,1)S(1)}, u32[]{:S(2)}, u32[]{:S(2)}) %collective-permute-start.12) | collective-permute-done | bytes 196640 | tf_op jit(solution)/shard_map/ppermute | solution.py:78
  158.0 13.2 %shard_map.271 = (bf16[1152,256]{1,0:T(8,128)(2,1)S(1)}, f32[4,1152]{1,0:T(4,128)S(1)}) custom-call(s32[6]{0:T(128)S(1)} %pad_add_fusion.bounds, bf16[1152,768]{1,0:T(8,128)(2,1)S(1)} %fusion.qkv_ref, s32[1,1152]{1,0:T(1,128)S(1)} %copy-done, s32[1152,1]{1,0:T(8,128)S(1)} %copy.55.seg_col), custom_call_target="tpu_custom_call" | custom-call | flops 1358954496 | bytes 2359296 | tf_op jit(solution)/shard_map/pallas_call | solution.py:288
  172.5 3.4 collective-permute-start.48
  178.0 3.4 collective-permute-start.41
  188.5 12.8 %collective-permute-done.30 = bf16[288,1024]{1,0:T(8,128)(2,1)S(1)} collective-permute-done((bf16[288,1024]{1,0:T(8,128)(2,1)S(1)}, bf16[288,1024]{1,0:T(8,128)(2,1)S(1)}, u32[]{:S(2)}, u32[]{:S(2)}) %collective-permute-start.30) | collective-permute-done | bytes 589856 | tf_op jit(solution)/shard_map/ppermute | solution.py:70
  202.0 3.2 fusion.32
  205.3 6.2 %multiply_convert_fusion.3 = (bf16[576,1024]{1,0:T(8,128)(2,1)S(1)}, bf16[576,1024]{1,0:T(8,128)(2,1)S(1)}, f32[576,1024]{1,0:T(8,128)}) fusion(f32[1024]{0:T(1024)S(1)} %bitcast.559, f32[576,1024]{1,0:T(8,128)S(1)} %fusion.32, bf16[576,1024]{1,0:T(8,128)(2,1)S(1)} %constant_dynamic-update-slice_fusion.4, bf16[1024,1024]{1,0:T(8,128)(2,1)} %bitcast.78), kind=kOutput, calls=%fused_computation.24 | convolution fusion | flops 1215037440 | bytes 10358784 | tf_op jit(solution)/shard_map/dot_general | solution.py:22
  219.3 14.8 %collective-permute-done.50 = bf16[288,1024]{1,0:T(8,128)(2,1)} collective-permute-done((bf16[288,1024]{1,0:T(8,128)(2,1)}, bf16[288,1024]{1,0:T(8,128)(2,1)}, u32[]{:S(2)}, u32[]{:S(2)}) %collective-permute-start.50) | collective-permute-done | bytes 589856 | tf_op jit(solution)/shard_map/ppermute | solution.py:70
  241.6 4.8 %convert_reduce_fusion.2 = (f32[1024]{0:T(1024)S(1)}, bf16[576,1024]{1,0:T(8,128)(2,1)S(1)}) fusion(f32[576,1024]{1,0:T(8,128)} %copy-done.49, f32[1024]{0:T(1024)S(1)} %bitcast.560, bf16[1024,1024]{1,0:T(8,128)(2,1)} %bitcast.511, bf16[288,1024]{1,0:T(8,128)(2,1)} %collective-permute-done.57, bf16[288,1024]{1,0:T(8,128)(2,1)} %get-tuple-element.37), kind=kOutput, calls=%fused_computation.19 | convolution fusion | flops 1219165184 | bytes 6823936 | tf_op jit(solution)/shard_map/dot_general | solution.py:30
  246.4 8.9 %collective-permute-done.53 = bf16[288,1024]{1,0:T(8,128)(2,1)} collective-permute-done((bf16[288,1024]{1,0:T(8,128)(2,1)}, bf16[288,1024]{1,0:T(8,128)(2,1)}, u32[]{:S(2)}, u32[]{:S(2)}) %collective-permute-start.53) | collective-permute-done | bytes 589856 | tf_op jit(solution)/shard_map/ppermute | solution.py:70
  255.3 3.1 fusion.30
  272.4 4.0 collective-permute-done.97
  276.6 3.1 convolution_convert_fusion.4
  282.5 5.2 %collective-permute-done.107 = bf16[128,1024]{1,0:T(8,128)(2,1)S(1)} collective-permute-done((bf16[128,1024]{1,0:T(8,128)(2,1)S(1)}, bf16[128,1024]{1,0:T(8,128)(2,1)S(1)}, u32[]{:S(2)}, u32[]{:S(2)}) %collective-permute-start.107) | collective-permute-done | bytes 262176 | tf_op jit(solution)/shard_map/ppermute | solution.py:78
  291.3 3.1 convolution_convert_fusion.3
  295.8 2.9 collective-permute-done.106
  306.6 6.6 %collective-permute-done.105 = bf16[128,1024]{1,0:T(8,128)(2,1)S(1)} collective-permute-done((bf16[128,1024]{1,0:T(8,128)(2,1)}, bf16[128,1024]{1,0:T(8,128)(2,1)S(1)}, u32[]{:S(2)}, u32[]{:S(2)}) %collective-permute-start.105) | collective-permute-done | bytes 262176 | tf_op jit(solution)/shard_map/ppermute | solution.py:78
  321.5 3.9 collective-permute-done.110
  346.2 7.4 %collective-permute-done.90 = f32[32,10,32]{2,1,0:T(8,128)S(1)} collective-permute-done((f32[32,10,32]{2,1,0:T(8,128)S(1)}, f32[32,10,32]{2,1,0:T(8,128)S(1)}, u32[]{:S(2)}, u32[]{:S(2)}) %collective-permute-start.90) | collective-permute-done | bytes 40992 | tf_op jit(solution)/shard_map/ppermute | solution.py:152
  356.9 4.7 collective-permute-done.91
  361.7 3.2 collective-permute-start.92
  365.9 4.2 collective-permute-done.92
  371.7 11.3 %collective-permute-done.93 = f32[32,10,32]{2,1,0:T(8,128)S(1)} collective-permute-done((f32[32,10,32]{2,1,0:T(8,128)S(1)}, f32[32,10,32]{2,1,0:T(8,128)S(1)}, u32[]{:S(2)}, u32[]{:S(2)}) %collective-permute-start.93) | collective-permute-done | bytes 40992 | tf_op jit(solution)/shard_map/ppermute | solution.py:152
  383.1 14.9 %shard_map.272 = bf16[1152,768]{1,0:T(8,128)(2,1)S(1)} custom-call(s32[6]{0:T(128)S(1)} %pad_add_fusion.bounds, bf16[1152,768]{1,0:T(8,128)(2,1)S(1)} %copy-done.2, bf16[1152,256]{1,0:T(8,128)(2,1)S(1)} %get-tuple-element.17.mixed_ref, bf16[1152,256]{1,0:T(8,128)(2,1)S(1)} %bitcast.487, f32[4,1152]{1,0:T(4,128)S(1)} %get-tuple-element.18.log_ref, ...), custom_call_target="tpu_custom_call" | custom-call | flops 3397386240 | bytes 4718592 | tf_op jit(solution)/shard_map/pallas_call | solution.py:315
  401.5 3.9 convolution_convert_fusion.2
  405.5 4.1 collective-permute-start.77
  417.1 3.4 collective-permute-done.79
  422.9 4.3 collective-permute-done.67
  430.7 2.7 collective-permute-done.66
  433.4 5.1 %collective-permute-done.70 = bf16[128,768]{1,0:T(8,128)(2,1)S(1)} collective-permute-done((bf16[128,768]{1,0:T(8,128)(2,1)S(1)}, bf16[128,768]{1,0:T(8,128)(2,1)S(1)}, u32[]{:S(2)}, u32[]{:S(2)}) %collective-permute-start.70) | collective-permute-done | bytes 196640 | tf_op jit(solution)/shard_map/ppermute | solution.py:84
  440.6 5.5 %collective-permute-done.71 = bf16[128,768]{1,0:T(8,128)(2,1)S(1)} collective-permute-done((bf16[128,768]{1,0:T(8,128)(2,1)S(1)}, bf16[128,768]{1,0:T(8,128)(2,1)S(1)}, u32[]{:S(2)}, u32[]{:S(2)}) %collective-permute-start.71) | collective-permute-done | bytes 196640 | tf_op jit(solution)/shard_map/ppermute | solution.py:84
  447.5 8.3 %collective-permute-done.81 = bf16[8,32,1024]{2,1,0:T(8,128)(2,1)S(1)} collective-permute-done((bf16[8,32,1024]{2,1,0:T(8,128)(2,1)S(1)}, bf16[8,32,1024]{2,1,0:T(8,128)(2,1)S(1)}, u32[]{:S(2)}, u32[]{:S(2)}) %collective-permute-start.81) | collective-permute-done | bytes 524320 | tf_op jit(solution)/shard_map/ppermute | solution.py:70
  463.0 3.6 collective-permute-done.86
  472.9 2.6 fusion.34
  475.5 3.4 collective-permute-done.88
  (527 shorter events, 191.3 us)
Async XLA Ops:
  0.7 128.4 %collective-permute-start = (bf16[288,1024]{1,0:T(8,128)(2,1)}, bf16[288,1024]{1,0:T(8,128)(2,1)}, u32[]{:S(2)}, u32[]{:S(2)}) collective-permute-start(bf16[288,1024]{1,0:T(8,128)(2,1)} %bitcast.551), channel_id=1, source_target_pairs={{0,1},{1,0},{2,3},{3,2},{4,5},{5,4},{6,7},{7,6},{8,9},{9,8},{10,11... | collective-permute-start | bytes 1769480 | tf_op jit(solution)/shard_map/ppermute | solution.py:66
  1.2 138.7 %collective-permute-start.1 = (bf16[288,1024]{1,0:T(8,128)(2,1)}, bf16[288,1024]{1,0:T(8,128)(2,1)S(1)}, u32[]{:S(2)}, u32[]{:S(2)}) collective-permute-start(bf16[288,1024]{1,0:T(8,128)(2,1)} %bitcast.552), channel_id=1, source_target_pairs={{0,2},{1,3},{2,0},{3,1},{4,6},{5,7},{6,4},{7,5},{8,10},{9,11},{10,... | collective-permute-start | bytes 1769480 | tf_op jit(solution)/shard_map/ppermute | solution.py:70
  7.4 12.1 %collective-permute-start.21 = (bf16[32,1024]{1,0:T(8,128)(2,1)S(1)}, bf16[32,1024]{1,0:T(8,128)(2,1)S(1)}, u32[]{:S(2)}, u32[]{:S(2)}) collective-permute-start(bf16[32,1024]{1,0:T(8,128)(2,1)S(1)} %copy-done.41), channel_id=1, source_target_pairs={{0,2},{1,3},{2,0},{3,1},{4,6},{5,7},{6,4},{7,5},{8,10},{9,11},{10,... | collective-permute-start | bytes 196616 | tf_op jit(solution)/shard_map/ppermute | solution.py:70
  12.0 21.0 %collective-permute-start.4 = (bf16[2,32,768]{2,1,0:T(8,128)(2,1)S(1)}, bf16[2,32,768]{2,1,0:T(8,128)(2,1)S(1)}, u32[]{:S(2)}, u32[]{:S(2)}) collective-permute-start(bf16[2,32,768]{2,1,0:T(8,128)(2,1)S(1)} %dynamic-slice_bitcast_fusion.25), channel_id=1, source_target_pairs={{0,2},{1,3},{2,0},{3,1},{4,6},{5,7},{6,4},{7,5},{8,10},{9,11},{10,... | collective-permute-start | bytes 294920 | tf_op jit(solution)/shard_map/ppermute | solution.py:70
  19.6 13.9 %collective-permute-start.33 = (bf16[2,32,1024]{2,1,0:T(8,128)(2,1)}, bf16[2,32,1024]{2,1,0:T(8,128)(2,1)S(1)}, u32[]{:S(2)}, u32[]{:S(2)}) collective-permute-start(bf16[2,32,1024]{2,1,0:T(8,128)(2,1)} %dynamic-slice_bitcast_fusion.23), channel_id=1, source_target_pairs={{0,2},{1,3},{2,0},{3,1},{4,6},{5,7},{6,4},{7,5},{8,10},{9,11},{10,... | collective-permute-start | bytes 393224 | tf_op jit(solution)/shard_map/ppermute | solution.py:70
  30.4 51.1 %collective-permute-start.42 = (bf16[128,1024]{1,0:T(8,128)(2,1)}, bf16[128,1024]{1,0:T(8,128)(2,1)}, u32[]{:S(2)}, u32[]{:S(2)}) collective-permute-start(bf16[128,1024]{1,0:T(8,128)(2,1)} %param.27), channel_id=1, source_target_pairs={{0,4},{4,0},{8,12},{12,8},{16,20},{20,16},{24,28},{28,24},{1,5},{5... | collective-permute-start | bytes 786440 | tf_op jit(solution)/shard_map/ppermute | solution.py:78
  33.0 14.5 %collective-permute-start.22 = (bf16[64,1024]{1,0:T(8,128)(2,1)S(1)}, bf16[64,1024]{1,0:T(8,128)(2,1)S(1)}, u32[]{:S(2)}, u32[]{:S(2)}) collective-permute-start(bf16[64,1024]{1,0:T(8,128)(2,1)S(1)} %bitcast.556), channel_id=1, source_target_pairs={{0,4},{4,0},{8,12},{12,8},{16,20},{20,16},{24,28},{28,24},{1,5},{5... | collective-permute-start | bytes 393224 | tf_op jit(solution)/shard_map/ppermute | solution.py:78
  34.8 11.3 %collective-permute-start.15 = (f32[32,12,32]{2,1,0:T(8,128)S(1)}, f32[32,12,32]{2,1,0:T(8,128)S(1)}, u32[]{:S(2)}, u32[]{:S(2)}) collective-permute-start(f32[32,12,32]{2,1,0:T(8,128)S(1)} %add.841), channel_id=1, source_target_pairs={{0,4},{4,0},{8,12},{12,8},{16,20},{20,16},{24,28},{28,24},{1,5},{5... | collective-permute-start | bytes 147464 | tf_op jit(solution)/shard_map/ppermute | solution.py:152
  46.0 37.2 %collective-permute-start.43 = (bf16[128,1024]{1,0:T(8,128)(2,1)}, bf16[128,1024]{1,0:T(8,128)(2,1)}, u32[]{:S(2)}, u32[]{:S(2)}) collective-permute-start(bf16[128,1024]{1,0:T(8,128)(2,1)} %param.27), channel_id=1, source_target_pairs={{0,8},{4,12},{8,16},{12,20},{16,24},{20,28},{24,0},{28,4},{1,9},{5... | collective-permute-start | bytes 786440 | tf_op jit(solution)/shard_map/ppermute | solution.py:84
  64.6 13.0 %collective-permute-start.17 = (f32[32,12,32]{2,1,0:T(8,128)S(1)}, f32[32,12,32]{2,1,0:T(8,128)S(1)}, u32[]{:S(2)}, u32[]{:S(2)}) collective-permute-start(f32[32,12,32]{2,1,0:T(8,128)S(1)} %add.843), channel_id=1, source_target_pairs={{0,16},{4,20},{8,24},{12,28},{16,0},{20,4},{24,8},{28,12},{1,17},{... | collective-permute-start | bytes 147464 | tf_op jit(solution)/shard_map/ppermute | solution.py:152
  77.6 18.4 %collective-permute-start.6 = (bf16[128,768]{1,0:T(8,128)(2,1)S(1)}, bf16[128,768]{1,0:T(8,128)(2,1)S(1)}, u32[]{:S(2)}, u32[]{:S(2)}) collective-permute-start(bf16[128,768]{1,0:T(8,128)(2,1)S(1)} %bitcast.546), channel_id=1, source_target_pairs={{0,4},{4,0},{8,12},{12,8},{16,20},{20,16},{24,28},{28,24},{1,5},{5... | collective-permute-start | bytes 589832 | tf_op jit(solution)/shard_map/ppermute | solution.py:78
  81.5 15.3 %collective-permute-start.7 = (bf16[128,768]{1,0:T(8,128)(2,1)S(1)}, bf16[128,768]{1,0:T(8,128)(2,1)S(1)}, u32[]{:S(2)}, u32[]{:S(2)}) collective-permute-start(bf16[128,768]{1,0:T(8,128)(2,1)S(1)} %bitcast.547), channel_id=1, source_target_pairs={{0,8},{4,12},{8,16},{12,20},{16,24},{20,28},{24,0},{28,4},{1,9},{5... | collective-permute-start | bytes 589832 | tf_op jit(solution)/shard_map/ppermute | solution.py:84
  96.8 22.9 %collective-permute-start.44 = (bf16[128,1024]{1,0:T(8,128)(2,1)}, bf16[128,1024]{1,0:T(8,128)(2,1)S(1)}, u32[]{:S(2)}, u32[]{:S(2)}) collective-permute-start(bf16[128,1024]{1,0:T(8,128)(2,1)} %collective-permute-done.43), channel_id=1, source_target_pairs={{0,4},{4,0},{8,12},{12,8},{16,20},{20,16},{24,28},{28,24},{1,5},{5... | collective-permute-start | bytes 786440 | tf_op jit(solution)/shard_map/ppermute | solution.py:78
  104.8 15.0 %collective-permute-start.45 = (bf16[128,1024]{1,0:T(8,128)(2,1)}, bf16[128,1024]{1,0:T(8,128)(2,1)S(1)}, u32[]{:S(2)}, u32[]{:S(2)}) collective-permute-start(bf16[128,1024]{1,0:T(8,128)(2,1)} %collective-permute-done.43), channel_id=1, source_target_pairs={{0,8},{4,12},{8,16},{12,20},{16,24},{20,28},{24,0},{28,4},{1,9},{5... | collective-permute-start | bytes 786440 | tf_op jit(solution)/shard_map/ppermute | solution.py:84
  129.1 17.6 %collective-permute-start.46 = (bf16[128,1024]{1,0:T(8,128)(2,1)S(1)}, bf16[128,1024]{1,0:T(8,128)(2,1)S(1)}, u32[]{:S(2)}, u32[]{:S(2)}) collective-permute-start(bf16[128,1024]{1,0:T(8,128)(2,1)S(1)} %collective-permute-done.45), channel_id=1, source_target_pairs={{0,4},{4,0},{8,12},{12,8},{16,20},{20,16},{24,28},{28,24},{1,5},{5... | collective-permute-start | bytes 786440 | tf_op jit(solution)/shard_map/ppermute | solution.py:78
  130.3 42.0 %collective-permute-start.47 = (bf16[128,1024]{1,0:T(8,128)(2,1)S(1)}, bf16[128,1024]{1,0:T(8,128)(2,1)S(1)}, u32[]{:S(2)}, u32[]{:S(2)}) collective-permute-start(bf16[128,1024]{1,0:T(8,128)(2,1)S(1)} %collective-permute-done.45), channel_id=1, source_target_pairs={{0,8},{4,12},{8,16},{12,20},{16,24},{20,28},{24,0},{28,4},{1,9},{5... | collective-permute-start | bytes 786440 | tf_op jit(solution)/shard_map/ppermute | solution.py:84
  139.9 43.6 %collective-permute-start.29 = (bf16[16,1,32,1024]{3,2,1,0:T(8,128)(2,1)S(1)}, bf16[16,1,32,1024]{3,2,1,0:T(8,128)(2,1)S(1)}, u32[]{:S(2)}, u32[]{:S(2)}) collective-permute-start(bf16[16,1,32,1024]{3,2,1,0:T(8,128)(2,1)S(1)} %bitcast.492), channel_id=1, source_target_pairs={{0,1},{1,0},{2,3},{3,2},{4,5},{5,4},{6,7},{7,6},{8,9},{9,8},{10,11... | collective-permute-start | bytes 3145736 | tf_op jit(solution)/shard_map/ppermute | solution.py:66
  140.3 15.3 %collective-permute-start.2 = (bf16[288,1024]{1,0:T(8,128)(2,1)S(1)}, bf16[288,1024]{1,0:T(8,128)(2,1)S(1)}, u32[]{:S(2)}, u32[]{:S(2)}) collective-permute-start(bf16[288,1024]{1,0:T(8,128)(2,1)S(1)} %collective-permute-done.1), channel_id=1, source_target_pairs={{0,1},{1,0},{2,3},{3,2},{4,5},{5,4},{6,7},{7,6},{8,9},{9,8},{10,11... | collective-permute-start | bytes 1769480 | tf_op jit(solution)/shard_map/ppermute | solution.py:66
  146.6 40.3 %collective-permute-start.39 = (bf16[128,1024]{1,0:T(8,128)(2,1)S(1)}, bf16[128,1024]{1,0:T(8,128)(2,1)S(1)}, u32[]{:S(2)}, u32[]{:S(2)}) collective-permute-start(bf16[128,1024]{1,0:T(8,128)(2,1)S(1)} %collective-permute-done.38), channel_id=1, source_target_pairs={{0,4},{4,0},{8,12},{12,8},{16,20},{20,16},{24,28},{28,24},{1,5},{5... | collective-permute-start | bytes 786440 | tf_op jit(solution)/shard_map/ppermute | solution.py:78
  155.1 17.4 %collective-permute-start.40 = (bf16[128,1024]{1,0:T(8,128)(2,1)S(1)}, bf16[128,1024]{1,0:T(8,128)(2,1)S(1)}, u32[]{:S(2)}, u32[]{:S(2)}) collective-permute-start(bf16[128,1024]{1,0:T(8,128)(2,1)S(1)} %collective-permute-done.38), channel_id=1, source_target_pairs={{0,8},{4,12},{8,16},{12,20},{16,24},{20,28},{24,0},{28,4},{1,9},{5... | collective-permute-start | bytes 786440 | tf_op jit(solution)/shard_map/ppermute | solution.py:84
  172.5 15.9 %collective-permute-start.48 = (bf16[128,1024]{1,0:T(8,128)(2,1)S(1)}, bf16[128,1024]{1,0:T(8,128)(2,1)S(1)}, u32[]{:S(2)}, u32[]{:S(2)}) collective-permute-start(bf16[128,1024]{1,0:T(8,128)(2,1)S(1)} %collective-permute-done.47), channel_id=1, source_target_pairs={{0,4},{4,0},{8,12},{12,8},{16,20},{20,16},{24,28},{28,24},{1,5},{5... | collective-permute-start | bytes 786440 | tf_op jit(solution)/shard_map/ppermute | solution.py:78
  178.0 23.3 %collective-permute-start.41 = (bf16[128,1024]{1,0:T(8,128)(2,1)S(1)}, bf16[128,1024]{1,0:T(8,128)(2,1)S(1)}, u32[]{:S(2)}, u32[]{:S(2)}) collective-permute-start(bf16[128,1024]{1,0:T(8,128)(2,1)S(1)} %collective-permute-done.40), channel_id=1, source_target_pairs={{0,4},{4,0},{8,12},{12,8},{16,20},{20,16},{24,28},{28,24},{1,5},{5... | collective-permute-start | bytes 786440 | tf_op jit(solution)/shard_map/ppermute | solution.py:78
  185.8 15.4 %collective-permute-start.30 = (bf16[288,1024]{1,0:T(8,128)(2,1)S(1)}, bf16[288,1024]{1,0:T(8,128)(2,1)S(1)}, u32[]{:S(2)}, u32[]{:S(2)}) collective-permute-start(bf16[288,1024]{1,0:T(8,128)(2,1)S(1)} %fusion.29), channel_id=1, source_target_pairs={{0,2},{1,3},{2,0},{3,1},{4,6},{5,7},{6,4},{7,5},{8,10},{9,11},{10,... | collective-permute-start | bytes 1769480 | tf_op jit(solution)/shard_map/ppermute | solution.py:70
  188.4 13.6 %collective-permute-start.51 = (bf16[288,1024]{1,0:T(8,128)(2,1)S(1)}, bf16[288,1024]{1,0:T(8,128)(2,1)S(1)}, u32[]{:S(2)}, u32[]{:S(2)}) collective-permute-start(bf16[288,1024]{1,0:T(8,128)(2,1)S(1)} %fusion.29), channel_id=1, source_target_pairs={{0,1},{1,0},{2,3},{3,2},{4,5},{5,4},{6,7},{7,6},{8,9},{9,8},{10,11... | collective-permute-start | bytes 1769480 | tf_op jit(solution)/shard_map/ppermute | solution.py:66
  218.0 16.0 %collective-permute-start.50 = (bf16[288,1024]{1,0:T(8,128)(2,1)}, bf16[288,1024]{1,0:T(8,128)(2,1)}, u32[]{:S(2)}, u32[]{:S(2)}) collective-permute-start(bf16[288,1024]{1,0:T(8,128)(2,1)} %add_convert_fusion.4), channel_id=1, source_target_pairs={{0,2},{1,3},{2,0},{3,1},{4,6},{5,7},{6,4},{7,5},{8,10},{9,11},{10,... | collective-permute-start | bytes 1769480 | tf_op jit(solution)/shard_map/ppermute | solution.py:70
  239.2 16.1 %collective-permute-start.53 = (bf16[288,1024]{1,0:T(8,128)(2,1)}, bf16[288,1024]{1,0:T(8,128)(2,1)}, u32[]{:S(2)}, u32[]{:S(2)}) collective-permute-start(bf16[288,1024]{1,0:T(8,128)(2,1)} %get-tuple-element.37), channel_id=1, source_target_pairs={{0,2},{1,3},{2,0},{3,1},{4,6},{5,7},{6,4},{7,5},{8,10},{9,11},{10,... | collective-permute-start | bytes 1769480 | tf_op jit(solution)/shard_map/ppermute | solution.py:70
  267.4 21.2 %collective-permute-start.96 = (bf16[128,1024]{1,0:T(8,128)(2,1)S(1)}, bf16[128,1024]{1,0:T(8,128)(2,1)S(1)}, u32[]{:S(2)}, u32[]{:S(2)}) collective-permute-start(bf16[128,1024]{1,0:T(8,128)(2,1)S(1)} %get-tuple-element.51), channel_id=1, source_target_pairs={{0,4},{4,0},{8,12},{12,8},{16,20},{20,16},{24,28},{28,24},{1,5},{5... | collective-permute-start | bytes 786440 | tf_op jit(solution)/shard_map/ppermute | solution.py:78
  272.4 15.3 %collective-permute-start.107 = (bf16[128,1024]{1,0:T(8,128)(2,1)S(1)}, bf16[128,1024]{1,0:T(8,128)(2,1)S(1)}, u32[]{:S(2)}, u32[]{:S(2)}) collective-permute-start(bf16[128,1024]{1,0:T(8,128)(2,1)S(1)} %get-tuple-element.46), channel_id=1, source_target_pairs={{0,4},{4,0},{8,12},{12,8},{16,20},{20,16},{24,28},{28,24},{1,5},{5... | collective-permute-start | bytes 786440 | tf_op jit(solution)/shard_map/ppermute | solution.py:78
  276.5 13.9 %collective-permute-start.98 = (bf16[128,1024]{1,0:T(8,128)(2,1)S(1)}, bf16[128,1024]{1,0:T(8,128)(2,1)S(1)}, u32[]{:S(2)}, u32[]{:S(2)}) collective-permute-start(bf16[128,1024]{1,0:T(8,128)(2,1)S(1)} %fusion.41), channel_id=1, source_target_pairs={{0,8},{4,12},{8,16},{12,20},{16,24},{20,28},{24,0},{28,4},{1,9},{5... | collective-permute-start | bytes 786440 | tf_op jit(solution)/shard_map/ppermute | solution.py:84
  280.6 24.6 %collective-permute-start.55 = (bf16[288,1024]{1,0:T(8,128)(2,1)}, bf16[288,1024]{1,0:T(8,128)(2,1)}, u32[]{:S(2)}, u32[]{:S(2)}) collective-permute-start(bf16[288,1024]{1,0:T(8,128)(2,1)} %slice.124), channel_id=1, source_target_pairs={{0,1},{1,0},{2,3},{3,2},{4,5},{5,4},{6,7},{7,6},{8,9},{9,8},{10,11... | collective-permute-start | bytes 1769480 | tf_op jit(solution)/shard_map/ppermute | solution.py:66
  280.6 22.5 %collective-permute-start.95 = (bf16[128,1024]{1,0:T(8,128)(2,1)}, bf16[128,1024]{1,0:T(8,128)(2,1)}, u32[]{:S(2)}, u32[]{:S(2)}) collective-permute-start(bf16[128,1024]{1,0:T(8,128)(2,1)} %get-tuple-element.52), channel_id=1, source_target_pairs={{0,4},{4,0},{8,12},{12,8},{16,20},{20,16},{24,28},{28,24},{1,5},{5... | collective-permute-start | bytes 786440 | tf_op jit(solution)/shard_map/ppermute | solution.py:78
  288.6 11.4 %collective-permute-start.108 = (bf16[128,1024]{1,0:T(8,128)(2,1)}, bf16[128,1024]{1,0:T(8,128)(2,1)}, u32[]{:S(2)}, u32[]{:S(2)}) collective-permute-start(bf16[128,1024]{1,0:T(8,128)(2,1)} %fusion.35), channel_id=1, source_target_pairs={{0,8},{4,12},{8,16},{12,20},{16,24},{20,28},{24,0},{28,4},{1,9},{5... | collective-permute-start | bytes 786440 | tf_op jit(solution)/shard_map/ppermute | solution.py:84
  291.3 12.7 %collective-permute-start.99 = (bf16[128,1024]{1,0:T(8,128)(2,1)}, bf16[128,1024]{1,0:T(8,128)(2,1)}, u32[]{:S(2)}, u32[]{:S(2)}) collective-permute-start(bf16[128,1024]{1,0:T(8,128)(2,1)} %fusion.43), channel_id=1, source_target_pairs={{0,8},{4,12},{8,16},{12,20},{16,24},{20,28},{24,0},{28,4},{1,9},{5... | collective-permute-start | bytes 786440 | tf_op jit(solution)/shard_map/ppermute | solution.py:84
  298.6 28.7 %collective-permute-start.58 = (bf16[288,1024]{1,0:T(8,128)(2,1)}, bf16[288,1024]{1,0:T(8,128)(2,1)S(1)}, u32[]{:S(2)}, u32[]{:S(2)}) collective-permute-start(bf16[288,1024]{1,0:T(8,128)(2,1)} %slice.126), channel_id=1, source_target_pairs={{0,1},{1,0},{2,3},{3,2},{4,5},{5,4},{6,7},{7,6},{8,9},{9,8},{10,11... | collective-permute-start | bytes 1769480 | tf_op jit(solution)/shard_map/ppermute | solution.py:66
  299.9 17.3 %collective-permute-start.94 = (bf16[128,1024]{1,0:T(8,128)(2,1)}, bf16[128,1024]{1,0:T(8,128)(2,1)S(1)}, u32[]{:S(2)}, u32[]{:S(2)}) collective-permute-start(bf16[128,1024]{1,0:T(8,128)(2,1)} %get-tuple-element.49), channel_id=1, source_target_pairs={{0,4},{4,0},{8,12},{12,8},{16,20},{20,16},{24,28},{28,24},{1,5},{5... | collective-permute-start | bytes 786440 | tf_op jit(solution)/shard_map/ppermute | solution.py:78
  305.2 13.1 %collective-permute-start.100 = (bf16[128,1024]{1,0:T(8,128)(2,1)S(1)}, bf16[128,1024]{1,0:T(8,128)(2,1)S(1)}, u32[]{:S(2)}, u32[]{:S(2)}) collective-permute-start(bf16[128,1024]{1,0:T(8,128)(2,1)S(1)} %fusion.45), channel_id=1, source_target_pairs={{0,8},{4,12},{8,16},{12,20},{16,24},{20,28},{24,0},{28,4},{1,9},{5... | collective-permute-start | bytes 786440 | tf_op jit(solution)/shard_map/ppermute | solution.py:84
  315.0 13.1 %collective-permute-start.56 = (bf16[288,1024]{1,0:T(8,128)(2,1)S(1)}, bf16[288,1024]{1,0:T(8,128)(2,1)S(1)}, u32[]{:S(2)}, u32[]{:S(2)}) collective-permute-start(bf16[288,1024]{1,0:T(8,128)(2,1)S(1)} %add_convert_fusion.2), channel_id=1, source_target_pairs={{0,2},{1,3},{2,0},{3,1},{4,6},{5,7},{6,4},{7,5},{8,10},{9,11},{10,... | collective-permute-start | bytes 1769480 | tf_op jit(solution)/shard_map/ppermute | solution.py:70
  320.2 21.9 %collective-permute-start.102 = (bf16[2,32,1024]{2,1,0:T(8,128)(2,1)}, bf16[2,32,1024]{2,1,0:T(8,128)(2,1)}, u32[]{:S(2)}, u32[]{:S(2)}) collective-permute-start(bf16[2,32,1024]{2,1,0:T(8,128)(2,1)} %dynamic-slice_bitcast_fusion.22), channel_id=1, source_target_pairs={{0,2},{1,3},{2,0},{3,1},{4,6},{5,7},{6,4},{7,5},{8,10},{9,11},{10,... | collective-permute-start | bytes 393224 | tf_op jit(solution)/shard_map/ppermute | solution.py:70
  338.5 26.3 %collective-permute-start.59 = (bf16[288,256]{1,0:T(8,128)(2,1)S(1)}, bf16[288,256]{1,0:T(8,128)(2,1)}, u32[]{:S(2)}, u32[]{:S(2)}) collective-permute-start(bf16[288,256]{1,0:T(8,128)(2,1)S(1)} %dynamic-slice_bitcast_fusion.19), channel_id=1, source_target_pairs={{0,1},{1,0},{2,3},{3,2},{4,5},{5,4},{6,7},{7,6},{8,9},{9,8},{10,11... | collective-permute-start | bytes 442376 | tf_op jit(solution)/shard_map/ppermute | solution.py:66
  338.6 32.9 %collective-permute-start.60 = (bf16[2,288,256]{2,1,0:T(8,128)(2,1)S(1)}, bf16[2,288,256]{2,1,0:T(8,128)(2,1)S(1)}, u32[]{:S(2)}, u32[]{:S(2)}) collective-permute-start(bf16[2,288,256]{2,1,0:T(8,128)(2,1)S(1)} %dynamic-slice_bitcast_fusion.4), channel_id=1, source_target_pairs={{0,2},{1,3},{2,0},{3,1},{4,6},{5,7},{6,4},{7,5},{8,10},{9,11},{10,... | collective-permute-start | bytes 884744 | tf_op jit(solution)/shard_map/ppermute | solution.py:70
  341.0 97.6 %collective-permute-start.80 = (bf16[16,32,1024]{2,1,0:T(8,128)(2,1)}, bf16[16,32,1024]{2,1,0:T(8,128)(2,1)}, u32[]{:S(2)}, u32[]{:S(2)}) collective-permute-start(bf16[16,32,1024]{2,1,0:T(8,128)(2,1)} %dynamic-slice_bitcast_fusion), channel_id=1, source_target_pairs={{0,1},{1,0},{2,3},{3,2},{4,5},{5,4},{6,7},{7,6},{8,9},{9,8},{10,11... | collective-permute-start | bytes 3145736 | tf_op jit(solution)/shard_map/ppermute | solution.py:66
  370.1 12.9 %collective-permute-start.93 = (f32[32,10,32]{2,1,0:T(8,128)S(1)}, f32[32,10,32]{2,1,0:T(8,128)S(1)}, u32[]{:S(2)}, u32[]{:S(2)}) collective-permute-start(f32[32,10,32]{2,1,0:T(8,128)S(1)} %add.925), channel_id=1, source_target_pairs={{0,16},{4,20},{8,24},{12,28},{16,0},{20,4},{24,8},{28,12},{1,17},{... | collective-permute-start | bytes 122888 | tf_op jit(solution)/shard_map/ppermute | solution.py:152
  371.6 11.5 %collective-permute-start.61 = (bf16[288,256]{1,0:T(8,128)(2,1)S(1)}, bf16[288,256]{1,0:T(8,128)(2,1)S(1)}, u32[]{:S(2)}, u32[]{:S(2)}) collective-permute-start(bf16[288,256]{1,0:T(8,128)(2,1)S(1)} %dynamic-slice_bitcast_fusion.18), channel_id=1, source_target_pairs={{0,1},{1,0},{2,3},{3,2},{4,5},{5,4},{6,7},{7,6},{8,9},{9,8},{10,11... | collective-permute-start | bytes 442376 | tf_op jit(solution)/shard_map/ppermute | solution.py:66
  416.6 56.3 %collective-permute-start.64 = (bf16[288,1024]{1,0:T(8,128)(2,1)}, bf16[288,1024]{1,0:T(8,128)(2,1)}, u32[]{:S(2)}, u32[]{:S(2)}) collective-permute-start(bf16[288,1024]{1,0:T(8,128)(2,1)} %get-tuple-element.44), channel_id=1, source_target_pairs={{0,1},{1,0},{2,3},{3,2},{4,5},{5,4},{6,7},{7,6},{8,9},{9,8},{10,11... | collective-permute-start | bytes 1769480 | tf_op jit(solution)/shard_map/ppermute | solution.py:66
  416.6 13.6 %collective-permute-start.62 = (bf16[288,1024]{1,0:T(8,128)(2,1)S(1)}, bf16[288,1024]{1,0:T(8,128)(2,1)S(1)}, u32[]{:S(2)}, u32[]{:S(2)}) collective-permute-start(bf16[288,1024]{1,0:T(8,128)(2,1)S(1)} %get-tuple-element.43), channel_id=1, source_target_pairs={{0,1},{1,0},{2,3},{3,2},{4,5},{5,4},{6,7},{7,6},{8,9},{9,8},{10,11... | collective-permute-start | bytes 1769480 | tf_op jit(solution)/shard_map/ppermute | solution.py:66
  433.3 39.5 %collective-permute-start.63 = (bf16[288,1024]{1,0:T(8,128)(2,1)S(1)}, bf16[288,1024]{1,0:T(8,128)(2,1)}, u32[]{:S(2)}, u32[]{:S(2)}) collective-permute-start(bf16[288,1024]{1,0:T(8,128)(2,1)S(1)} %fusion.27), channel_id=1, source_target_pairs={{0,2},{1,3},{2,0},{3,1},{4,6},{5,7},{6,4},{7,5},{8,10},{9,11},{10,... | collective-permute-start | bytes 1769480 | tf_op jit(solution)/shard_map/ppermute | solution.py:70
  440.2 15.6 %collective-permute-start.81 = (bf16[8,32,1024]{2,1,0:T(8,128)(2,1)S(1)}, bf16[8,32,1024]{2,1,0:T(8,128)(2,1)S(1)}, u32[]{:S(2)}, u32[]{:S(2)}) collective-permute-start(bf16[8,32,1024]{2,1,0:T(8,128)(2,1)S(1)} %dynamic-slice_bitcast_fusion.3), channel_id=1, source_target_pairs={{0,2},{1,3},{2,0},{3,1},{4,6},{5,7},{6,4},{7,5},{8,10},{9,11},{10,... | collective-permute-start | bytes 1572872 | tf_op jit(solution)/shard_map/ppermute | solution.py:70
  446.3 11.7 %collective-permute-start.73 = (bf16[2,32,768]{2,1,0:T(8,128)(2,1)S(1)}, bf16[2,32,768]{2,1,0:T(8,128)(2,1)S(1)}, u32[]{:S(2)}, u32[]{:S(2)}) collective-permute-start(bf16[2,32,768]{2,1,0:T(8,128)(2,1)S(1)} %dynamic-slice_bitcast_fusion.24), channel_id=1, source_target_pairs={{0,2},{1,3},{2,0},{3,1},{4,6},{5,7},{6,4},{7,5},{8,10},{9,11},{10,... | collective-permute-start | bytes 294920 | tf_op jit(solution)/shard_map/ppermute | solution.py:70
  (114 other events, 845.2 us)

commit v2 on v1

--- a/solution.py
+++ b/solution.py
@@ -12,6 +12,8 @@
 EPSILON = 1e-06
 MASKED = -1e30
 CORES = 2
+EXTRA = 16
+VMEM = pl.BlockSpec(memory_space=pltpu.VMEM)
 F32 = jnp.float32
 BF16 = jnp.bfloat16
 DN_T = (((1,), (1,)), ((), ()))
@@ -102,74 +104,111 @@
 def exchange_seq(place, blocks):
     n = place.nx
     view = blocks.reshape(n, CORES, *blocks.shape[1:])
-    out = jnp.zeros((n, CORES, *blocks.shape[1:]), blocks.dtype)
+    arrived = []
     for k in range(n):
-        peer = (place.x + k) % n
-        send = take(view, peer)
-        if k:
-            send = place.to_x(send, k)
-        source = (place.x - k) % n
-        mine = take(send, place.c)
-        other = place.core(take(send, 1 - place.c))
-        out = put(out, place.pair(mine[None], other[None], 0), source)
-    return out.reshape(blocks.shape)
-
-
-def gather_dp(place, block):
+        send = take(view, (place.x + k) % n)
+        arrived.append(place.to_x(send, k) if k else send)
+    arrived = jnp.stack(arrived)
+    mine = lax.dynamic_index_in_dim(arrived, place.c, 1, keepdims=True)
+    other = place.core(lax.dynamic_index_in_dim(arrived, 1 - place.c, 1, keepdims=True))
+    both = place.pair(mine, other, 1)
+    ordered = jnp.stack([take(both, (place.x - source) % n) for source in range(n)])
+    return ordered.reshape(blocks.shape)
+
+
+def assemble_kernel(plan, counts, where, *refs):
+    blocks, outs = refs[: len(plan)], refs[len(plan) :]
+    ny, nz = counts
+    for block, (k, j, pieces) in zip(blocks, plan):
+        owner = lax.rem(where[0] - k + nz, nz) * ny + lax.rem(where[1] - j + ny, ny)
+        for i, start, size, col in pieces:
+            outs[i][pl.ds(owner, 1), :, col : col + block.shape[1]] = block[start : start + size][None]
+
+
+class Gather:
+    def __init__(self, place, block):
+        self.place, self.here, self.k = place, block, 0
+        self.blocks = [(0, 0, block)]
+
+    def start(self):
+        p = self.place
+        self.sent = [p.to_y(self.here, j) for j in range(1, p.ny)]
+        self.after = p.to_z(self.here, 1) if self.k < p.nz - 1 else self.here
+
+    def settle(self):
+        if self.k == self.place.nz:
+            return
+        sent, after = lax.optimization_barrier((self.sent, self.after))
+        self.blocks += [(self.k, j + 1, b) for j, b in enumerate(sent)]
+        self.k += 1
+        self.here = after
+        if self.k < self.place.nz:
+            self.blocks.append((self.k, 0, after))
+            self.start()
+
+    def finish(self, pieces, shapes):
+        p = self.place
+        plan = [(k, j, pieces) for k, j, _ in self.blocks]
+        return pl.pallas_call(
+            partial(assemble_kernel, plan, (p.ny, p.nz)),
+            in_specs=[pl.BlockSpec(memory_space=pltpu.SMEM)] + [VMEM] * len(plan),
+            out_specs=[VMEM] * len(shapes),
+            out_shape=[jax.ShapeDtypeStruct((p.ny * p.nz, *shape), BF16) for shape in shapes],
+            compiler_params=pltpu.CompilerParams(vmem_limit_bytes=32 << 20),
+        )(jnp.stack([p.z, p.y]), *[b for _, _, b in self.blocks])
+
+
+def scatter_dp(place, views, beside):
     ny, nz = place.ny, place.nz
-    out = jnp.zeros((nz * ny, *block.shape), block.dtype)
-    here = block
-    for k in range(nz):
-        z = (place.z - k) % nz
-        out = put(out, here, z * ny + place.y)
-        for j in range(1, ny):
-            out = put(out, place.to_y(here, j), z * ny + (place.y - j) % ny)
-        if k < nz - 1:
-            here = place.to_z(here, 1)
-    return out.reshape(nz * ny * block.shape[0], *block.shape[1:])
-
-
-def scatter_dp(place, grads):
-    ny, nz = place.ny, place.nz
-    view = grads.astype(BF16).reshape(nz * ny, grads.shape[0] // (nz * ny), *grads.shape[1:])
+
+    def piece(z, y):
+        return jnp.concatenate(
+            [take(v, z * ny + y)[:, c : c + n] for v, c, n in views], axis=0
+        )
+
     total = None
     for k in range(1, nz + 1):
         z = (place.z - k) % nz
-        part = take(view, z * ny + place.y).astype(F32)
+        part = piece(z, place.y).astype(F32)
         for j in range(1, ny):
-            sent = place.to_y(take(view, z * ny + (place.y + j) % ny), j)
+            send = piece(z, (place.y + j) % ny)
+            sent = place.to_y(send, j)
             part = part + sent.astype(F32)
         if total is not None:
-            part = part + place.to_z(total.astype(BF16), 1).astype(F32)
+            send = total.astype(BF16)
+            sent = place.to_z(send, 1)
+            part = part + sent.astype(F32)
+        if k == nz - 1:
+            part, _ = lax.optimization_barrier((part, beside))
         total = part
     return total
 
 
-def all_sum(place, value):
-    for axis, size in (("seq", place.seq), ("dp", place.dp)):
-        bit = 1
-        while bit < size:
-            value = value + lax.ppermute(value, axis, [(i, i ^ bit) for i in range(size)])
-            bit *= 2
-    return value
+def pad_rows(values, cols):
+    return jnp.pad(values, (0, EXTRA * cols - values.shape[0])).reshape(EXTRA, cols)
 
 
 def rows_all(place, rows):
     out = []
     for k in range(place.nx):
-        here = rows if k == 0 else place.to_x(rows, (place.nx - k) % place.nx)
+        here = rows
+        if k:
+            here = place.to_x(rows, place.nx - k)
         out.append(jnp.concatenate([here, place.core(here)], axis=0))
     return out
 
 
-def rows_sum(place, parts):
+def rows_sum(place, part):
     total = None
     for k in reversed(range(place.nx)):
-        low = parts[k].astype(BF16)
+        low = part(k)
+        low = low.astype(BF16)
         half = low.shape[0] // 2
         both = low[:half].astype(F32) + place.core(low[half:]).astype(F32)
         if k:
-            both = place.to_x(both.astype(BF16), k).astype(F32)
+            both = both.astype(BF16)
+            both = place.to_x(both, k)
+            both = both.astype(F32)
         total = both if total is None else total + both
     return total
 
@@ -277,9 +316,6 @@
     @pl.when(i == length // BLOCK - 1)
     def _():
         out_ref[:, width:] = acc_ref[...].astype(BF16)
-
-
-VMEM = pl.BlockSpec(memory_space=pltpu.VMEM)
 
 
 def attend(qkv, seg_row, seg_col, bounds, heads):
@@ -331,6 +367,36 @@
     )(bounds, qkv, mixed, grad, logs, seg_row, seg_col)
 
 
+TILE = 256
+
+
+def grads_kernel(count, *refs):
+    out_ref = refs[-1]
+    out_ref[...] = sum(left_product(refs[i][...], refs[count + i][...]) for i in range(count)).astype(
+        BF16
+    )
+
+
+def weight_grads(lefts, rights):
+    count = len(lefts)
+    inner, cols = lefts[0].shape[1], rights[0].shape[1]
+    tile = min(TILE, inner)
+    return pl.pallas_call(
+        partial(grads_kernel, count),
+        grid=(inner // tile,),
+        in_specs=[pl.BlockSpec((v.shape[0], tile), lambda i: (0, i)) for v in lefts]
+        + [pl.BlockSpec(v.shape, lambda i: (0, 0)) for v in rights],
+        out_specs=pl.BlockSpec((tile, cols), lambda i: (i, 0)),
+        out_shape=jax.ShapeDtypeStruct((inner, cols), BF16),
+        compiler_params=pltpu.CompilerParams(vmem_limit_bytes=40 << 20),
+        cost_estimate=pl.CostEstimate(
+            flops=2 * sum(v.shape[0] for v in lefts) * inner * cols,
+            bytes_accessed=2 * sum(v.size for v in (*lefts, *rights)) + 2 * inner * cols,
+            transcendentals=0,
+        ),
+    )(*lefts, *rights)
+
+
 def gelu_pair(preact):
     half = 0.5 + 0.5 * lax.erf(preact * (2.0**-0.5))
     slope = half + preact * jnp.exp(-0.5 * preact * preact) * 0.3989422804014327
@@ -359,7 +425,6 @@
 ):
     place = Place(dp, seq)
     everyone = dp * seq
-    me = place.d * seq + place.s
     _, count, width = tokens.shape
     hidden_own = up_weight.shape[1] // seq
     heads = HEADS // seq
@@ -369,19 +434,60 @@
     length = segment_ids.shape[1]
     rows = tokens.reshape(count, width)
 
+    qkv_cols = 3 * head_cols
+    smalls = (query_bias, value_bias, out_bias, first_gain, first_shift, down_bias, second_gain, second_shift)
+    packed = jnp.concatenate([*smalls, up_bias])
     qkv_blocks = qkv_weight.reshape(shard, 3, seq, head_cols).transpose(2, 0, 1, 3)
-    qkv_block = exchange_seq(place, qkv_blocks.reshape(seq, shard, 3 * head_cols))
-    full_qkv = gather_dp(place, qkv_block.reshape(seq * shard, 3 * head_cols))
-
-    smalls = (query_bias, value_bias, out_bias, first_gain, first_shift, down_bias, second_gain, second_shift)
-    packed = jnp.concatenate([v.reshape(1, shard) for v in smalls] + [up_bias.reshape(-1, shard)], axis=0)
-    packed = all_sum(
-        place, put(jnp.zeros((everyone, *packed.shape), F32), packed.astype(F32), me)
-    )
-    vectors = packed[:, : len(smalls)].transpose(1, 0, 2).reshape(len(smalls), 1, width)
+    up_blocks = up_weight.reshape(shard, dp, seq, ff_shard).transpose(2, 0, 1, 3)
+    blocks = jnp.concatenate(
+        [qkv_blocks.reshape(seq, shard, qkv_cols), up_blocks.reshape(seq, shard, hidden_own)], axis=2
+    )
+    extra = jnp.broadcast_to(pad_rows(packed, blocks.shape[2]), (seq, EXTRA, blocks.shape[2]))
+    blocks = exchange_seq(place, jnp.concatenate([blocks, extra], axis=1))
+    qkv_block = blocks[:, :shard, :qkv_cols].reshape(seq * shard, qkv_cols)
+    up_block = blocks[:, :shard, qkv_cols:].reshape(seq * shard, hidden_own)
+    packed_seq = blocks[:, shard, : packed.shape[0]].reshape(-1)
+    out_x = jnp.zeros((place.nx, shard, width), BF16)
+    for k in range(place.nx):
+        here = out_weight if k == 0 else place.to_x(out_weight, k)
+        out_x = put(out_x, here, (place.x - k) % place.nx)
+    out_x = out_x.reshape(place.nx * shard, width)
+
+    def columns(a):
+        return [a[:, i : i + head_cols] for i in range(0, a.shape[1], head_cols)]
+
+    stack = [(0, b, i * head_cols) for i, b in enumerate(columns(qkv_block))]
+    stack += [(1, b, i * head_cols) for i, b in enumerate(columns(out_x))]
+    stack += [(2, pad_rows(packed_seq, head_cols), 0)]
+    pieces, at = [], 0
+    for i, b, col in stack:
+        pieces.append((i, at, b.shape[0], col))
+        at += b.shape[0]
+    attention = Gather(place, jnp.concatenate([b for _, b, _ in stack], axis=0))
+    attention.start()
+    for _ in range(place.nz - 1):
+        attention.settle()
+    up_block, down_late, _ = lax.optimization_barrier((up_block, down_weight, attention.here))
+    full_up = lax.all_gather(up_block, "dp", axis=0, tiled=True)
+    full_down = lax.all_gather(down_late, "dp", axis=0, tiled=True)
+    attention.settle()
+    full_qkv, packed_all = attention.finish(
+        [(i // 2, *rest) for i, *rest in pieces if i != 1], ((seq * shard, qkv_cols), (EXTRA, head_cols))
+    )
+    (out_half,) = attention.finish(
+        [(0, *rest) for i, *rest in pieces if i == 1], ((place.nx * shard, width),)
+    )
+    out_half = out_half.reshape(dp * place.nx, 1, shard, width)
+    full_out = place.pair(out_half, place.core(out_half), 1).reshape(width, width)
+    full_qkv = full_qkv.reshape(width, qkv_cols)
+    packed_all = packed_all.reshape(dp, -1)[:, : packed_seq.shape[0]]
+    packed_all = packed_all.reshape(dp, seq, packed.shape[0]).astype(F32)
+    vectors = [
+        packed_all[:, :, i * shard : (i + 1) * shard].reshape(1, width) for i in range(len(smalls))
+    ]
     full_query, full_value, bias_out, gain_one, shift_one, bias_down, gain_two, shift_two = vectors
-    up_bias_all = packed[:, len(smalls) :].reshape(dp, seq, ff_shard)
-    bias_up = lax.dynamic_index_in_dim(up_bias_all, place.s, 1, keepdims=False).reshape(1, hidden_own)
+    bias_up = lax.dynamic_index_in_dim(packed_all, place.s, 1, keepdims=False)
+    bias_up = bias_up[:, len(smalls) * shard :].reshape(1, hidden_own)
 
     row_blocks = rows_all(place, rows)
     all_rows = jnp.zeros((place.nx, CORES * count, width), BF16)
@@ -389,19 +495,6 @@
         mine, other = both[:count], both[count:]
         all_rows = put(all_rows, place.pair(mine, other, 0), (place.x + k) % place.nx)
     all_rows = all_rows.reshape(length, width)
-
-    out_x = jnp.zeros((place.nx, shard, width), BF16)
-    for k in range(place.nx):
-        here = out_weight if k == 0 else place.to_x(out_weight, k)
-        out_x = put(out_x, here, (place.x - k) % place.nx)
-    out_half = gather_dp(place, out_x.reshape(place.nx * shard, width))
-    out_half = out_half.reshape(dp * place.nx, 1, shard, width)
-    full_out = place.pair(out_half, place.core(out_half), 1).reshape(width, width)
-
-    up_blocks = up_weight.reshape(shard, dp, seq, ff_shard).transpose(2, 0, 1, 3)
-    up_block = exchange_seq(place, up_blocks.reshape(seq, shard, hidden_own))
-    full_up = gather_dp(place, up_block.reshape(seq * shard, hidden_own))
-    full_down = gather_dp(place, down_weight)
 
     seg_row = segment_ids
     seg_col = segment_ids.reshape(length, 1)
@@ -424,14 +517,14 @@
     branch = matmul(mixed, full_out) + bias_out
     first, normed_one, factor_one = norm_forward(rows.astype(F32) + branch, gain_one, shift_one)
     first_low = first.astype(BF16)
-
     first_all = rows_all(place, first_low)
     hidden_all, slope_all = [], []
-    for block in first_all:
-        hidden, slope = gelu_pair(matmul(block, full_up) + bias_up)
+    for k, block in enumerate(first_all):
+        preact = matmul(block, full_up)
+        hidden, slope = gelu_pair(preact + bias_up)
         hidden_all.append(hidden)
         slope_all.append(slope)
-    second = rows_sum(place, [matmul(hidden, full_down) for hidden in hidden_all]) + bias_down
+    second = rows_sum(place, lambda k: matmul(hidden_all[k], full_down)) + bias_down
     result, normed_two, factor_two = norm_forward(first + second, gain_two, shift_two)
     output = result.astype(BF16).reshape(tokens.shape)
 
@@ -442,19 +535,16 @@
     second_low = second_grad.astype(BF16)
     down_bias_grad = jnp.sum(second_low, axis=0, dtype=F32)
     second_all = rows_all(place, second_low)
-    preact_all = [
-        (right_product(block, full_down) * slope.astype(F32)).astype(BF16)
-        for block, slope in zip(second_all, slope_all)
-    ]
-    first_grad = second_grad + rows_sum(place, [right_product(p, full_up) for p in preact_all])
-    down_grad = sum(left_product(h, g) for h, g in zip(hidden_all, second_all))
-    up_grad = sum(left_product(f, g) for f, g in zip(first_all, preact_all))
+    preact_all = []
+    for k, (block, slope) in enumerate(zip(second_all, slope_all)):
+        hidden_grad = right_product(block, full_down)
+        preact_all.append((hidden_grad * slope.astype(F32)).astype(BF16))
+    first_grad = second_grad + rows_sum(place, lambda k: right_product(preact_all[k], full_up))
+    down_grad = weight_grads(hidden_all, second_all)
+    down_owned = lax.psum_scatter(down_grad, "dp", scatter_dimension=0, tiled=True).astype(F32)
+    up_grad = weight_grads(first_all, preact_all)
+    up_owned = lax.psum_scatter(up_grad, "dp", scatter_dimension=0, tiled=True)
     up_bias_grad = sum(jnp.sum(p, axis=0, dtype=F32) for p in preact_all)
-    down_owned = scatter_dp(place, down_grad)
-    up_owned = scatter_dp(place, up_grad).astype(BF16)
-    up_owned = up_owned.reshape(seq, shard, hidden_own)
-    up_owned = exchange_seq(place, up_owned).reshape(seq, shard, dp, ff_shard)
-    up_owned = up_owned.transpose(1, 2, 0, 3).reshape(up_weight.shape).astype(F32)
 
     residual_grad, gain_one_grad, shift_one_grad = norm_backward(
         first_grad, normed_one, factor_one, gain_one
@@ -465,58 +555,33 @@
     grad_blocks = mixed_grad.reshape(count, seq, head_cols).transpose(1, 0, 2)
     grad_own = exchange_seq(place, grad_blocks).reshape(length, head_cols)
 
-    out_grad = left_product(mixed, branch_low).astype(BF16)
-    view = out_grad.reshape(dp * place.nx, CORES, shard, width)
+    up_bias_wide = lax.dynamic_update_index_in_dim(
+        jnp.zeros((dp, seq, ff_shard), F32), up_bias_grad.reshape(dp, ff_shard), place.s, 1
+    ).reshape(everyone, ff_shard)
+    vector_sums = (
+        out_bias_grad,
+        gain_one_grad,
+        shift_one_grad,
+        down_bias_grad,
+        gain_two_grad,
+        shift_two_grad,
+    )
+    extra = jnp.concatenate([v.reshape(everyone, shard) for v in vector_sums] + [up_bias_wide], axis=1)
+    wide_count = extra.shape[1]
+    extra = jnp.pad(extra.astype(BF16)[:, None], ((0, 0), (0, EXTRA - 1), (0, width - wide_count)))
+    out_grad = weight_grads([mixed], [branch_low]).reshape(everyone, shard, width)
+    view = jnp.concatenate([out_grad, extra], axis=1)
+    view = view.reshape(dp * place.nx, CORES, shard + EXTRA, width)
     mine = lax.dynamic_index_in_dim(view, place.c, 1, keepdims=False)
     other = lax.dynamic_index_in_dim(view, 1 - place.c, 1, keepdims=False)
     view = (mine.astype(F32) + place.core(other).astype(F32)).astype(BF16)
-    view = view.reshape(dp, place.nx, shard, width)
+    view = view.reshape(dp, place.nx, shard + EXTRA, width)
     summed = lax.dynamic_index_in_dim(view, place.x, 1, keepdims=False).astype(F32)
     for k in range(1, place.nx):
         sent = lax.dynamic_index_in_dim(view, (place.x + k) % place.nx, 1, keepdims=False)
         summed = summed + place.to_x(sent, k).astype(F32)
-    out_owned = scatter_dp(place, summed.reshape(dp * shard, width))
-
-    up_bias_wide = lax.dynamic_update_index_in_dim(
-        jnp.zeros((dp, seq, ff_shard), F32),
-        up_bias_grad.reshape(dp, ff_shard),
-        place.s,
-        1,
-    )
-    wide = jnp.concatenate(
-        [
-            v.reshape(1, width)
-            for v in (
-                out_bias_grad,
-                gain_one_grad,
-                shift_one_grad,
-                down_bias_grad,
-                gain_two_grad,
-                shift_two_grad,
-            )
-        ],
-        axis=0,
-    ).reshape(6, everyone, shard)
-    wide = jnp.concatenate(
-        [wide.transpose(1, 0, 2), up_bias_wide.reshape(everyone, ff_shard // shard, shard)], axis=1
-    )
-    wide = take(all_sum(place, wide), me)
-    out_bias_owned, gain_one_owned, shift_one_owned = wide[0], wide[1], wide[2]
-    down_bias_owned, gain_two_owned, shift_two_owned = wide[3], wide[4], wide[5]
-    up_bias_owned = wide[6:].reshape(ff_shard)
-
     qkv_grad = attend_back(qkv, mixed_own, grad_own, logs, seg_row, seg_col, bounds, heads)
-    joint_grad = left_product(all_rows, qkv_grad)
-    joint_owned = scatter_dp(place, joint_grad).astype(BF16)
-    joint_owned = exchange_seq(place, joint_owned.reshape(seq, shard, 3 * head_cols))
-    joint_owned = joint_owned.reshape(seq, shard, 3, head_cols).transpose(1, 2, 0, 3)
-    joint_owned = joint_owned.reshape(qkv_weight.shape).astype(F32)
-    sums = jnp.sum(qkv_grad, axis=0, dtype=F32).reshape(3, head_cols)
-    ends = jnp.stack([sums[0], sums[2]])[:, None]
-    ends = lax.dynamic_update_slice_in_dim(jnp.zeros((2, seq, head_cols), F32), ends, place.s, 1)
-    ends = all_sum(place, ends.reshape(2, everyone, shard))
-    ends = lax.dynamic_index_in_dim(ends, me, 1, keepdims=False)
-
+    qkv_grad, summed = lax.optimization_barrier((qkv_grad, summed))
     token_parts = right_product(qkv_grad, full_qkv).astype(BF16)
     token_parts = token_parts.reshape(place.nx, CORES, count, width)
     ordered = []
@@ -525,7 +590,43 @@
         ordered.append(
             jnp.concatenate([take(both, place.c), take(both, 1 - place.c)], axis=0)
         )
-    tokens_grad = (residual_grad + rows_sum(place, ordered)).astype(BF16).reshape(tokens.shape)
+    token_sum = rows_sum(place, lambda k: ordered[k])
+    joint_grad = weight_grads([all_rows], [qkv_grad])
+    up_owned = up_owned.reshape(seq, shard, hidden_own)
+    up_owned = exchange_seq(place, up_owned).reshape(seq, shard, dp, ff_shard)
+    up_owned = up_owned.transpose(1, 2, 0, 3).reshape(up_weight.shape).astype(F32)
+
+    joint_grad = joint_grad.reshape(dp, seq * shard, qkv_cols)
+    sums = jnp.sum(qkv_grad, axis=0, dtype=F32).reshape(3, head_cols)
+    ends = jnp.stack([sums[0], sums[2]])
+    ends = lax.dynamic_update_slice_in_dim(jnp.zeros((2, width), F32), ends, own_cols, 1)
+    ends = ends.reshape(2, dp, seq * shard).transpose(1, 0, 2).reshape(dp, 1, 2 * seq * shard)
+    ends = jnp.pad(ends.astype(BF16), ((0, 0), (0, EXTRA - 1), (0, head_cols - 2 * seq * shard)))
+    views = [(joint_grad, i * head_cols, head_cols) for i in range(3)]
+    views += [(ends, 0, head_cols)]
+    views += [(summed.astype(BF16), i, head_cols) for i in range(0, width, head_cols)]
+    owned = scatter_dp(place, views, token_sum)
+    per = seq * shard
+    joint = jnp.concatenate([owned[i * per : (i + 1) * per] for i in range(3)], axis=1).astype(BF16)
+    ends = owned[3 * per]
+    owned = owned[3 * per + EXTRA :].reshape(-1, shard + EXTRA, head_cols)
+    out_owned = owned[:, :shard].transpose(1, 0, 2).reshape(shard, width)
+    wide = owned[:, shard].reshape(width)
+    out_bias_owned, gain_one_owned, shift_one_owned, down_bias_owned, gain_two_owned, shift_two_owned = [
+        wide[i * shard : (i + 1) * shard] for i in range(len(vector_sums))
+    ]
+    up_bias_owned = wide[len(vector_sums) * shard : wide_count]
+    ends = ends[: 2 * per].astype(BF16).reshape(2, seq, shard).transpose(1, 0, 2)
+    ends = jnp.pad(
+        ends.reshape(seq, 1, 2 * shard), ((0, 0), (0, EXTRA - 1), (0, qkv_cols - 2 * shard))
+    )
+    joint = jnp.concatenate([joint.reshape(seq, shard, qkv_cols), ends], axis=1)
+    joint = exchange_seq(place, joint)
+    joint_owned = joint[:, :shard].reshape(seq, shard, 3, head_cols).transpose(1, 2, 0, 3)
+    joint_owned = joint_owned.reshape(qkv_weight.shape).astype(F32)
+    ends = jnp.sum(joint[:, shard, : 2 * shard].astype(F32), axis=0).reshape(2, shard)
+
+    tokens_grad = (residual_grad + token_sum).astype(BF16).reshape(tokens.shape)
     return (
         output,
         tokens_grad,

time: 488 us -> 409 us (0.84)
  waiting for transfers between devices: 239 us -> 175 us
  starting transfers between devices: 85.8 us -> 46.3 us
  matrix products: 46.5 us -> 30.2 us
  Pallas kernels: 28.1 us -> 43.9 us
  between operations: 3.13 us -> 16.1 us
  other arithmetic: 30.6 us -> 37.9 us
  local copies, waits for them, and re-layouts: 47 us -> 52.4 us
    ppermute x15 -> x0, waiting for transfers between devices: 68.7 us -> none  [all_sum(): lax.ppermute(value, axis, [(i, i ^ bit) for i in range(size)])]
    ppermute x24 -> x6, waiting for transfers between devices: 58.1 us -> 17.9 us  [to_z(): lax.ppermute(a, 'dp', [(i, (i // m + k) % n * m + i % m) for i in range(s...]
    ppermute x32 -> x8, starting transfers between devices: 43.2 us -> 8.07 us  [to_y(): lax.ppermute(a, 'dp', [(i, i // n * n + (i % n + k) % n) for i in range(s...]
    ppermute x14 -> x13, waiting for transfers between devices: 51.7 us -> 79.5 us  [to_x(): lax.ppermute(a, 'seq', [(i, (i // CORES + k) % n * CORES + i % CORES) for...]
    reduce_scatter x0 -> x2, waiting for transfers between devices: none -> 24.1 us  [the longest x1 24.1 us: body(): lax.psum_scatter(down_grad, 'dp', scatter_dimension=0, tiled=True)]
    ppermute x32 -> x8, waiting for transfers between devices: 55 us -> 31.2 us  [to_y(): lax.ppermute(a, 'dp', [(i, i // n * n + (i % n + k) % n) for i in range(s...]
    all_gather x0 -> x2, waiting for transfers between devices: none -> 18.2 us  [the longest x1 18.2 us: body(): full_down = lax.all_gather(down_late, 'dp', axis=0, tiled=True)]
    ppermute x15 -> x0, starting transfers between devices: 16.8 us -> none  [all_sum(): lax.ppermute(value, axis, [(i, i ^ bit) for i in range(size)])]
  transfers between devices with their start and end apart: 111 -> 50, of which waited for: 56 -> 27; matrix products, arithmetic and copies ran while one was open for 20% -> 21% of each run, Pallas kernels for 6% -> 11%
where the time goes in v2:
time: 409 us; the launch traced here: 402 us
  waiting for transfers between devices  175 us (43%)
  local copies, waits for them, and re-layouts  52.4 us (13%)
  starting transfers between devices  46.3 us (11%)
  Pallas kernels  43.9 us (11%)
  other arithmetic  37.9 us (9%)
  matrix products  30.2 us (7%)
  between operations  16.1 us (4%)
    ppermute x13, waiting for transfers between devices, to_x(): lax.ppermute(a, 'seq', [(i, (i // CORES + k) % n * CORES + i % CORES) for...  79.5 us
    ppermute x8, waiting for transfers between devices, to_y(): lax.ppermute(a, 'dp', [(i, i // n * n + (i % n + k) % n) for i in range(s...  31.2 us
    reduce_scatter x1, waiting for transfers between devices, body(): lax.psum_scatter(down_grad, 'dp', scatter_dimension=0, tiled=True)  24.1 us
    unnamed x202, local copies, waits for them, and re-layouts  22.5 us
    ppermute x13, starting transfers between devices, to_x(): lax.ppermute(a, 'seq', [(i, (i // CORES + k) % n * CORES + i % CORES) for...  19.8 us
    all_gather x1, waiting for transfers between devices, body(): full_down = lax.all_gather(down_late, 'dp', axis=0, tiled=True)  18.2 us
    ppermute x6, waiting for transfers between devices, to_z(): lax.ppermute(a, 'dp', [(i, (i // m + k) % n * m + i % m) for i in range(s...  17.9 us
    dot_general x6, matrix products, matmul(): return jnp.dot(left, right, preferred_element_type=F32)  16 us
  transfers between devices with their start and end apart: 50, of which 27 were waited for; matrix products, arithmetic and copies ran while one was open for 21% of the time, Pallas kernels for 11%

profile of v2, /device:TPU:0, one launch (start us, length us, event | category | flops | bytes accessed | tf_op | source)
XLA Modules:
  0.0 402.1 jit_solution(313834764144516338)
XLA Ops:
  7.3 6.1 %concatenate.133 = bf16[384]{0:T(512)(128)(2,1)S(1)} concatenate(bf16[32]{0:T(256)(128)(2,1)} %param.19, bf16[32]{0:T(256)(128)(2,1)} %param.20, bf16[32]{0:T(256)(128)(2,1)} %param.22, bf16[32]{0:T(256)(128)(2,1)} %param.23, bf16[32]{0:T(256)(128)(2,1)} %param.24, bf16[32]{0:T(256)(128)(2,1)} %param.28, bf16[32]{0:T(256)(128)(2,1)} %param.29, bf16[32]{0:T(256)(128)(2,1)} %param.30, ...), dimensions={0} | concatenate | bytes 1536 | tf_op jit(solution)/shard_map/concatenate | solution.py:439
  15.4 3.0 collective-permute-start.3
  19.1 8.1 %collective-permute-done.3 = bf16[2,48,1792]{2,1,0:T(8,128)(2,1)S(1)} collective-permute-done((bf16[2,48,1792]{2,1,0:T(8,128)(2,1)S(1)}, bf16[2,48,1792]{2,1,0:T(8,128)(2,1)S(1)}, u32[]{:S(2)}, u32[]{:S(2)}) %collective-permute-start.3) | collective-permute-done | bytes 344096 | tf_op jit(solution)/shard_map/ppermute | solution.py:72
  29.4 1.8 collective-permute-start.6
  32.8 6.6 %collective-permute-done.6.refs_1_ = bf16[656,256]{1,0:T(8,128)(2,1)S(1)} collective-permute-done((bf16[656,256]{1,0:T(8,128)(2,1)S(1)}, bf16[656,256]{1,0:T(8,128)(2,1)S(1)}, u32[]{:S(2)}, u32[]{:S(2)}) %collective-permute-start.6) | collective-permute-done | bytes 335904 | tf_op jit(solution)/shard_map/ppermute | solution.py:80
  39.4 3.3 collective-permute-done.7.refs_2_
  43.3 8.4 %collective-permute-done.8.refs_3_ = bf16[656,256]{1,0:T(8,128)(2,1)S(1)} collective-permute-done((bf16[656,256]{1,0:T(8,128)(2,1)S(1)}, bf16[656,256]{1,0:T(8,128)(2,1)S(1)}, u32[]{:S(2)}, u32[]{:S(2)}) %collective-permute-start.8) | collective-permute-done | bytes 335904 | tf_op jit(solution)/shard_map/ppermute | solution.py:80
  57.6 4.2 %collective-permute-done.10.refs_5_ = bf16[656,256]{1,0:T(8,128)(2,1)S(1)} collective-permute-done((bf16[656,256]{1,0:T(8,128)(2,1)S(1)}, bf16[656,256]{1,0:T(8,128)(2,1)S(1)}, u32[]{:S(2)}, u32[]{:S(2)}) %collective-permute-start.10) | collective-permute-done | bytes 335904 | tf_op jit(solution)/shard_map/ppermute | solution.py:80
  61.8 2.5 collective-permute-done.11.refs_6_
  64.7 3.6 collective-permute-done.1
  74.6 7.9 %collective-permute-done.12.refs_7_ = bf16[656,256]{1,0:T(8,128)(2,1)S(1)} collective-permute-done((bf16[656,256]{1,0:T(8,128)(2,1)S(1)}, bf16[656,256]{1,0:T(8,128)(2,1)S(1)}, u32[]{:S(2)}, u32[]{:S(2)}) %collective-permute-start.12) | collective-permute-done | bytes 335904 | tf_op jit(solution)/shard_map/ppermute | solution.py:80
  87.9 3.5 fusion.qkv_ref
  91.4 13.1 %shard_map.272 = (bf16[1152,256]{1,0:T(8,128)(2,1)S(1)}, f32[4,1152]{1,0:T(4,128)S(1)}) custom-call(s32[6]{0:T(128)S(1)} %pad_add_fusion.bounds, bf16[1152,768]{1,0:T(8,128)(2,1)S(1)} %fusion.qkv_ref, s32[1,1152]{1,0:T(1,128)S(1)} %copy-done.23, s32[1152,1]{1,0:T(8,128)S(1)} %copy-done.17), custom_call_target="tpu_custom_call" | custom-call | flops 1358954496 | bytes 2359296 | tf_op jit(solution)/shard_map/pallas_call | solution.py:324
  106.9 6.6 %collective-permute-done.13 = bf16[2,288,256]{2,1,0:T(8,128)(2,1)S(1)} collective-permute-done((bf16[2,288,256]{2,1,0:T(8,128)(2,1)S(1)}, bf16[2,288,256]{2,1,0:T(8,128)(2,1)S(1)}, u32[]{:S(2)}, u32[]{:S(2)}) %collective-permute-start.13) | collective-permute-done | bytes 294944 | tf_op jit(solution)/shard_map/ppermute | solution.py:72
  123.9 13.8 %collective-permute-done.16 = bf16[288,1024]{1,0:T(8,128)(2,1)S(1)} collective-permute-done((bf16[288,1024]{1,0:T(8,128)(2,1)S(1)}, bf16[288,1024]{1,0:T(8,128)(2,1)S(1)}, u32[]{:S(2)}, u32[]{:S(2)}) %collective-permute-start.16) | collective-permute-done | bytes 589856 | tf_op jit(solution)/shard_map/ppermute | solution.py:72
  141.0 3.3 fusion.54
  145.8 3.4 multiply_convert_fusion.3
  149.2 18.2 %all-gather.5.cloned.1.call-done = bf16[1024,1024]{1,0:T(8,128)(2,1)} async-done(((bf16[128,1024]{1,0:T(8,128)(2,1)}), bf16[1024,1024]{1,0:T(8,128)(2,1)}) %all-gather.5.cloned.1.call-update) | async-done | bytes 2097168 | tf_op jit(solution)/shard_map/all_gather | solution.py:472
  167.4 3.5 convolution_convert_fusion.4
  177.2 14.4 %collective-permute-done.19 = bf16[288,1024]{1,0:T(8,128)(2,1)} collective-permute-done((bf16[288,1024]{1,0:T(8,128)(2,1)}, bf16[288,1024]{1,0:T(8,128)(2,1)}, u32[]{:S(2)}, u32[]{:S(2)}) %collective-permute-start.19) | collective-permute-done | bytes 589856 | tf_op jit(solution)/shard_map/ppermute | solution.py:72
  191.6 2.2 fusion.61
  199.1 12.3 %collective-permute-done.22 = bf16[288,1024]{1,0:T(8,128)(2,1)S(1)} collective-permute-done((bf16[288,1024]{1,0:T(8,128)(2,1)S(1)}, bf16[288,1024]{1,0:T(8,128)(2,1)S(1)}, u32[]{:S(2)}, u32[]{:S(2)}) %collective-permute-start.22) | collective-permute-done | bytes 589856 | tf_op jit(solution)/shard_map/ppermute | solution.py:72
  211.6 2.9 convert_reduce_fusion.2
  214.6 2.4 convert_reduce_fusion.1
  219.9 5.2 %shard_map.277 = bf16[1024,1024]{1,0:T(8,128)(2,1)} custom-call(bf16[576,1024]{1,0:T(8,128)(2,1)S(1)} %pad_maximum_fusion.1.refs_0_, bf16[576,1024]{1,0:T(8,128)(2,1)S(1)} %constant_dynamic-update-slice_fusion.8.refs_1_, bf16[576,1024]{1,0:T(8,128)(2,1)S(1)} %get-tuple-element.158.refs_2_, bf16[576,1024]{1,0:T(8,128)(2,1)S(1)} %get-tuple-element.160.refs_3_), custom_call_target="tpu_custom_call" | custom-call | flops 2415919104 | bytes 6815744 | tf_op jit(solution)/shard_map/pallas_call | solution.py:384
  225.2 10.7 %reduce-scatter.5.cloned.1.call-start = ((), (), s32[]{:S(2)}) async-start(), calls=%async_computation.5 | async-start | bytes 2359296 | tf_op jit(solution)/shard_map/reduce_scatter | solution.py:544
  235.8 3.0 convolution_convert_fusion.1
  240.8 2.2 add_convert_fusion.1
  245.0 13.9 %collective-permute-done.25 = bf16[288,1024]{1,0:T(8,128)(2,1)} collective-permute-done((bf16[288,1024]{1,0:T(8,128)(2,1)}, bf16[288,1024]{1,0:T(8,128)(2,1)}, u32[]{:S(2)}, u32[]{:S(2)}) %collective-permute-start.25) | collective-permute-done | bytes 589856 | tf_op jit(solution)/shard_map/ppermute | solution.py:72
  258.9 3.6 multiply_reduce_fusion
  264.5 2.0 shard_map.275
  267.9 2.4 convolution_convert_fusion.5
  273.5 4.4 %shard_map.278 = bf16[1024,1024]{1,0:T(8,128)(2,1)S(1)} custom-call(bf16[576,1024]{1,0:T(8,128)(2,1)S(1)} %copy-done.28, bf16[576,1024]{1,0:T(8,128)(2,1)S(1)} %copy-done.26, bf16[576,1024]{1,0:T(8,128)(2,1)S(1)} %pad_maximum_fusion.2.refs_2_, bf16[576,1024]{1,0:T(8,128)(2,1)S(1)} %copy-done.22), custom_call_target="tpu_custom_call" | custom-call | flops 2415919104 | bytes 6815744 | tf_op jit(solution)/shard_map/pallas_call | solution.py:384
  279.2 2.2 collective-permute-done.28
  282.6 2.1 fusion.1
  288.9 14.7 %shard_map.274.refs_1_ = bf16[1152,768]{1,0:T(8,128)(2,1)S(1)} custom-call(s32[6]{0:T(128)S(1)} %pad_add_fusion.bounds, bf16[1152,768]{1,0:T(8,128)(2,1)S(1)} %copy-done.32, bf16[1152,256]{1,0:T(8,128)(2,1)S(1)} %copy-done.20, bf16[1152,256]{1,0:T(8,128)(2,1)S(1)} %bitcast.234, f32[4,1152]{1,0:T(4,128)S(1)} %get-tuple-element.43.log_ref, ...), custom_call_target="tpu_custom_call" | custom-call | flops 3397386240 | bytes 4718592 | tf_op jit(solution)/shard_map/pallas_call | solution.py:351
  305.1 2.0 convolution_convert_fusion
  307.2 3.3 shard_map.276
  329.4 4.1 %collective-permute-done.37 = bf16[592,256]{1,0:T(8,128)(2,1)S(1)} collective-permute-done((bf16[592,256]{1,0:T(8,128)(2,1)S(1)}, bf16[592,256]{1,0:T(8,128)(2,1)S(1)}, u32[]{:S(2)}, u32[]{:S(2)}) %collective-permute-start.37) | collective-permute-done | bytes 303136 | tf_op jit(solution)/shard_map/ppermute | solution.py:80
  333.5 3.1 collective-permute-done.39
  337.6 1.7 dynamic-slice_bitcast_fusion.15
  341.0 24.1 %reduce-scatter.5.cloned.1.call-done = bf16[128,1024]{1,0:T(8,128)(2,1)} async-done(((bf16[1024,1024]{1,0:T(8,128)(2,1)}), bf16[128,1024]{1,0:T(8,128)(2,1)}) %reduce-scatter.5.cloned.1.call-update) | async-done | bytes 262160 | tf_op jit(solution)/shard_map/reduce_scatter | solution.py:544
  365.1 1.8 convert_element_type.390
  368.7 2.0 convert_add_fusion.5
  370.7 2.5 fusion.30
  373.1 1.7 collective-permute-start.41
  377.3 7.4 %collective-permute-done.41 = bf16[592,256]{1,0:T(8,128)(2,1)S(1)} collective-permute-done((bf16[592,256]{1,0:T(8,128)(2,1)}, bf16[592,256]{1,0:T(8,128)(2,1)S(1)}, u32[]{:S(2)}, u32[]{:S(2)}) %collective-permute-start.41) | collective-permute-done | bytes 303136 | tf_op jit(solution)/shard_map/ppermute | solution.py:86
  389.0 2.7 collective-permute-done.42
  (444 shorter events, 108.0 us)
Async XLA Ops:
  7.2 133.8 %all-gather.3.cloned.1.call-start = ((), (), s32[]{:S(2)}) async-start(), calls=%async_computation.2 | async-start | bytes 2359296 | tf_op jit(solution)/shard_map/all_gather | solution.py:471
  15.4 11.8 %collective-permute-start.3 = (bf16[2,48,1792]{2,1,0:T(8,128)(2,1)S(1)}, bf16[2,48,1792]{2,1,0:T(8,128)(2,1)S(1)}, u32[]{:S(2)}, u32[]{:S(2)}) collective-permute-start(bf16[2,48,1792]{2,1,0:T(8,128)(2,1)S(1)} %get-tuple-element.101), channel_id=1, source_target_pairs={{0,2},{1,3},{2,0},{3,1},{4,6},{5,7},{6,4},{7,5},{8,10},{9,11},{10,... | collective-permute-start | bytes 1032200 | tf_op jit(solution)/shard_map/ppermute | solution.py:72
  18.4 9.5 %collective-permute-start.5 = (bf16[32,1024]{1,0:T(8,128)(2,1)S(1)}, bf16[32,1024]{1,0:T(8,128)(2,1)S(1)}, u32[]{:S(2)}, u32[]{:S(2)}) collective-permute-start(bf16[32,1024]{1,0:T(8,128)(2,1)S(1)} %copy-done.56), channel_id=1, source_target_pairs={{0,2},{1,3},{2,0},{3,1},{4,6},{5,7},{6,4},{7,5},{8,10},{9,11},{10,... | collective-permute-start | bytes 196616 | tf_op jit(solution)/shard_map/ppermute | solution.py:72
  27.2 1.7 collective-permute-start.4
  29.4 10.0 %collective-permute-start.6 = (bf16[656,256]{1,0:T(8,128)(2,1)S(1)}, bf16[656,256]{1,0:T(8,128)(2,1)S(1)}, u32[]{:S(2)}, u32[]{:S(2)}) collective-permute-start(bf16[656,256]{1,0:T(8,128)(2,1)S(1)} %constant_dynamic-update-slice_fusion.refs_0_), channel_id=1, source_target_pairs={{0,4},{4,0},{8,12},{12,8},{16,20},{20,16},{24,28},{28,24},{1,5},{5... | collective-permute-start | bytes 1007624 | tf_op jit(solution)/shard_map/ppermute | solution.py:80
  31.2 11.5 %collective-permute-start.7 = (bf16[656,256]{1,0:T(8,128)(2,1)S(1)}, bf16[656,256]{1,0:T(8,128)(2,1)S(1)}, u32[]{:S(2)}, u32[]{:S(2)}) collective-permute-start(bf16[656,256]{1,0:T(8,128)(2,1)S(1)} %constant_dynamic-update-slice_fusion.refs_0_), channel_id=1, source_target_pairs={{0,8},{4,12},{8,16},{12,20},{16,24},{20,28},{24,0},{28,4},{1,9},{5... | collective-permute-start | bytes 1007624 | tf_op jit(solution)/shard_map/ppermute | solution.py:86
  42.7 8.9 %collective-permute-start.8 = (bf16[656,256]{1,0:T(8,128)(2,1)S(1)}, bf16[656,256]{1,0:T(8,128)(2,1)S(1)}, u32[]{:S(2)}, u32[]{:S(2)}) collective-permute-start(bf16[656,256]{1,0:T(8,128)(2,1)S(1)} %collective-permute-done.7.refs_2_), channel_id=1, source_target_pairs={{0,4},{4,0},{8,12},{12,8},{16,20},{20,16},{24,28},{28,24},{1,5},{5... | collective-permute-start | bytes 1007624 | tf_op jit(solution)/shard_map/ppermute | solution.py:80
  43.3 10.6 %collective-permute-start.9 = (bf16[656,256]{1,0:T(8,128)(2,1)S(1)}, bf16[656,256]{1,0:T(8,128)(2,1)S(1)}, u32[]{:S(2)}, u32[]{:S(2)}) collective-permute-start(bf16[656,256]{1,0:T(8,128)(2,1)S(1)} %collective-permute-done.7.refs_2_), channel_id=1, source_target_pairs={{0,8},{4,12},{8,16},{12,20},{16,24},{20,28},{24,0},{28,4},{1,9},{5... | collective-permute-start | bytes 1007624 | tf_op jit(solution)/shard_map/ppermute | solution.py:86
  53.9 7.9 %collective-permute-start.10 = (bf16[656,256]{1,0:T(8,128)(2,1)S(1)}, bf16[656,256]{1,0:T(8,128)(2,1)S(1)}, u32[]{:S(2)}, u32[]{:S(2)}) collective-permute-start(bf16[656,256]{1,0:T(8,128)(2,1)S(1)} %collective-permute-done.9.refs_4_), channel_id=1, source_target_pairs={{0,4},{4,0},{8,12},{12,8},{16,20},{20,16},{24,28},{28,24},{1,5},{5... | collective-permute-start | bytes 1007624 | tf_op jit(solution)/shard_map/ppermute | solution.py:80
  55.2 9.2 %collective-permute-start.11 = (bf16[656,256]{1,0:T(8,128)(2,1)S(1)}, bf16[656,256]{1,0:T(8,128)(2,1)S(1)}, u32[]{:S(2)}, u32[]{:S(2)}) collective-permute-start(bf16[656,256]{1,0:T(8,128)(2,1)S(1)} %collective-permute-done.9.refs_4_), channel_id=1, source_target_pairs={{0,8},{4,12},{8,16},{12,20},{16,24},{20,28},{24,0},{28,4},{1,9},{5... | collective-permute-start | bytes 1007624 | tf_op jit(solution)/shard_map/ppermute | solution.py:86
  55.2 13.1 %collective-permute-start.1 = (bf16[288,1024]{1,0:T(8,128)(2,1)}, bf16[288,1024]{1,0:T(8,128)(2,1)}, u32[]{:S(2)}, u32[]{:S(2)}) collective-permute-start(bf16[288,1024]{1,0:T(8,128)(2,1)} %bitcast.273), channel_id=1, source_target_pairs={{0,2},{1,3},{2,0},{3,1},{4,6},{5,7},{6,4},{7,5},{8,10},{9,11},{10,... | collective-permute-start | bytes 1769480 | tf_op jit(solution)/shard_map/ppermute | solution.py:72
  56.7 12.9 %collective-permute-start = (bf16[288,1024]{1,0:T(8,128)(2,1)}, bf16[288,1024]{1,0:T(8,128)(2,1)S(1)}, u32[]{:S(2)}, u32[]{:S(2)}) collective-permute-start(bf16[288,1024]{1,0:T(8,128)(2,1)} %bitcast.274), channel_id=1, source_target_pairs={{0,1},{1,0},{2,3},{3,2},{4,5},{5,4},{6,7},{7,6},{8,9},{9,8},{10,11... | collective-permute-start | bytes 1769480 | tf_op jit(solution)/shard_map/ppermute | solution.py:68
  64.4 103.0 %all-gather.5.cloned.1.call-start = ((), (), s32[]{:S(2)}) async-start(), calls=%async_computation.3 | async-start | bytes 2359296 | tf_op jit(solution)/shard_map/all_gather | solution.py:472
  68.3 4.7 %collective-permute-start.2 = (bf16[288,1024]{1,0:T(8,128)(2,1)}, bf16[288,1024]{1,0:T(8,128)(2,1)}, u32[]{:S(2)}, u32[]{:S(2)}) collective-permute-start(bf16[288,1024]{1,0:T(8,128)(2,1)} %collective-permute-done.1), channel_id=1, source_target_pairs={{0,1},{1,0},{2,3},{3,2},{4,5},{5,4},{6,7},{7,6},{8,9},{9,8},{10,11... | collective-permute-start | bytes 1769480 | tf_op jit(solution)/shard_map/ppermute | solution.py:68
  72.0 10.4 %collective-permute-start.12 = (bf16[656,256]{1,0:T(8,128)(2,1)S(1)}, bf16[656,256]{1,0:T(8,128)(2,1)S(1)}, u32[]{:S(2)}, u32[]{:S(2)}) collective-permute-start(bf16[656,256]{1,0:T(8,128)(2,1)S(1)} %copy-done.13), channel_id=1, source_target_pairs={{0,4},{4,0},{8,12},{12,8},{16,20},{20,16},{24,28},{28,24},{1,5},{5... | collective-permute-start | bytes 1007624 | tf_op jit(solution)/shard_map/ppermute | solution.py:80
  104.6 8.8 %collective-permute-start.13 = (bf16[2,288,256]{2,1,0:T(8,128)(2,1)S(1)}, bf16[2,288,256]{2,1,0:T(8,128)(2,1)S(1)}, u32[]{:S(2)}, u32[]{:S(2)}) collective-permute-start(bf16[2,288,256]{2,1,0:T(8,128)(2,1)S(1)} %get-tuple-element.109), channel_id=1, source_target_pairs={{0,2},{1,3},{2,0},{3,1},{4,6},{5,7},{6,4},{7,5},{8,10},{9,11},{10,... | collective-permute-start | bytes 884744 | tf_op jit(solution)/shard_map/ppermute | solution.py:72
  106.8 10.8 %collective-permute-start.15 = (bf16[16,1,32,1024]{3,2,1,0:T(8,128)(2,1)S(1)}, bf16[16,1,32,1024]{3,2,1,0:T(8,128)(2,1)}, u32[]{:S(2)}, u32[]{:S(2)}) collective-permute-start(bf16[16,1,32,1024]{3,2,1,0:T(8,128)(2,1)S(1)} %bitcast.227), channel_id=1, source_target_pairs={{0,1},{1,0},{2,3},{3,2},{4,5},{5,4},{6,7},{7,6},{8,9},{9,8},{10,11... | collective-permute-start | bytes 3145736 | tf_op jit(solution)/shard_map/ppermute | solution.py:68
  114.3 223.3 %reduce-scatter.3.cloned.1.call-start = ((), (), s32[]{:S(2)}) async-start(), calls=%async_computation.4 | async-start | bytes 2359296 | tf_op jit(solution)/shard_map/reduce_scatter | solution.py:546
  122.3 15.4 %collective-permute-start.16 = (bf16[288,1024]{1,0:T(8,128)(2,1)S(1)}, bf16[288,1024]{1,0:T(8,128)(2,1)S(1)}, u32[]{:S(2)}, u32[]{:S(2)}) collective-permute-start(bf16[288,1024]{1,0:T(8,128)(2,1)S(1)} %fusion.28), channel_id=1, source_target_pairs={{0,2},{1,3},{2,0},{3,1},{4,6},{5,7},{6,4},{7,5},{8,10},{9,11},{10,... | collective-permute-start | bytes 1769480 | tf_op jit(solution)/shard_map/ppermute | solution.py:72
  137.7 2.1 collective-permute-start.17
  137.7 3.2 collective-permute-start.20
  170.9 3.5 collective-permute-start.18
  174.5 2.7 collective-permute-start.21
  175.6 16.1 %collective-permute-start.19 = (bf16[288,1024]{1,0:T(8,128)(2,1)}, bf16[288,1024]{1,0:T(8,128)(2,1)}, u32[]{:S(2)}, u32[]{:S(2)}) collective-permute-start(bf16[288,1024]{1,0:T(8,128)(2,1)} %add_convert_fusion.3), channel_id=1, source_target_pairs={{0,2},{1,3},{2,0},{3,1},{4,6},{5,7},{6,4},{7,5},{8,10},{9,11},{10,... | collective-permute-start | bytes 1769480 | tf_op jit(solution)/shard_map/ppermute | solution.py:72
  196.4 15.0 %collective-permute-start.22 = (bf16[288,1024]{1,0:T(8,128)(2,1)S(1)}, bf16[288,1024]{1,0:T(8,128)(2,1)S(1)}, u32[]{:S(2)}, u32[]{:S(2)}) collective-permute-start(bf16[288,1024]{1,0:T(8,128)(2,1)S(1)} %get-tuple-element.61), channel_id=1, source_target_pairs={{0,2},{1,3},{2,0},{3,1},{4,6},{5,7},{6,4},{7,5},{8,10},{9,11},{10,... | collective-permute-start | bytes 1769480 | tf_op jit(solution)/shard_map/ppermute | solution.py:72
  198.0 13.5 %collective-permute-start.26 = (bf16[288,1024]{1,0:T(8,128)(2,1)S(1)}, bf16[288,1024]{1,0:T(8,128)(2,1)S(1)}, u32[]{:S(2)}, u32[]{:S(2)}) collective-permute-start(bf16[288,1024]{1,0:T(8,128)(2,1)S(1)} %get-tuple-element.61), channel_id=1, source_target_pairs={{0,1},{1,0},{2,3},{3,2},{4,5},{5,4},{6,7},{7,6},{8,9},{9,8},{10,11... | collective-permute-start | bytes 1769480 | tf_op jit(solution)/shard_map/ppermute | solution.py:68
  211.5 3.0 collective-permute-start.23
  219.4 20.7 %collective-permute-start.24 = (bf16[288,1024]{1,0:T(8,128)(2,1)}, bf16[288,1024]{1,0:T(8,128)(2,1)}, u32[]{:S(2)}, u32[]{:S(2)}) collective-permute-start(bf16[288,1024]{1,0:T(8,128)(2,1)} %slice.463), channel_id=1, source_target_pairs={{0,1},{1,0},{2,3},{3,2},{4,5},{5,4},{6,7},{7,6},{8,9},{9,8},{10,11... | collective-permute-start | bytes 1769480 | tf_op jit(solution)/shard_map/ppermute | solution.py:68
  225.2 140.0 %reduce-scatter.5.cloned.1.call-start = ((), (), s32[]{:S(2)}) async-start(), calls=%async_computation.5 | async-start | bytes 2359296 | tf_op jit(solution)/shard_map/reduce_scatter | solution.py:544
  239.7 5.2 %collective-permute-start.27 = (bf16[288,1024]{1,0:T(8,128)(2,1)}, bf16[288,1024]{1,0:T(8,128)(2,1)S(1)}, u32[]{:S(2)}, u32[]{:S(2)}) collective-permute-start(bf16[288,1024]{1,0:T(8,128)(2,1)} %slice.465), channel_id=1, source_target_pairs={{0,1},{1,0},{2,3},{3,2},{4,5},{5,4},{6,7},{7,6},{8,9},{9,8},{10,11... | collective-permute-start | bytes 1769480 | tf_op jit(solution)/shard_map/ppermute | solution.py:68
  243.0 15.9 %collective-permute-start.25 = (bf16[288,1024]{1,0:T(8,128)(2,1)}, bf16[288,1024]{1,0:T(8,128)(2,1)}, u32[]{:S(2)}, u32[]{:S(2)}) collective-permute-start(bf16[288,1024]{1,0:T(8,128)(2,1)} %add_convert_fusion.1), channel_id=1, source_target_pairs={{0,2},{1,3},{2,0},{3,1},{4,6},{5,7},{6,4},{7,5},{8,10},{9,11},{10,... | collective-permute-start | bytes 1769480 | tf_op jit(solution)/shard_map/ppermute | solution.py:72
  267.9 14.6 %collective-permute-start.30 = (bf16[16,48,1024]{2,1,0:T(8,128)(2,1)}, bf16[16,48,1024]{2,1,0:T(8,128)(2,1)}, u32[]{:S(2)}, u32[]{:S(2)}) collective-permute-start(bf16[16,48,1024]{2,1,0:T(8,128)(2,1)} %fusion.13), channel_id=1, source_target_pairs={{0,1},{1,0},{2,3},{3,2},{4,5},{5,4},{6,7},{7,6},{8,9},{9,8},{10,11... | collective-permute-start | bytes 4718600 | tf_op jit(solution)/shard_map/ppermute | solution.py:68
  271.7 9.7 %collective-permute-start.28 = (bf16[2,288,256]{2,1,0:T(8,128)(2,1)}, bf16[2,288,256]{2,1,0:T(8,128)(2,1)}, u32[]{:S(2)}, u32[]{:S(2)}) collective-permute-start(bf16[2,288,256]{2,1,0:T(8,128)(2,1)} %get-tuple-element.105), channel_id=1, source_target_pairs={{0,2},{1,3},{2,0},{3,1},{4,6},{5,7},{6,4},{7,5},{8,10},{9,11},{10,... | collective-permute-start | bytes 884744 | tf_op jit(solution)/shard_map/ppermute | solution.py:72
  282.5 3.9 collective-permute-start.29
  284.8 20.0 %collective-permute-start.31 = (bf16[8,48,1024]{2,1,0:T(8,128)(2,1)S(1)}, bf16[8,48,1024]{2,1,0:T(8,128)(2,1)S(1)}, u32[]{:S(2)}, u32[]{:S(2)}) collective-permute-start(bf16[8,48,1024]{2,1,0:T(8,128)(2,1)S(1)} %dynamic-slice_bitcast_fusion), channel_id=1, source_target_pairs={{0,2},{1,3},{2,0},{3,1},{4,6},{5,7},{6,4},{7,5},{8,10},{9,11},{10,... | collective-permute-start | bytes 2359304 | tf_op jit(solution)/shard_map/ppermute | solution.py:72
  311.7 59.0 %collective-permute-start.34 = (bf16[288,1024]{1,0:T(8,128)(2,1)}, bf16[288,1024]{1,0:T(8,128)(2,1)}, u32[]{:S(2)}, u32[]{:S(2)}) collective-permute-start(bf16[288,1024]{1,0:T(8,128)(2,1)} %get-tuple-element.69), channel_id=1, source_target_pairs={{0,1},{1,0},{2,3},{3,2},{4,5},{5,4},{6,7},{7,6},{8,9},{9,8},{10,11... | collective-permute-start | bytes 1769480 | tf_op jit(solution)/shard_map/ppermute | solution.py:68
  311.8 15.1 %collective-permute-start.32 = (bf16[288,1024]{1,0:T(8,128)(2,1)S(1)}, bf16[288,1024]{1,0:T(8,128)(2,1)S(1)}, u32[]{:S(2)}, u32[]{:S(2)}) collective-permute-start(bf16[288,1024]{1,0:T(8,128)(2,1)S(1)} %get-tuple-element.68), channel_id=1, source_target_pairs={{0,1},{1,0},{2,3},{3,2},{4,5},{5,4},{6,7},{7,6},{8,9},{9,8},{10,11... | collective-permute-start | bytes 1769480 | tf_op jit(solution)/shard_map/ppermute | solution.py:68
  312.6 12.0 %collective-permute-start.38 = (bf16[592,256]{1,0:T(8,128)(2,1)S(1)}, bf16[592,256]{1,0:T(8,128)(2,1)S(1)}, u32[]{:S(2)}, u32[]{:S(2)}) collective-permute-start(bf16[592,256]{1,0:T(8,128)(2,1)S(1)} %constant_dynamic-update-slice_fusion.68), channel_id=1, source_target_pairs={{0,4},{4,0},{8,12},{12,8},{16,20},{20,16},{24,28},{28,24},{1,5},{5... | collective-permute-start | bytes 909320 | tf_op jit(solution)/shard_map/ppermute | solution.py:80
  313.5 20.0 %collective-permute-start.37 = (bf16[592,256]{1,0:T(8,128)(2,1)S(1)}, bf16[592,256]{1,0:T(8,128)(2,1)S(1)}, u32[]{:S(2)}, u32[]{:S(2)}) collective-permute-start(bf16[592,256]{1,0:T(8,128)(2,1)S(1)} %constant_dynamic-update-slice_fusion.52), channel_id=1, source_target_pairs={{0,4},{4,0},{8,12},{12,8},{16,20},{20,16},{24,28},{28,24},{1,5},{5... | collective-permute-start | bytes 909320 | tf_op jit(solution)/shard_map/ppermute | solution.py:80
  320.0 48.5 %collective-permute-start.36 = (bf16[592,256]{1,0:T(8,128)(2,1)}, bf16[592,256]{1,0:T(8,128)(2,1)}, u32[]{:S(2)}, u32[]{:S(2)}) collective-permute-start(bf16[592,256]{1,0:T(8,128)(2,1)} %constant_dynamic-update-slice_fusion.36), channel_id=1, source_target_pairs={{0,4},{4,0},{8,12},{12,8},{16,20},{20,16},{24,28},{28,24},{1,5},{5... | collective-permute-start | bytes 909320 | tf_op jit(solution)/shard_map/ppermute | solution.py:80
  324.7 11.8 %collective-permute-start.39 = (bf16[592,256]{1,0:T(8,128)(2,1)S(1)}, bf16[592,256]{1,0:T(8,128)(2,1)S(1)}, u32[]{:S(2)}, u32[]{:S(2)}) collective-permute-start(bf16[592,256]{1,0:T(8,128)(2,1)S(1)} %add_convert_fusion.5), channel_id=1, source_target_pairs={{0,8},{4,12},{8,16},{12,20},{16,24},{20,28},{24,0},{28,4},{1,9},{5... | collective-permute-start | bytes 909320 | tf_op jit(solution)/shard_map/ppermute | solution.py:86
  327.9 42.7 %collective-permute-start.33 = (bf16[288,1024]{1,0:T(8,128)(2,1)}, bf16[288,1024]{1,0:T(8,128)(2,1)}, u32[]{:S(2)}, u32[]{:S(2)}) collective-permute-start(bf16[288,1024]{1,0:T(8,128)(2,1)} %fusion.27), channel_id=1, source_target_pairs={{0,2},{1,3},{2,0},{3,1},{4,6},{5,7},{6,4},{7,5},{8,10},{9,11},{10,... | collective-permute-start | bytes 1769480 | tf_op jit(solution)/shard_map/ppermute | solution.py:72
  337.4 31.2 %collective-permute-start.40 = (bf16[592,256]{1,0:T(8,128)(2,1)}, bf16[592,256]{1,0:T(8,128)(2,1)}, u32[]{:S(2)}, u32[]{:S(2)}) collective-permute-start(bf16[592,256]{1,0:T(8,128)(2,1)} %add_convert_fusion.4), channel_id=1, source_target_pairs={{0,8},{4,12},{8,16},{12,20},{16,24},{20,28},{24,0},{28,4},{1,9},{5... | collective-permute-start | bytes 909320 | tf_op jit(solution)/shard_map/ppermute | solution.py:86
  339.3 27.6 %collective-permute-start.44 = (bf16[2,32,1024]{2,1,0:T(8,128)(2,1)}, bf16[2,32,1024]{2,1,0:T(8,128)(2,1)}, u32[]{:S(2)}, u32[]{:S(2)}) collective-permute-start(bf16[2,32,1024]{2,1,0:T(8,128)(2,1)} %get-tuple-element.124), channel_id=1, source_target_pairs={{0,2},{1,3},{2,0},{3,1},{4,6},{5,7},{6,4},{7,5},{8,10},{9,11},{10,... | collective-permute-start | bytes 393224 | tf_op jit(solution)/shard_map/ppermute | solution.py:72
  366.9 10.4 %collective-permute-start.35 = (bf16[592,256]{1,0:T(8,128)(2,1)}, bf16[592,256]{1,0:T(8,128)(2,1)}, u32[]{:S(2)}, u32[]{:S(2)}) collective-permute-start(bf16[592,256]{1,0:T(8,128)(2,1)} %copy-done.57), channel_id=1, source_target_pairs={{0,4},{4,0},{8,12},{12,8},{16,20},{20,16},{24,28},{28,24},{1,5},{5... | collective-permute-start | bytes 909320 | tf_op jit(solution)/shard_map/ppermute | solution.py:80
  368.6 6.2 %collective-permute-start.45 = (bf16[2,1,32,1024]{3,2,1,0:T(8,128)(2,1)S(1)}, bf16[2,1,32,1024]{3,2,1,0:T(8,128)(2,1)S(1)}, u32[]{:S(2)}, u32[]{:S(2)}) collective-permute-start(bf16[2,1,32,1024]{3,2,1,0:T(8,128)(2,1)S(1)} %fusion.49), channel_id=1, source_target_pairs={{0,1},{1,0},{2,3},{3,2},{4,5},{5,4},{6,7},{7,6},{8,9},{9,8},{10,11... | collective-permute-start | bytes 393224 | tf_op jit(solution)/shard_map/ppermute | solution.py:68
  373.1 11.6 %collective-permute-start.41 = (bf16[592,256]{1,0:T(8,128)(2,1)}, bf16[592,256]{1,0:T(8,128)(2,1)S(1)}, u32[]{:S(2)}, u32[]{:S(2)}) collective-permute-start(bf16[592,256]{1,0:T(8,128)(2,1)} %convert_add_fusion.5), channel_id=1, source_target_pairs={{0,8},{4,12},{8,16},{12,20},{16,24},{20,28},{24,0},{28,4},{1,9},{5... | collective-permute-start | bytes 909320 | tf_op jit(solution)/shard_map/ppermute | solution.py:86
  386.2 5.5 %collective-permute-start.42 = (bf16[2,48,768]{2,1,0:T(8,128)(2,1)S(1)}, bf16[2,48,768]{2,1,0:T(8,128)(2,1)S(1)}, u32[]{:S(2)}, u32[]{:S(2)}) collective-permute-start(bf16[2,48,768]{2,1,0:T(8,128)(2,1)S(1)} %get-tuple-element.120), channel_id=1, source_target_pairs={{0,2},{1,3},{2,0},{3,1},{4,6},{5,7},{6,4},{7,5},{8,10},{9,11},{10,... | collective-permute-start | bytes 442376 | tf_op jit(solution)/shard_map/ppermute | solution.py:72
  (67 other events, 372.6 us)
Sparse Core Ops, SparseCore 0:
  64.5 48.2 all-gather.2
  114.9 52.4 all-gather.4
  225.3 66.1 reduce-scatter.2
  294.9 70.2 reduce-scatter.4

commit v3 on v2

--- a/solution.py
+++ b/solution.py
@@ -184,32 +184,32 @@
     return total
 
 
-def pad_rows(values, cols):
-    return jnp.pad(values, (0, EXTRA * cols - values.shape[0])).reshape(EXTRA, cols)
-
-
-def rows_all(place, rows):
-    out = []
+def rows_each(place, rows, work):
+    sent = [place.to_x(rows, place.nx - k) for k in range(1, place.nx)]
+    blocks, done = [], []
     for k in range(place.nx):
         here = rows
         if k:
-            here = place.to_x(rows, place.nx - k)
-        out.append(jnp.concatenate([here, place.core(here)], axis=0))
-    return out
-
-
-def rows_sum(place, part):
-    total = None
+            here, _ = lax.optimization_barrier((sent[k - 1], done[-1]))
+        blocks.append(jnp.concatenate([here, place.core(here)], axis=0))
+        done.append(work(k, blocks[-1]))
+    return blocks, done
+
+
+def rows_sum(place, values, part):
+    total, both = None, None
     for k in reversed(range(place.nx)):
-        low = part(k)
-        low = low.astype(BF16)
+        value = values[k]
+        if both is not None:
+            value, _ = lax.optimization_barrier((value, both))
+        low = part(value).astype(BF16)
         half = low.shape[0] // 2
         both = low[:half].astype(F32) + place.core(low[half:]).astype(F32)
+        term = both
         if k:
             both = both.astype(BF16)
-            both = place.to_x(both, k)
-            both = both.astype(F32)
-        total = both if total is None else total + both
+            term = place.to_x(both, k).astype(F32)
+        total = term if total is None else total + term
     return total
 
 
@@ -372,29 +372,42 @@
 
 def grads_kernel(count, *refs):
     out_ref = refs[-1]
-    out_ref[...] = sum(left_product(refs[i][...], refs[count + i][...]) for i in range(count)).astype(
-        BF16
-    )
-
-
-def weight_grads(lefts, rights):
-    count = len(lefts)
-    inner, cols = lefts[0].shape[1], rights[0].shape[1]
+    at = 0
+    for i in range(0, len(refs) - 1, 2 * count):
+        lefts, rights = refs[i : i + count], refs[i + count : i + 2 * count]
+        cols = rights[0].shape[1]
+        total = sum(left_product(a[...], b[...]) for a, b in zip(lefts, rights))
+        out_ref[:, at : at + cols] = total.astype(BF16)
+        at += cols
+
+
+def weight_grads(*sides):
+    count = len(sides[0])
+    inner = sides[0][0].shape[1]
+    cols = sum(rights[0].shape[1] for rights in sides[1::2])
     tile = min(TILE, inner)
+    specs, values = [], []
+    for n, side in enumerate(sides):
+        for v in side:
+            values.append(v)
+            if n % 2:
+                specs.append(VMEM)
+            else:
+                specs.append(pl.BlockSpec((v.shape[0], tile), lambda i: (0, i)))
+    rows = sum(v.shape[0] for v in sides[0])
     return pl.pallas_call(
         partial(grads_kernel, count),
         grid=(inner // tile,),
-        in_specs=[pl.BlockSpec((v.shape[0], tile), lambda i: (0, i)) for v in lefts]
-        + [pl.BlockSpec(v.shape, lambda i: (0, 0)) for v in rights],
+        in_specs=specs,
         out_specs=pl.BlockSpec((tile, cols), lambda i: (i, 0)),
         out_shape=jax.ShapeDtypeStruct((inner, cols), BF16),
         compiler_params=pltpu.CompilerParams(vmem_limit_bytes=40 << 20),
         cost_estimate=pl.CostEstimate(
-            flops=2 * sum(v.shape[0] for v in lefts) * inner * cols,
-            bytes_accessed=2 * sum(v.size for v in (*lefts, *rights)) + 2 * inner * cols,
+            flops=2 * rows * inner * cols,
+            bytes_accessed=2 * sum(v.size for v in values) + 2 * inner * cols,
             transcendentals=0,
         ),
-    )(*lefts, *rights)
+    )(*values)
 
 
 def gelu_pair(preact):
@@ -436,17 +449,21 @@
 
     qkv_cols = 3 * head_cols
     smalls = (query_bias, value_bias, out_bias, first_gain, first_shift, down_bias, second_gain, second_shift)
-    packed = jnp.concatenate([*smalls, up_bias])
+    up_rows = ff_shard // shard
+    packed = jnp.concatenate([v.reshape(1, shard) for v in smalls] + [up_bias.reshape(up_rows, shard)])
+    vector_count = packed.shape[0]
     qkv_blocks = qkv_weight.reshape(shard, 3, seq, head_cols).transpose(2, 0, 1, 3)
     up_blocks = up_weight.reshape(shard, dp, seq, ff_shard).transpose(2, 0, 1, 3)
     blocks = jnp.concatenate(
         [qkv_blocks.reshape(seq, shard, qkv_cols), up_blocks.reshape(seq, shard, hidden_own)], axis=2
     )
-    extra = jnp.broadcast_to(pad_rows(packed, blocks.shape[2]), (seq, EXTRA, blocks.shape[2]))
+    extra = jnp.pad(packed, ((0, EXTRA - vector_count), (0, blocks.shape[2] - shard)))
+    extra = jnp.broadcast_to(extra, (seq, *extra.shape))
     blocks = exchange_seq(place, jnp.concatenate([blocks, extra], axis=1))
     qkv_block = blocks[:, :shard, :qkv_cols].reshape(seq * shard, qkv_cols)
     up_block = blocks[:, :shard, qkv_cols:].reshape(seq * shard, hidden_own)
-    packed_seq = blocks[:, shard, : packed.shape[0]].reshape(-1)
+    packed_seq = blocks[:, shard:, :shard].transpose(1, 0, 2).reshape(EXTRA, seq * shard)
+    packed_seq = jnp.pad(packed_seq, ((0, 0), (0, head_cols - seq * shard)))
     out_x = jnp.zeros((place.nx, shard, width), BF16)
     for k in range(place.nx):
         here = out_weight if k == 0 else place.to_x(out_weight, k)
@@ -458,16 +475,18 @@
 
     stack = [(0, b, i * head_cols) for i, b in enumerate(columns(qkv_block))]
     stack += [(1, b, i * head_cols) for i, b in enumerate(columns(out_x))]
-    stack += [(2, pad_rows(packed_seq, head_cols), 0)]
+    stack += [(2, packed_seq, 0)]
     pieces, at = [], 0
     for i, b, col in stack:
         pieces.append((i, at, b.shape[0], col))
         at += b.shape[0]
     attention = Gather(place, jnp.concatenate([b for _, b, _ in stack], axis=0))
     attention.start()
-    for _ in range(place.nz - 1):
+    for step in range(place.nz - 1):
         attention.settle()
-    up_block, down_late, _ = lax.optimization_barrier((up_block, down_weight, attention.here))
+        if step == place.nz - 3:
+            early = attention.here
+    up_block, down_late, _ = lax.optimization_barrier((up_block, down_weight, early))
     full_up = lax.all_gather(up_block, "dp", axis=0, tiled=True)
     full_down = lax.all_gather(down_late, "dp", axis=0, tiled=True)
     attention.settle()
@@ -480,16 +499,13 @@
     out_half = out_half.reshape(dp * place.nx, 1, shard, width)
     full_out = place.pair(out_half, place.core(out_half), 1).reshape(width, width)
     full_qkv = full_qkv.reshape(width, qkv_cols)
-    packed_all = packed_all.reshape(dp, -1)[:, : packed_seq.shape[0]]
-    packed_all = packed_all.reshape(dp, seq, packed.shape[0]).astype(F32)
-    vectors = [
-        packed_all[:, :, i * shard : (i + 1) * shard].reshape(1, width) for i in range(len(smalls))
-    ]
+    packed_all = packed_all[:, :vector_count, : seq * shard].astype(F32)
+    vectors = [packed_all[:, i].reshape(1, width) for i in range(len(smalls))]
     full_query, full_value, bias_out, gain_one, shift_one, bias_down, gain_two, shift_two = vectors
-    bias_up = lax.dynamic_index_in_dim(packed_all, place.s, 1, keepdims=False)
-    bias_up = bias_up[:, len(smalls) * shard :].reshape(1, hidden_own)
-
-    row_blocks = rows_all(place, rows)
+    bias_up = packed_all[:, len(smalls) :].reshape(dp, up_rows, seq, shard)
+    bias_up = lax.dynamic_index_in_dim(bias_up, place.s, 2, keepdims=False).reshape(1, hidden_own)
+
+    row_blocks, _ = rows_each(place, rows, lambda k, block: ())
     all_rows = jnp.zeros((place.nx, CORES * count, width), BF16)
     for k, both in enumerate(row_blocks):
         mine, other = both[:count], both[count:]
@@ -517,14 +533,11 @@
     branch = matmul(mixed, full_out) + bias_out
     first, normed_one, factor_one = norm_forward(rows.astype(F32) + branch, gain_one, shift_one)
     first_low = first.astype(BF16)
-    first_all = rows_all(place, first_low)
-    hidden_all, slope_all = [], []
-    for k, block in enumerate(first_all):
-        preact = matmul(block, full_up)
-        hidden, slope = gelu_pair(preact + bias_up)
-        hidden_all.append(hidden)
-        slope_all.append(slope)
-    second = rows_sum(place, lambda k: matmul(hidden_all[k], full_down)) + bias_down
+    first_all, hidden_slopes = rows_each(
+        place, first_low, lambda k, block: gelu_pair(matmul(block, full_up) + bias_up)
+    )
+    hidden_all = [hidden for hidden, _ in hidden_slopes]
+    second = rows_sum(place, hidden_all, lambda hidden: matmul(hidden, full_down)) + bias_down
     result, normed_two, factor_two = norm_forward(first + second, gain_two, shift_two)
     output = result.astype(BF16).reshape(tokens.shape)
 
@@ -534,16 +547,23 @@
     )
     second_low = second_grad.astype(BF16)
     down_bias_grad = jnp.sum(second_low, axis=0, dtype=F32)
-    second_all = rows_all(place, second_low)
-    preact_all = []
-    for k, (block, slope) in enumerate(zip(second_all, slope_all)):
-        hidden_grad = right_product(block, full_down)
-        preact_all.append((hidden_grad * slope.astype(F32)).astype(BF16))
-    first_grad = second_grad + rows_sum(place, lambda k: right_product(preact_all[k], full_up))
-    down_grad = weight_grads(hidden_all, second_all)
-    down_owned = lax.psum_scatter(down_grad, "dp", scatter_dimension=0, tiled=True).astype(F32)
-    up_grad = weight_grads(first_all, preact_all)
-    up_owned = lax.psum_scatter(up_grad, "dp", scatter_dimension=0, tiled=True)
+    second_all, preact_all = rows_each(
+        place,
+        second_low,
+        lambda k, block: (
+            right_product(block, full_down) * hidden_slopes[k][1].astype(F32)
+        ).astype(BF16),
+    )
+    first_grad = second_grad + rows_sum(place, preact_all, lambda p: right_product(p, full_up))
+    if hidden_own == width:
+        both_grads = weight_grads(hidden_all, second_all, first_all, preact_all)
+        both_owned = lax.psum_scatter(both_grads, "dp", scatter_dimension=0, tiled=True)
+        down_owned, up_owned = both_owned[:, :width].astype(F32), both_owned[:, width:]
+    else:
+        down_grad = weight_grads(hidden_all, second_all)
+        down_owned = lax.psum_scatter(down_grad, "dp", scatter_dimension=0, tiled=True).astype(F32)
+        up_grad = weight_grads(first_all, preact_all)
+        up_owned = lax.psum_scatter(up_grad, "dp", scatter_dimension=0, tiled=True)
     up_bias_grad = sum(jnp.sum(p, axis=0, dtype=F32) for p in preact_all)
 
     residual_grad, gain_one_grad, shift_one_grad = norm_backward(
@@ -590,11 +610,8 @@
         ordered.append(
             jnp.concatenate([take(both, place.c), take(both, 1 - place.c)], axis=0)
         )
-    token_sum = rows_sum(place, lambda k: ordered[k])
+    token_sum = rows_sum(place, ordered, lambda v: v)
     joint_grad = weight_grads([all_rows], [qkv_grad])
-    up_owned = up_owned.reshape(seq, shard, hidden_own)
-    up_owned = exchange_seq(place, up_owned).reshape(seq, shard, dp, ff_shard)
-    up_owned = up_owned.transpose(1, 2, 0, 3).reshape(up_weight.shape).astype(F32)
 
     joint_grad = joint_grad.reshape(dp, seq * shard, qkv_cols)
     sums = jnp.sum(qkv_grad, axis=0, dtype=F32).reshape(3, head_cols)
@@ -622,6 +639,10 @@
     )
     joint = jnp.concatenate([joint.reshape(seq, shard, qkv_cols), ends], axis=1)
     joint = exchange_seq(place, joint)
+    up_owned, joint = lax.optimization_barrier((up_owned, joint))
+    up_owned = up_owned.reshape(seq, shard, hidden_own)
+    up_owned = exchange_seq(place, up_owned).reshape(seq, shard, dp, ff_shard)
+    up_owned = up_owned.transpose(1, 2, 0, 3).reshape(up_weight.shape).astype(F32)
     joint_owned = joint[:, :shard].reshape(seq, shard, 3, head_cols).transpose(1, 2, 0, 3)
     joint_owned = joint_owned.reshape(qkv_weight.shape).astype(F32)
     ends = jnp.sum(joint[:, shard, : 2 * shard].astype(F32), axis=0).reshape(2, shard)

time: 409 us -> 397 us (0.971); the launches traced: 402 us -> 397 us
  waiting for transfers between devices: 175 us -> 187 us
  other arithmetic: 37.9 us -> 30.6 us
  matrix products: 30.2 us -> 25.7 us
    ppermute x6, starting transfers between devices: 5 us -> 18.5 us  [to_z(): lax.ppermute(a, 'dp', [(i, (i // m + k) % n * m + i % m) for i in range(s...]
    reduce_scatter x2 -> x1, waiting for transfers between devices: 24.1 us -> 12.6 us  [body(): lax.psum_scatter(both_grads, 'dp', scatter_dimension=0, tiled=True)]
    ppermute x8, waiting for transfers between devices: 31.2 us -> 42.1 us  [to_y(): lax.ppermute(a, 'dp', [(i, i // n * n + (i % n + k) % n) for i in range(s...]
    reduce_scatter x2 -> x1, starting transfers between devices: 11 us -> 0.3 us  [body(): lax.psum_scatter(both_grads, 'dp', scatter_dimension=0, tiled=True)]
    ppermute x13, waiting for transfers between devices: 79.5 us -> 69.9 us  [to_x(): lax.ppermute(a, 'seq', [(i, (i // CORES + k) % n * CORES + i % CORES) for...]
    ppermute x19, waiting for transfers between devices: 4.38 us -> 12.4 us  [core(): return lax.ppermute(a, 'seq', [(i, i ^ 1) for i in range(self.seq)])]
    ppermute x6, waiting for transfers between devices: 17.9 us -> 25.6 us  [to_z(): lax.ppermute(a, 'dp', [(i, (i // m + k) % n * m + i % m) for i in range(s...]
    all_gather x1, waiting for transfers between devices: 18.2 us -> 23.8 us  [body(): full_down = lax.all_gather(down_late, 'dp', axis=0, tiled=True)]
  transfers between devices with their start and end apart: 50 -> 49, of which waited for: 27 -> 36; matrix products, arithmetic and copies ran while one was open for 21% -> 12% of each run, Pallas kernels for 11% -> 10%
where the time goes in v3:
time: 397 us
  waiting for transfers between devices  187 us (47%)
  local copies, waits for them, and re-layouts  48.5 us (12%)
  starting transfers between devices  47.3 us (12%)
  Pallas kernels  42.2 us (11%)
  other arithmetic  30.6 us (8%)
  matrix products  25.7 us (6%)
  between operations  16.1 us (4%)
    ppermute x13, waiting for transfers between devices, to_x(): lax.ppermute(a, 'seq', [(i, (i // CORES + k) % n * CORES + i % CORES) for...  69.9 us
    ppermute x8, waiting for transfers between devices, to_y(): lax.ppermute(a, 'dp', [(i, i // n * n + (i % n + k) % n) for i in range(s...  42.1 us
    ppermute x6, waiting for transfers between devices, to_z(): lax.ppermute(a, 'dp', [(i, (i // m + k) % n * m + i % m) for i in range(s...  25.6 us
    all_gather x1, waiting for transfers between devices, body(): full_down = lax.all_gather(down_late, 'dp', axis=0, tiled=True)  23.8 us
    ppermute x13, starting transfers between devices, to_x(): lax.ppermute(a, 'seq', [(i, (i // CORES + k) % n * CORES + i % CORES) for...  18.8 us
    ppermute x6, starting transfers between devices, to_z(): lax.ppermute(a, 'dp', [(i, (i // m + k) % n * m + i % m) for i in range(s...  18.5 us
    unnamed x192, local copies, waits for them, and re-layouts  18.4 us
    dot_general x6, matrix products, matmul(): return jnp.dot(left, right, preferred_element_type=F32)  15.3 us
  transfers between devices with their start and end apart: 49, of which 36 were waited for; matrix products, arithmetic and copies ran while one was open for 12% of the time, Pallas kernels for 10%

profile of v3, /device:TPU:0, one launch (start us, length us, event | category | flops | bytes accessed | tf_op | source)
XLA Modules:
  0.0 396.9 jit_solution(8821050348055096985)
XLA Ops:
  10.2 3.0 collective-permute-start.3
  13.9 8.1 %collective-permute-done.3 = bf16[2,48,1792]{2,1,0:T(8,128)(2,1)S(1)} collective-permute-done((bf16[2,48,1792]{2,1,0:T(8,128)(2,1)S(1)}, bf16[2,48,1792]{2,1,0:T(8,128)(2,1)S(1)}, u32[]{:S(2)}, u32[]{:S(2)}) %collective-permute-start.3) | collective-permute-done | bytes 344096 | tf_op jit(solution)/shard_map/ppermute | solution.py:72
  27.6 6.6 %collective-permute-done.6.refs_1_ = bf16[656,256]{1,0:T(8,128)(2,1)S(1)} collective-permute-done((bf16[656,256]{1,0:T(8,128)(2,1)S(1)}, bf16[656,256]{1,0:T(8,128)(2,1)S(1)}, u32[]{:S(2)}, u32[]{:S(2)}) %collective-permute-start.6) | collective-permute-done | bytes 335904 | tf_op jit(solution)/shard_map/ppermute | solution.py:80
  34.2 3.3 collective-permute-done.7.refs_2_
  40.3 6.1 %collective-permute-done.8.refs_3_ = bf16[656,256]{1,0:T(8,128)(2,1)S(1)} collective-permute-done((bf16[656,256]{1,0:T(8,128)(2,1)S(1)}, bf16[656,256]{1,0:T(8,128)(2,1)S(1)}, u32[]{:S(2)}, u32[]{:S(2)}) %collective-permute-start.8) | collective-permute-done | bytes 335904 | tf_op jit(solution)/shard_map/ppermute | solution.py:80
  46.4 2.3 collective-permute-done.9.refs_4_
  49.3 3.3 collective-permute-done.1
  57.1 9.1 %collective-permute-done.10.refs_5_ = bf16[656,256]{1,0:T(8,128)(2,1)S(1)} collective-permute-done((bf16[656,256]{1,0:T(8,128)(2,1)S(1)}, bf16[656,256]{1,0:T(8,128)(2,1)S(1)}, u32[]{:S(2)}, u32[]{:S(2)}) %collective-permute-start.10) | collective-permute-done | bytes 335904 | tf_op jit(solution)/shard_map/ppermute | solution.py:80
  66.2 7.2 %collective-permute-done.11.refs_6_ = bf16[656,256]{1,0:T(8,128)(2,1)S(1)} collective-permute-done((bf16[656,256]{1,0:T(8,128)(2,1)S(1)}, bf16[656,256]{1,0:T(8,128)(2,1)S(1)}, u32[]{:S(2)}, u32[]{:S(2)}) %collective-permute-start.11) | collective-permute-done | bytes 335904 | tf_op jit(solution)/shard_map/ppermute | solution.py:86
  75.1 8.7 %collective-permute-done.12.refs_7_ = bf16[656,256]{1,0:T(8,128)(2,1)S(1)} collective-permute-done((bf16[656,256]{1,0:T(8,128)(2,1)S(1)}, bf16[656,256]{1,0:T(8,128)(2,1)S(1)}, u32[]{:S(2)}, u32[]{:S(2)}) %collective-permute-start.12) | collective-permute-done | bytes 335904 | tf_op jit(solution)/shard_map/ppermute | solution.py:80
  85.6 2.0 fusion.qkv_ref
  87.6 13.1 %shard_map.272 = (bf16[1152,256]{1,0:T(8,128)(2,1)S(1)}, f32[4,1152]{1,0:T(4,128)S(1)}) custom-call(s32[6]{0:T(128)S(1)} %pad_add_fusion.bounds, bf16[1152,768]{1,0:T(8,128)(2,1)S(1)} %fusion.qkv_ref, s32[1,1152]{1,0:T(1,128)S(1)} %copy-done.13, s32[1152,1]{1,0:T(8,128)S(1)} %copy.68.seg_col), custom_call_target="tpu_custom_call" | custom-call | flops 1358954496 | bytes 2359296 | tf_op jit(solution)/shard_map/pallas_call | solution.py:324
  100.8 2.5 collective-permute-start.13
  104.0 4.0 %collective-permute-done.13 = bf16[2,288,256]{2,1,0:T(8,128)(2,1)S(1)} collective-permute-done((bf16[2,288,256]{2,1,0:T(8,128)(2,1)S(1)}, bf16[2,288,256]{2,1,0:T(8,128)(2,1)S(1)}, u32[]{:S(2)}, u32[]{:S(2)}) %collective-permute-start.13) | collective-permute-done | bytes 294944 | tf_op jit(solution)/shard_map/ppermute | solution.py:72
  116.7 2.0 collective-permute-start.16
  119.8 5.1 %fusion.6 = (bf16[576,1024]{1,0:T(8,128)(2,1)}, bf16[576,1024]{1,0:T(8,128)(2,1)S(1)}) fusion(f32[1024]{0:T(1024)S(1)} %add.555, bf16[1024,1024]{1,0:T(8,128)(2,1)} %all-gather.3.cloned.1.call-done, bf16[288,1024]{1,0:T(8,128)(2,1)} %copy-done.43, bf16[288,1024]{1,0:T(8,128)(2,1)S(1)} %fusion.27), kind=kOutput, calls=%fused_computation.16 | convolution fusion | flops 1217396736 | bytes 5640192 | tf_op jit(solution)/shard_map/dot_general | solution.py:24
  124.9 7.7 %collective-permute-done.16 = bf16[288,1024]{1,0:T(8,128)(2,1)S(1)} collective-permute-done((bf16[288,1024]{1,0:T(8,128)(2,1)S(1)}, bf16[288,1024]{1,0:T(8,128)(2,1)S(1)}, u32[]{:S(2)}, u32[]{:S(2)}) %collective-permute-start.16) | collective-permute-done | bytes 589856 | tf_op jit(solution)/shard_map/ppermute | solution.py:72
  134.6 2.9 multiply_convert_fusion.2
  138.6 23.8 %all-gather.5.cloned.1.call-done = bf16[1024,1024]{1,0:T(8,128)(2,1)} async-done(((bf16[128,1024]{1,0:T(8,128)(2,1)}), bf16[1024,1024]{1,0:T(8,128)(2,1)}) %all-gather.5.cloned.1.call-update) | async-done | bytes 2097168 | tf_op jit(solution)/shard_map/all_gather | solution.py:491
  162.4 3.0 convolution_convert_fusion.4
  165.5 2.0 collective-permute-done.19
  171.3 13.7 %collective-permute-done.20 = bf16[288,1024]{1,0:T(8,128)(2,1)S(1)} collective-permute-done((bf16[288,1024]{1,0:T(8,128)(2,1)S(1)}, bf16[288,1024]{1,0:T(8,128)(2,1)S(1)}, u32[]{:S(2)}, u32[]{:S(2)}) %collective-permute-start.20) | collective-permute-done | bytes 589856 | tf_op jit(solution)/shard_map/ppermute | solution.py:72
  191.4 12.3 %collective-permute-done.22 = bf16[288,1024]{1,0:T(8,128)(2,1)S(1)} collective-permute-done((bf16[288,1024]{1,0:T(8,128)(2,1)S(1)}, bf16[288,1024]{1,0:T(8,128)(2,1)S(1)}, u32[]{:S(2)}, u32[]{:S(2)}) %collective-permute-start.22) | collective-permute-done | bytes 589856 | tf_op jit(solution)/shard_map/ppermute | solution.py:72
  203.7 2.0 collective-permute-done.24
  205.7 12.5 %constant_dynamic-update-slice_fusion.10.refs_3_ = bf16[576,1024]{1,0:T(8,128)(2,1)S(1)} fusion(bf16[576,1024]{1,0:T(8,128)(2,1)S(1)} %constant_dynamic-update-slice_fusion.11, bf16[288,1024]{1,0:T(8,128)(2,1)S(1)} %collective-permute-done.24), kind=kLoop, calls=%fused_computation.193 | loop fusion | bytes 1179648 | tf_op jit(solution)/shard_map/concatenate | solution.py:194
  218.2 2.4 convert_reduce_fusion.1
  231.7 13.0 %collective-permute-done.26 = bf16[288,1024]{1,0:T(8,128)(2,1)} collective-permute-done((bf16[288,1024]{1,0:T(8,128)(2,1)}, bf16[288,1024]{1,0:T(8,128)(2,1)}, u32[]{:S(2)}, u32[]{:S(2)}) %collective-permute-start.26) | collective-permute-done | bytes 589856 | tf_op jit(solution)/shard_map/ppermute | solution.py:72
  244.6 3.7 multiply_reduce_fusion
  249.8 2.0 shard_map.275
  253.9 2.3 pad_maximum_fusion.1.refs_4_
  259.8 2.5 reshape.439
  272.4 7.9 %shard_map.276 = bf16[1024,2048]{1,0:T(8,128)(2,1)S(1)} custom-call(bf16[576,1024]{1,0:T(8,128)(2,1)S(1)} %copy-done.17, bf16[576,1024]{1,0:T(8,128)(2,1)S(1)} %copy-done.19, bf16[576,1024]{1,0:T(8,128)(2,1)S(1)} %copy-done.4, bf16[576,1024]{1,0:T(8,128)(2,1)S(1)} %copy-done.12, bf16[576,1024]{1,0:T(8,128)(2,1)S(1)} %copy-done.3, ...), custom_call_target="tpu_custom_call" | custom-call | flops 4831838208 | bytes 13631488 | tf_op jit(solution)/shard_map/pallas_call | solution.py:398
  280.3 2.0 copy-done
  283.7 2.1 fusion.1
  289.4 14.7 %shard_map.274.refs_1_ = bf16[1152,768]{1,0:T(8,128)(2,1)S(1)} custom-call(s32[6]{0:T(128)S(1)} %pad_add_fusion.bounds, bf16[1152,768]{1,0:T(8,128)(2,1)S(1)} %copy-done.25, bf16[1152,256]{1,0:T(8,128)(2,1)S(1)} %copy-done.8, bf16[1152,256]{1,0:T(8,128)(2,1)S(1)} %bitcast.245, f32[4,1152]{1,0:T(4,128)S(1)} %get-tuple-element.54.log_ref, ...), custom_call_target="tpu_custom_call" | custom-call | flops 3397386240 | bytes 4718592 | tf_op jit(solution)/shard_map/pallas_call | solution.py:351
  306.1 2.0 convolution_convert_fusion
  308.2 3.2 shard_map.277
  317.4 5.3 %collective-permute-done.38 = bf16[592,256]{1,0:T(8,128)(2,1)S(1)} collective-permute-done((bf16[592,256]{1,0:T(8,128)(2,1)S(1)}, bf16[592,256]{1,0:T(8,128)(2,1)S(1)}, u32[]{:S(2)}, u32[]{:S(2)}) %collective-permute-start.38) | collective-permute-done | bytes 303136 | tf_op jit(solution)/shard_map/ppermute | solution.py:80
  322.8 8.9 %collective-permute-start.39 = (bf16[592,256]{1,0:T(8,128)(2,1)S(1)}, bf16[592,256]{1,0:T(8,128)(2,1)S(1)}, u32[]{:S(2)}, u32[]{:S(2)}) collective-permute-start(bf16[592,256]{1,0:T(8,128)(2,1)S(1)} %add_convert_fusion.5), channel_id=1, source_target_pairs={{0,8},{4,12},{8,16},{12,20},{16,24},{20,28},{24,0},{28,4},{1,9},{5... | collective-permute-start | bytes 909320 | tf_op jit(solution)/shard_map/ppermute | solution.py:86
  332.6 2.0 collective-permute-done.37
  336.5 3.4 collective-permute-start.40
  339.9 4.1 %collective-permute-done.36 = bf16[592,256]{1,0:T(8,128)(2,1)S(1)} collective-permute-done((bf16[592,256]{1,0:T(8,128)(2,1)S(1)}, bf16[592,256]{1,0:T(8,128)(2,1)S(1)}, u32[]{:S(2)}, u32[]{:S(2)}) %collective-permute-start.36) | collective-permute-done | bytes 303136 | tf_op jit(solution)/shard_map/ppermute | solution.py:80
  344.1 4.0 %collective-permute-done.40 = bf16[592,256]{1,0:T(8,128)(2,1)S(1)} collective-permute-done((bf16[592,256]{1,0:T(8,128)(2,1)S(1)}, bf16[592,256]{1,0:T(8,128)(2,1)S(1)}, u32[]{:S(2)}, u32[]{:S(2)}) %collective-permute-start.40) | collective-permute-done | bytes 303136 | tf_op jit(solution)/shard_map/ppermute | solution.py:86
  349.4 3.6 collective-permute-start.41
  353.1 7.0 %collective-permute-done.41 = bf16[592,256]{1,0:T(8,128)(2,1)S(1)} collective-permute-done((bf16[592,256]{1,0:T(8,128)(2,1)S(1)}, bf16[592,256]{1,0:T(8,128)(2,1)S(1)}, u32[]{:S(2)}, u32[]{:S(2)}) %collective-permute-start.41) | collective-permute-done | bytes 303136 | tf_op jit(solution)/shard_map/ppermute | solution.py:86
  362.4 3.4 collective-permute-done.42
  367.3 12.6 %reduce-scatter.2.cloned.1.call-done = bf16[128,2048]{1,0:T(8,128)(2,1)} async-done(((bf16[1024,2048]{1,0:T(8,128)(2,1)}), bf16[128,2048]{1,0:T(8,128)(2,1)}) %reduce-scatter.2.cloned.1.call-update) | async-done | bytes 524304 | tf_op jit(solution)/shard_map/reduce_scatter | solution.py:560
  384.8 2.3 collective-permute-done.44
  (424 shorter events, 99.7 us)
Async XLA Ops:
  7.2 112.6 %all-gather.3.cloned.1.call-start = ((), (), s32[]{:S(2)}) async-start(), calls=%async_computation.1 | async-start | bytes 2359296 | tf_op jit(solution)/shard_map/all_gather | solution.py:490
  10.2 11.8 %collective-permute-start.3 = (bf16[2,48,1792]{2,1,0:T(8,128)(2,1)S(1)}, bf16[2,48,1792]{2,1,0:T(8,128)(2,1)S(1)}, u32[]{:S(2)}, u32[]{:S(2)}) collective-permute-start(bf16[2,48,1792]{2,1,0:T(8,128)(2,1)S(1)} %get-tuple-element.118), channel_id=1, source_target_pairs={{0,2},{1,3},{2,0},{3,1},{4,6},{5,7},{6,4},{7,5},{8,10},{9,11},{10,... | collective-permute-start | bytes 1032200 | tf_op jit(solution)/shard_map/ppermute | solution.py:72
  13.2 9.5 %collective-permute-start.5 = (bf16[32,1024]{1,0:T(8,128)(2,1)S(1)}, bf16[32,1024]{1,0:T(8,128)(2,1)S(1)}, u32[]{:S(2)}, u32[]{:S(2)}) collective-permute-start(bf16[32,1024]{1,0:T(8,128)(2,1)S(1)} %copy-done.47), channel_id=1, source_target_pairs={{0,2},{1,3},{2,0},{3,1},{4,6},{5,7},{6,4},{7,5},{8,10},{9,11},{10,... | collective-permute-start | bytes 196616 | tf_op jit(solution)/shard_map/ppermute | solution.py:72
  22.0 1.7 collective-permute-start.4
  24.2 10.0 %collective-permute-start.6 = (bf16[656,256]{1,0:T(8,128)(2,1)S(1)}, bf16[656,256]{1,0:T(8,128)(2,1)S(1)}, u32[]{:S(2)}, u32[]{:S(2)}) collective-permute-start(bf16[656,256]{1,0:T(8,128)(2,1)S(1)} %constant_dynamic-update-slice_fusion.refs_0_), channel_id=1, source_target_pairs={{0,4},{4,0},{8,12},{12,8},{16,20},{20,16},{24,28},{28,24},{1,5},{5... | collective-permute-start | bytes 1007624 | tf_op jit(solution)/shard_map/ppermute | solution.py:80
  26.0 11.5 %collective-permute-start.7 = (bf16[656,256]{1,0:T(8,128)(2,1)S(1)}, bf16[656,256]{1,0:T(8,128)(2,1)S(1)}, u32[]{:S(2)}, u32[]{:S(2)}) collective-permute-start(bf16[656,256]{1,0:T(8,128)(2,1)S(1)} %constant_dynamic-update-slice_fusion.refs_0_), channel_id=1, source_target_pairs={{0,8},{4,12},{8,16},{12,20},{16,24},{20,28},{24,0},{28,4},{1,9},{5... | collective-permute-start | bytes 1007624 | tf_op jit(solution)/shard_map/ppermute | solution.py:86
  37.5 8.9 %collective-permute-start.8 = (bf16[656,256]{1,0:T(8,128)(2,1)S(1)}, bf16[656,256]{1,0:T(8,128)(2,1)S(1)}, u32[]{:S(2)}, u32[]{:S(2)}) collective-permute-start(bf16[656,256]{1,0:T(8,128)(2,1)S(1)} %collective-permute-done.7.refs_2_), channel_id=1, source_target_pairs={{0,4},{4,0},{8,12},{12,8},{16,20},{20,16},{24,28},{28,24},{1,5},{5... | collective-permute-start | bytes 1007624 | tf_op jit(solution)/shard_map/ppermute | solution.py:80
  38.0 10.6 %collective-permute-start.9 = (bf16[656,256]{1,0:T(8,128)(2,1)S(1)}, bf16[656,256]{1,0:T(8,128)(2,1)S(1)}, u32[]{:S(2)}, u32[]{:S(2)}) collective-permute-start(bf16[656,256]{1,0:T(8,128)(2,1)S(1)} %collective-permute-done.7.refs_2_), channel_id=1, source_target_pairs={{0,8},{4,12},{8,16},{12,20},{16,24},{20,28},{24,0},{28,4},{1,9},{5... | collective-permute-start | bytes 1007624 | tf_op jit(solution)/shard_map/ppermute | solution.py:86
  38.0 14.6 %collective-permute-start.1 = (bf16[288,1024]{1,0:T(8,128)(2,1)}, bf16[288,1024]{1,0:T(8,128)(2,1)}, u32[]{:S(2)}, u32[]{:S(2)}) collective-permute-start(bf16[288,1024]{1,0:T(8,128)(2,1)} %bitcast.283), channel_id=1, source_target_pairs={{0,2},{1,3},{2,0},{3,1},{4,6},{5,7},{6,4},{7,5},{8,10},{9,11},{10,... | collective-permute-start | bytes 1769480 | tf_op jit(solution)/shard_map/ppermute | solution.py:72
  48.7 113.7 %all-gather.5.cloned.1.call-start = ((), (), s32[]{:S(2)}) async-start(), calls=%async_computation.2 | async-start | bytes 2359296 | tf_op jit(solution)/shard_map/all_gather | solution.py:491
  48.7 6.5 %collective-permute-start = (bf16[288,1024]{1,0:T(8,128)(2,1)}, bf16[288,1024]{1,0:T(8,128)(2,1)}, u32[]{:S(2)}, u32[]{:S(2)}) collective-permute-start(bf16[288,1024]{1,0:T(8,128)(2,1)} %bitcast.284), channel_id=1, source_target_pairs={{0,1},{1,0},{2,3},{3,2},{4,5},{5,4},{6,7},{7,6},{8,9},{9,8},{10,11... | collective-permute-start | bytes 1769480 | tf_op jit(solution)/shard_map/ppermute | solution.py:68
  52.6 21.0 %collective-permute-start.2 = (bf16[288,1024]{1,0:T(8,128)(2,1)}, bf16[288,1024]{1,0:T(8,128)(2,1)}, u32[]{:S(2)}, u32[]{:S(2)}) collective-permute-start(bf16[288,1024]{1,0:T(8,128)(2,1)} %collective-permute-done.1), channel_id=1, source_target_pairs={{0,1},{1,0},{2,3},{3,2},{4,5},{5,4},{6,7},{7,6},{8,9},{9,8},{10,11... | collective-permute-start | bytes 1769480 | tf_op jit(solution)/shard_map/ppermute | solution.py:68
  53.1 13.1 %collective-permute-start.10 = (bf16[656,256]{1,0:T(8,128)(2,1)S(1)}, bf16[656,256]{1,0:T(8,128)(2,1)S(1)}, u32[]{:S(2)}, u32[]{:S(2)}) collective-permute-start(bf16[656,256]{1,0:T(8,128)(2,1)S(1)} %collective-permute-done.9.refs_4_), channel_id=1, source_target_pairs={{0,4},{4,0},{8,12},{12,8},{16,20},{20,16},{24,28},{28,24},{1,5},{5... | collective-permute-start | bytes 1007624 | tf_op jit(solution)/shard_map/ppermute | solution.py:80
  54.3 19.1 %collective-permute-start.11 = (bf16[656,256]{1,0:T(8,128)(2,1)S(1)}, bf16[656,256]{1,0:T(8,128)(2,1)S(1)}, u32[]{:S(2)}, u32[]{:S(2)}) collective-permute-start(bf16[656,256]{1,0:T(8,128)(2,1)S(1)} %collective-permute-done.9.refs_4_), channel_id=1, source_target_pairs={{0,8},{4,12},{8,16},{12,20},{16,24},{20,28},{24,0},{28,4},{1,9},{5... | collective-permute-start | bytes 1007624 | tf_op jit(solution)/shard_map/ppermute | solution.py:86
  73.4 10.4 %collective-permute-start.12 = (bf16[656,256]{1,0:T(8,128)(2,1)S(1)}, bf16[656,256]{1,0:T(8,128)(2,1)S(1)}, u32[]{:S(2)}, u32[]{:S(2)}) collective-permute-start(bf16[656,256]{1,0:T(8,128)(2,1)S(1)} %collective-permute-done.11.refs_6_), channel_id=1, source_target_pairs={{0,4},{4,0},{8,12},{12,8},{16,20},{20,16},{24,28},{28,24},{1,5},{5... | collective-permute-start | bytes 1007624 | tf_op jit(solution)/shard_map/ppermute | solution.py:80
  100.8 7.2 %collective-permute-start.13 = (bf16[2,288,256]{2,1,0:T(8,128)(2,1)S(1)}, bf16[2,288,256]{2,1,0:T(8,128)(2,1)S(1)}, u32[]{:S(2)}, u32[]{:S(2)}) collective-permute-start(bf16[2,288,256]{2,1,0:T(8,128)(2,1)S(1)} %get-tuple-element.126), channel_id=1, source_target_pairs={{0,2},{1,3},{2,0},{3,1},{4,6},{5,7},{6,4},{7,5},{8,10},{9,11},{10,... | collective-permute-start | bytes 884744 | tf_op jit(solution)/shard_map/ppermute | solution.py:72
  103.9 8.2 %collective-permute-start.15 = (bf16[16,1,32,1024]{3,2,1,0:T(8,128)(2,1)S(1)}, bf16[16,1,32,1024]{3,2,1,0:T(8,128)(2,1)}, u32[]{:S(2)}, u32[]{:S(2)}) collective-permute-start(bf16[16,1,32,1024]{3,2,1,0:T(8,128)(2,1)S(1)} %bitcast.238), channel_id=1, source_target_pairs={{0,1},{1,0},{2,3},{3,2},{4,5},{5,4},{6,7},{7,6},{8,9},{9,8},{10,11... | collective-permute-start | bytes 3145736 | tf_op jit(solution)/shard_map/ppermute | solution.py:68
  108.7 1.6 collective-permute-start.14
  108.8 271.1 %reduce-scatter.2.cloned.1.call-start = ((), (), s32[]{:S(2)}) async-start(), calls=%async_computation.3 | async-start | bytes 4718592 | tf_op jit(solution)/shard_map/reduce_scatter | solution.py:560
  116.5 2.4 collective-permute-start.17
  116.7 15.9 %collective-permute-start.16 = (bf16[288,1024]{1,0:T(8,128)(2,1)S(1)}, bf16[288,1024]{1,0:T(8,128)(2,1)S(1)}, u32[]{:S(2)}, u32[]{:S(2)}) collective-permute-start(bf16[288,1024]{1,0:T(8,128)(2,1)S(1)} %fusion.27), channel_id=1, source_target_pairs={{0,2},{1,3},{2,0},{3,1},{4,6},{5,7},{6,4},{7,5},{8,10},{9,11},{10,... | collective-permute-start | bytes 1769480 | tf_op jit(solution)/shard_map/ppermute | solution.py:72
  132.6 2.0 collective-permute-start.18
  165.5 2.1 collective-permute-start.19
  169.3 2.1 collective-permute-start.21
  169.5 15.6 %collective-permute-start.20 = (bf16[288,1024]{1,0:T(8,128)(2,1)S(1)}, bf16[288,1024]{1,0:T(8,128)(2,1)S(1)}, u32[]{:S(2)}, u32[]{:S(2)}) collective-permute-start(bf16[288,1024]{1,0:T(8,128)(2,1)S(1)} %add_convert_fusion.3), channel_id=1, source_target_pairs={{0,2},{1,3},{2,0},{3,1},{4,6},{5,7},{6,4},{7,5},{8,10},{9,11},{10,... | collective-permute-start | bytes 1769480 | tf_op jit(solution)/shard_map/ppermute | solution.py:72
  187.8 2.1 collective-permute-start.23
  187.9 15.7 %collective-permute-start.22 = (bf16[288,1024]{1,0:T(8,128)(2,1)S(1)}, bf16[288,1024]{1,0:T(8,128)(2,1)S(1)}, u32[]{:S(2)}, u32[]{:S(2)}) collective-permute-start(bf16[288,1024]{1,0:T(8,128)(2,1)S(1)} %get-tuple-element.75), channel_id=1, source_target_pairs={{0,2},{1,3},{2,0},{3,1},{4,6},{5,7},{6,4},{7,5},{8,10},{9,11},{10,... | collective-permute-start | bytes 1769480 | tf_op jit(solution)/shard_map/ppermute | solution.py:72
  203.6 2.0 collective-permute-start.24
  222.1 2.1 collective-permute-start.25
  228.6 3.1 collective-permute-start.27
  228.7 15.9 %collective-permute-start.26 = (bf16[288,1024]{1,0:T(8,128)(2,1)}, bf16[288,1024]{1,0:T(8,128)(2,1)}, u32[]{:S(2)}, u32[]{:S(2)}) collective-permute-start(bf16[288,1024]{1,0:T(8,128)(2,1)} %add_convert_fusion.1), channel_id=1, source_target_pairs={{0,2},{1,3},{2,0},{3,1},{4,6},{5,7},{6,4},{7,5},{8,10},{9,11},{10,... | collective-permute-start | bytes 1769480 | tf_op jit(solution)/shard_map/ppermute | solution.py:72
  253.8 29.9 %collective-permute-start.30 = (bf16[16,48,1024]{2,1,0:T(8,128)(2,1)}, bf16[16,48,1024]{2,1,0:T(8,128)(2,1)}, u32[]{:S(2)}, u32[]{:S(2)}) collective-permute-start(bf16[16,48,1024]{2,1,0:T(8,128)(2,1)} %fusion.13), channel_id=1, source_target_pairs={{0,1},{1,0},{2,3},{3,2},{4,5},{5,4},{6,7},{7,6},{8,9},{9,8},{10,11... | collective-permute-start | bytes 4718600 | tf_op jit(solution)/shard_map/ppermute | solution.py:68
  264.5 17.8 %collective-permute-start.28 = (bf16[2,288,256]{2,1,0:T(8,128)(2,1)}, bf16[2,288,256]{2,1,0:T(8,128)(2,1)}, u32[]{:S(2)}, u32[]{:S(2)}) collective-permute-start(bf16[2,288,256]{2,1,0:T(8,128)(2,1)} %get-tuple-element.122), channel_id=1, source_target_pairs={{0,2},{1,3},{2,0},{3,1},{4,6},{5,7},{6,4},{7,5},{8,10},{9,11},{10,... | collective-permute-start | bytes 884744 | tf_op jit(solution)/shard_map/ppermute | solution.py:72
  283.5 3.1 collective-permute-start.29
  286.0 19.8 %collective-permute-start.31 = (bf16[8,48,1024]{2,1,0:T(8,128)(2,1)S(1)}, bf16[8,48,1024]{2,1,0:T(8,128)(2,1)S(1)}, u32[]{:S(2)}, u32[]{:S(2)}) collective-permute-start(bf16[8,48,1024]{2,1,0:T(8,128)(2,1)S(1)} %dynamic-slice_bitcast_fusion), channel_id=1, source_target_pairs={{0,2},{1,3},{2,0},{3,1},{4,6},{5,7},{6,4},{7,5},{8,10},{9,11},{10,... | collective-permute-start | bytes 2359304 | tf_op jit(solution)/shard_map/ppermute | solution.py:72
  311.9 19.9 %collective-permute-start.32 = (bf16[288,1024]{1,0:T(8,128)(2,1)S(1)}, bf16[288,1024]{1,0:T(8,128)(2,1)S(1)}, u32[]{:S(2)}, u32[]{:S(2)}) collective-permute-start(bf16[288,1024]{1,0:T(8,128)(2,1)S(1)} %get-tuple-element.84), channel_id=1, source_target_pairs={{0,1},{1,0},{2,3},{3,2},{4,5},{5,4},{6,7},{7,6},{8,9},{9,8},{10,11... | collective-permute-start | bytes 1769480 | tf_op jit(solution)/shard_map/ppermute | solution.py:68
  312.4 10.3 %collective-permute-start.38 = (bf16[592,256]{1,0:T(8,128)(2,1)S(1)}, bf16[592,256]{1,0:T(8,128)(2,1)S(1)}, u32[]{:S(2)}, u32[]{:S(2)}) collective-permute-start(bf16[592,256]{1,0:T(8,128)(2,1)S(1)} %constant_dynamic-update-slice_fusion.68), channel_id=1, source_target_pairs={{0,4},{4,0},{8,12},{12,8},{16,20},{20,16},{24,28},{28,24},{1,5},{5... | collective-permute-start | bytes 909320 | tf_op jit(solution)/shard_map/ppermute | solution.py:80
  313.2 21.4 %collective-permute-start.37 = (bf16[592,256]{1,0:T(8,128)(2,1)S(1)}, bf16[592,256]{1,0:T(8,128)(2,1)S(1)}, u32[]{:S(2)}, u32[]{:S(2)}) collective-permute-start(bf16[592,256]{1,0:T(8,128)(2,1)S(1)} %constant_dynamic-update-slice_fusion.52), channel_id=1, source_target_pairs={{0,4},{4,0},{8,12},{12,8},{16,20},{20,16},{24,28},{28,24},{1,5},{5... | collective-permute-start | bytes 909320 | tf_op jit(solution)/shard_map/ppermute | solution.py:80
  314.9 29.2 %collective-permute-start.36 = (bf16[592,256]{1,0:T(8,128)(2,1)S(1)}, bf16[592,256]{1,0:T(8,128)(2,1)S(1)}, u32[]{:S(2)}, u32[]{:S(2)}) collective-permute-start(bf16[592,256]{1,0:T(8,128)(2,1)S(1)} %constant_dynamic-update-slice_fusion.36), channel_id=1, source_target_pairs={{0,4},{4,0},{8,12},{12,8},{16,20},{20,16},{24,28},{28,24},{1,5},{5... | collective-permute-start | bytes 909320 | tf_op jit(solution)/shard_map/ppermute | solution.py:80
  315.6 37.5 %collective-permute-start.35 = (bf16[592,256]{1,0:T(8,128)(2,1)S(1)}, bf16[592,256]{1,0:T(8,128)(2,1)S(1)}, u32[]{:S(2)}, u32[]{:S(2)}) collective-permute-start(bf16[592,256]{1,0:T(8,128)(2,1)S(1)} %constant_dynamic-update-slice_fusion.20), channel_id=1, source_target_pairs={{0,4},{4,0},{8,12},{12,8},{16,20},{20,16},{24,28},{28,24},{1,5},{5... | collective-permute-start | bytes 909320 | tf_op jit(solution)/shard_map/ppermute | solution.py:80
  322.8 13.5 %collective-permute-start.39 = (bf16[592,256]{1,0:T(8,128)(2,1)S(1)}, bf16[592,256]{1,0:T(8,128)(2,1)S(1)}, u32[]{:S(2)}, u32[]{:S(2)}) collective-permute-start(bf16[592,256]{1,0:T(8,128)(2,1)S(1)} %add_convert_fusion.5), channel_id=1, source_target_pairs={{0,8},{4,12},{8,16},{12,20},{16,24},{20,28},{24,0},{28,4},{1,9},{5... | collective-permute-start | bytes 909320 | tf_op jit(solution)/shard_map/ppermute | solution.py:86
  332.0 16.2 %collective-permute-start.33 = (bf16[288,1024]{1,0:T(8,128)(2,1)S(1)}, bf16[288,1024]{1,0:T(8,128)(2,1)S(1)}, u32[]{:S(2)}, u32[]{:S(2)}) collective-permute-start(bf16[288,1024]{1,0:T(8,128)(2,1)S(1)} %fusion.26), channel_id=1, source_target_pairs={{0,2},{1,3},{2,0},{3,1},{4,6},{5,7},{6,4},{7,5},{8,10},{9,11},{10,... | collective-permute-start | bytes 1769480 | tf_op jit(solution)/shard_map/ppermute | solution.py:72
  334.6 13.6 %collective-permute-start.34 = (bf16[288,1024]{1,0:T(8,128)(2,1)S(1)}, bf16[288,1024]{1,0:T(8,128)(2,1)S(1)}, u32[]{:S(2)}, u32[]{:S(2)}) collective-permute-start(bf16[288,1024]{1,0:T(8,128)(2,1)S(1)} %slice.373), channel_id=1, source_target_pairs={{0,1},{1,0},{2,3},{3,2},{4,5},{5,4},{6,7},{7,6},{8,9},{9,8},{10,11... | collective-permute-start | bytes 1769480 | tf_op jit(solution)/shard_map/ppermute | solution.py:68
  336.5 11.6 %collective-permute-start.40 = (bf16[592,256]{1,0:T(8,128)(2,1)S(1)}, bf16[592,256]{1,0:T(8,128)(2,1)S(1)}, u32[]{:S(2)}, u32[]{:S(2)}) collective-permute-start(bf16[592,256]{1,0:T(8,128)(2,1)S(1)} %add_convert_fusion.4), channel_id=1, source_target_pairs={{0,8},{4,12},{8,16},{12,20},{16,24},{20,28},{24,0},{28,4},{1,9},{5... | collective-permute-start | bytes 909320 | tf_op jit(solution)/shard_map/ppermute | solution.py:86
  349.4 10.7 %collective-permute-start.41 = (bf16[592,256]{1,0:T(8,128)(2,1)S(1)}, bf16[592,256]{1,0:T(8,128)(2,1)S(1)}, u32[]{:S(2)}, u32[]{:S(2)}) collective-permute-start(bf16[592,256]{1,0:T(8,128)(2,1)S(1)} %convert_add_fusion.4), channel_id=1, source_target_pairs={{0,8},{4,12},{8,16},{12,20},{16,24},{20,28},{24,0},{28,4},{1,9},{5... | collective-permute-start | bytes 909320 | tf_op jit(solution)/shard_map/ppermute | solution.py:86
  360.6 5.2 %collective-permute-start.42 = (bf16[2,48,768]{2,1,0:T(8,128)(2,1)S(1)}, bf16[2,48,768]{2,1,0:T(8,128)(2,1)S(1)}, u32[]{:S(2)}, u32[]{:S(2)}) collective-permute-start(bf16[2,48,768]{2,1,0:T(8,128)(2,1)S(1)} %get-tuple-element.139), channel_id=1, source_target_pairs={{0,2},{1,3},{2,0},{3,1},{4,6},{5,7},{6,4},{7,5},{8,10},{9,11},{10,... | collective-permute-start | bytes 442376 | tf_op jit(solution)/shard_map/ppermute | solution.py:72
  365.8 1.4 collective-permute-start.43
  381.8 5.4 %collective-permute-start.44 = (bf16[2,32,1024]{2,1,0:T(8,128)(2,1)S(1)}, bf16[2,32,1024]{2,1,0:T(8,128)(2,1)S(1)}, u32[]{:S(2)}, u32[]{:S(2)}) collective-permute-start(bf16[2,32,1024]{2,1,0:T(8,128)(2,1)S(1)} %get-tuple-element.143), channel_id=1, source_target_pairs={{0,2},{1,3},{2,0},{3,1},{4,6},{5,7},{6,4},{7,5},{8,10},{9,11},{10,... | collective-permute-start | bytes 393224 | tf_op jit(solution)/shard_map/ppermute | solution.py:72
  (62 other events, 329.7 us)
Sparse Core Ops, SparseCore 0:
  48.8 53.1 all-gather.2
  109.0 53.3 all-gather.4
  282.5 97.4 reduce-scatter.1

commit v4 on v3

--- a/solution.py
+++ b/solution.py
@@ -196,7 +196,7 @@
     return blocks, done
 
 
-def rows_sum(place, values, part):
+def rows_sum(place, values, part, beside=()):
     total, both = None, None
     for k in reversed(range(place.nx)):
         value = values[k]
@@ -208,7 +208,8 @@
         term = both
         if k:
             both = both.astype(BF16)
-            term = place.to_x(both, k).astype(F32)
+            term, _ = lax.optimization_barrier((place.to_x(both, k), beside))
+            term = term.astype(F32)
         total = term if total is None else total + term
     return total
 
@@ -484,11 +485,16 @@
     attention.start()
     for step in range(place.nz - 1):
         attention.settle()
-        if step == place.nz - 3:
+        if step == place.nz - 4:
             early = attention.here
-    up_block, down_late, _ = lax.optimization_barrier((up_block, down_weight, early))
-    full_up = lax.all_gather(up_block, "dp", axis=0, tiled=True)
-    full_down = lax.all_gather(down_late, "dp", axis=0, tiled=True)
+    up_block, down_block, _ = lax.optimization_barrier((up_block, down_weight, early))
+    if hidden_own == width:
+        later = lax.all_gather(jnp.concatenate([up_block, down_block], axis=0), "dp", axis=0)
+        full_up = later[:, : seq * shard].reshape(width, hidden_own)
+        full_down = later[:, seq * shard :].reshape(hidden_own, width)
+    else:
+        full_up = lax.all_gather(up_block, "dp", axis=0, tiled=True)
+        full_down = lax.all_gather(down_block, "dp", axis=0, tiled=True)
     attention.settle()
     full_qkv, packed_all = attention.finish(
         [(i // 2, *rest) for i, *rest in pieces if i != 1], ((seq * shard, qkv_cols), (EXTRA, head_cols))
@@ -554,16 +560,18 @@
             right_product(block, full_down) * hidden_slopes[k][1].astype(F32)
         ).astype(BF16),
     )
-    first_grad = second_grad + rows_sum(place, preact_all, lambda p: right_product(p, full_up))
     if hidden_own == width:
-        both_grads = weight_grads(hidden_all, second_all, first_all, preact_all)
-        both_owned = lax.psum_scatter(both_grads, "dp", scatter_dimension=0, tiled=True)
+        beside = weight_grads(hidden_all, second_all, first_all, preact_all)
+        both_owned = lax.psum_scatter(beside, "dp", scatter_dimension=0, tiled=True)
         down_owned, up_owned = both_owned[:, :width].astype(F32), both_owned[:, width:]
     else:
         down_grad = weight_grads(hidden_all, second_all)
         down_owned = lax.psum_scatter(down_grad, "dp", scatter_dimension=0, tiled=True).astype(F32)
-        up_grad = weight_grads(first_all, preact_all)
-        up_owned = lax.psum_scatter(up_grad, "dp", scatter_dimension=0, tiled=True)
+        beside = weight_grads(first_all, preact_all)
+        up_owned = lax.psum_scatter(beside, "dp", scatter_dimension=0, tiled=True)
+    first_grad = second_grad + rows_sum(
+        place, preact_all, lambda p: right_product(p, full_up), beside
+    )
     up_bias_grad = sum(jnp.sum(p, axis=0, dtype=F32) for p in preact_all)
 
     residual_grad, gain_one_grad, shift_one_grad = norm_backward(
@@ -589,7 +597,8 @@
     extra = jnp.concatenate([v.reshape(everyone, shard) for v in vector_sums] + [up_bias_wide], axis=1)
     wide_count = extra.shape[1]
     extra = jnp.pad(extra.astype(BF16)[:, None], ((0, 0), (0, EXTRA - 1), (0, width - wide_count)))
-    out_grad = weight_grads([mixed], [branch_low]).reshape(everyone, shard, width)
+    branch_late, _ = lax.optimization_barrier((branch_low, mixed_grad))
+    out_grad = weight_grads([mixed], [branch_late]).reshape(everyone, shard, width)
     view = jnp.concatenate([out_grad, extra], axis=1)
     view = view.reshape(dp * place.nx, CORES, shard + EXTRA, width)
     mine = lax.dynamic_index_in_dim(view, place.c, 1, keepdims=False)

time: 397 us -> 356 us (0.90); the launches traced: 397 us -> 351 us
  waiting for transfers between devices: 187 us -> 171 us
  starting transfers between devices: 47.3 us -> 31.6 us
  local copies, waits for them, and re-layouts: 48.5 us -> 37.9 us
  other arithmetic: 30.6 us -> 26.5 us
    all_gather x2 -> x1, waiting for transfers between devices: 23.8 us -> 0.95 us  [body(): lax.all_gather(jnp.concatenate([up_block, down_block], axis=0), 'dp', axi...]
    ppermute x6, starting transfers between devices: 18.5 us -> 4.25 us  [to_z(): lax.ppermute(a, 'dp', [(i, (i // m + k) % n * m + i % m) for i in range(s...]
    concatenate x2, local copies, waits for them, and re-layouts: 12.6 us -> 0.08 us  [rows_each(): blocks.append(jnp.concatenate([here, place.core(here)], axis=0))]
    ppermute x6, waiting for transfers between devices: 25.6 us -> 35.6 us  [to_z(): lax.ppermute(a, 'dp', [(i, (i // m + k) % n * m + i % m) for i in range(s...]
    reduce_scatter x1, waiting for transfers between devices: 12.6 us -> 3.77 us  [body(): both_owned = lax.psum_scatter(beside, 'dp', scatter_dimension=0, tiled=True)]
    ppermute x8, waiting for transfers between devices: 42.1 us -> 46.6 us  [to_y(): lax.ppermute(a, 'dp', [(i, i // n * n + (i % n + k) % n) for i in range(s...]
    unnamed x192 -> x175, local copies, waits for them, and re-layouts: 18.4 us -> 19.6 us
  transfers between devices with their start and end apart: 49 -> 48, of which waited for: 36 -> 36; matrix products, arithmetic and copies ran while one was open for 12% -> 12% of each run, Pallas kernels for 10% -> 12%
where the time goes in v4:
time: 356 us; the launch traced here: 351 us
  waiting for transfers between devices  171 us (48%)
  Pallas kernels  43 us (12%)
  local copies, waits for them, and re-layouts  37.9 us (11%)
  starting transfers between devices  31.6 us (9%)
  other arithmetic  26.5 us (7%)
  matrix products  24.8 us (7%)
  between operations  16.5 us (5%)
    ppermute x13, waiting for transfers between devices, to_x(): lax.ppermute(a, 'seq', [(i, (i // CORES + k) % n * CORES + i % CORES) for...  72.9 us
    ppermute x8, waiting for transfers between devices, to_y(): lax.ppermute(a, 'dp', [(i, i // n * n + (i % n + k) % n) for i in range(s...  46.6 us
    ppermute x6, waiting for transfers between devices, to_z(): lax.ppermute(a, 'dp', [(i, (i // m + k) % n * m + i % m) for i in range(s...  35.6 us
    unnamed x175, local copies, waits for them, and re-layouts  19.6 us
    ppermute x13, starting transfers between devices, to_x(): lax.ppermute(a, 'seq', [(i, (i // CORES + k) % n * CORES + i % CORES) for...  17.3 us
    pallas_call x1, Pallas kernels, attend_back(): pl.pallas_call(partial(attend_back_kernel, heads), grid_spec=pltpu.Prefet...  14.9 us
    pallas_call x3, Pallas kernels, weight_grads(): pl.pallas_call(partial(grads_kernel, count), grid=(inner // tile,), in_sp...  13.7 us
    dot_general x6, matrix products, right_product(): return lax.dot_general(left, right, DN_T, preferred_element_type=F32)  13.4 us
  transfers between devices with their start and end apart: 48, of which 36 were waited for; matrix products, arithmetic and copies ran while one was open for 12% of the time, Pallas kernels for 12%

profile of v4, /device:TPU:0, one launch (start us, length us, event | category | flops | bytes accessed | tf_op | source)
XLA Modules:
  0.0 351.4 jit_solution(6845372480892897883)
XLA Ops:
  10.2 3.0 collective-permute-start.3
  13.9 8.1 %collective-permute-done.3 = bf16[2,48,1792]{2,1,0:T(8,128)(2,1)S(1)} collective-permute-done((bf16[2,48,1792]{2,1,0:T(8,128)(2,1)S(1)}, bf16[2,48,1792]{2,1,0:T(8,128)(2,1)S(1)}, u32[]{:S(2)}, u32[]{:S(2)}) %collective-permute-start.3) | collective-permute-done | bytes 344096 | tf_op jit(solution)/shard_map/ppermute | solution.py:72
  24.2 1.8 collective-permute-start.6
  27.6 6.6 %collective-permute-done.6.refs_1_ = bf16[656,256]{1,0:T(8,128)(2,1)S(1)} collective-permute-done((bf16[656,256]{1,0:T(8,128)(2,1)S(1)}, bf16[656,256]{1,0:T(8,128)(2,1)S(1)}, u32[]{:S(2)}, u32[]{:S(2)}) %collective-permute-start.6) | collective-permute-done | bytes 335904 | tf_op jit(solution)/shard_map/ppermute | solution.py:80
  34.2 3.3 collective-permute-done.7.refs_2_
  41.1 11.8 %collective-permute-done.1 = bf16[288,1024]{1,0:T(8,128)(2,1)S(1)} collective-permute-done((bf16[288,1024]{1,0:T(8,128)(2,1)S(1)}, bf16[288,1024]{1,0:T(8,128)(2,1)S(1)}, u32[]{:S(2)}, u32[]{:S(2)}) %collective-permute-start.1) | collective-permute-done | bytes 589856 | tf_op jit(solution)/shard_map/ppermute | solution.py:72
  54.1 2.3 collective-permute-done.9.refs_4_
  60.1 4.1 %collective-permute-done.10.refs_5_ = bf16[656,256]{1,0:T(8,128)(2,1)S(1)} collective-permute-done((bf16[656,256]{1,0:T(8,128)(2,1)S(1)}, bf16[656,256]{1,0:T(8,128)(2,1)S(1)}, u32[]{:S(2)}, u32[]{:S(2)}) %collective-permute-start.10) | collective-permute-done | bytes 335904 | tf_op jit(solution)/shard_map/ppermute | solution.py:80
  64.2 12.8 %collective-permute-done.11.refs_6_ = bf16[656,256]{1,0:T(8,128)(2,1)S(1)} collective-permute-done((bf16[656,256]{1,0:T(8,128)(2,1)S(1)}, bf16[656,256]{1,0:T(8,128)(2,1)S(1)}, u32[]{:S(2)}, u32[]{:S(2)}) %collective-permute-start.11) | collective-permute-done | bytes 335904 | tf_op jit(solution)/shard_map/ppermute | solution.py:86
  78.9 9.2 %collective-permute-done.12.refs_7_ = bf16[656,256]{1,0:T(8,128)(2,1)S(1)} collective-permute-done((bf16[656,256]{1,0:T(8,128)(2,1)S(1)}, bf16[656,256]{1,0:T(8,128)(2,1)S(1)}, u32[]{:S(2)}, u32[]{:S(2)}) %collective-permute-start.12) | collective-permute-done | bytes 335904 | tf_op jit(solution)/shard_map/ppermute | solution.py:80
  89.9 2.0 fusion.qkv_ref
  92.0 13.1 %shard_map.272 = (bf16[1152,256]{1,0:T(8,128)(2,1)S(1)}, f32[4,1152]{1,0:T(4,128)S(1)}) custom-call(s32[6]{0:T(128)S(1)} %pad_add_fusion.bounds, bf16[1152,768]{1,0:T(8,128)(2,1)S(1)} %fusion.qkv_ref, s32[1,1152]{1,0:T(1,128)S(1)} %copy-done.10, s32[1152,1]{1,0:T(8,128)S(1)} %copy.103.seg_col), custom_call_target="tpu_custom_call" | custom-call | flops 1358954496 | bytes 2359296 | tf_op jit(solution)/shard_map/pallas_call | solution.py:325
  106.0 6.0 %collective-permute-done.13 = bf16[2,288,256]{2,1,0:T(8,128)(2,1)S(1)} collective-permute-done((bf16[2,288,256]{2,1,0:T(8,128)(2,1)S(1)}, bf16[2,288,256]{2,1,0:T(8,128)(2,1)S(1)}, u32[]{:S(2)}, u32[]{:S(2)}) %collective-permute-start.13) | collective-permute-done | bytes 294944 | tf_op jit(solution)/shard_map/ppermute | solution.py:72
  119.0 2.7 fusion.60
  121.7 3.7 %fusion.6 = (bf16[576,1024]{1,0:T(8,128)(2,1)S(1)}, bf16[576,1024]{1,0:T(8,128)(2,1)S(1)}) fusion(f32[1024]{0:T(1024)S(1)} %add.555, bf16[1024,1024]{1,0:T(8,128)(2,1)S(1)} %bitcast.270, bf16[288,1024]{1,0:T(8,128)(2,1)} %collective-permute-done.17, bf16[288,1024]{1,0:T(8,128)(2,1)S(1)} %fusion.27), kind=kOutput, calls=%fused_computation.16 | convolution fusion | flops 1217396736 | bytes 5640192 | tf_op jit(solution)/shard_map/dot_general | solution.py:24
  125.4 8.3 %collective-permute-done.16 = bf16[288,1024]{1,0:T(8,128)(2,1)} collective-permute-done((bf16[288,1024]{1,0:T(8,128)(2,1)S(1)}, bf16[288,1024]{1,0:T(8,128)(2,1)}, u32[]{:S(2)}, u32[]{:S(2)}) %collective-permute-start.16) | collective-permute-done | bytes 589856 | tf_op jit(solution)/shard_map/ppermute | solution.py:72
  136.0 2.0 multiply_convert_fusion.2
  139.6 1.9 collective-permute-done.19
  143.7 13.5 %collective-permute-done.20 = bf16[288,1024]{1,0:T(8,128)(2,1)S(1)} collective-permute-done((bf16[288,1024]{1,0:T(8,128)(2,1)S(1)}, bf16[288,1024]{1,0:T(8,128)(2,1)S(1)}, u32[]{:S(2)}, u32[]{:S(2)}) %collective-permute-start.20) | collective-permute-done | bytes 589856 | tf_op jit(solution)/shard_map/ppermute | solution.py:72
  162.4 2.5 convert_reduce_fusion.2
  164.9 11.2 %collective-permute-done.22 = bf16[288,1024]{1,0:T(8,128)(2,1)S(1)} collective-permute-done((bf16[288,1024]{1,0:T(8,128)(2,1)S(1)}, bf16[288,1024]{1,0:T(8,128)(2,1)S(1)}, u32[]{:S(2)}, u32[]{:S(2)}) %collective-permute-start.22) | collective-permute-done | bytes 589856 | tf_op jit(solution)/shard_map/ppermute | solution.py:72
  176.2 2.0 collective-permute-done.24
  178.2 2.4 convert_reduce_fusion.1
  185.3 2.3 add_convert_fusion.1
  187.9 3.4 convolution_convert_fusion.1
  203.3 8.2 %shard_map.274 = bf16[1024,2048]{1,0:T(8,128)(2,1)S(1)} custom-call(bf16[576,1024]{1,0:T(8,128)(2,1)S(1)} %copy-done.14, bf16[576,1024]{1,0:T(8,128)(2,1)S(1)} %copy-done.16, bf16[576,1024]{1,0:T(8,128)(2,1)S(1)} %copy-done.3, bf16[576,1024]{1,0:T(8,128)(2,1)S(1)} %copy-done.9, bf16[576,1024]{1,0:T(8,128)(2,1)S(1)} %pad_maximum_fusion.1.refs_4_, ...), custom_call_target="tpu_custom_call" | custom-call | flops 4831838208 | bytes 13631488 | tf_op jit(solution)/shard_map/pallas_call | solution.py:399
  211.5 2.0 copy-done
  213.5 4.3 %multiply_reduce_fusion = (bf16[1024]{0:T(1024)(128)(2,1)S(1)}, f32[288]{0:T(512)S(1)}, f32[288]{0:T(512)S(1)}, bf16[1024]{0:T(1024)(128)(2,1)S(1)}, f32[288,1024]{1,0:T(8,128)S(1)}, /*index=5*/bf16[1,288,1024]{2,1,0:T(8,128)(2,1)}) fusion(f32[288,1024]{1,0:T(8,128)} %copy-done.23, f32[288]{0:T(512)S(1)} %add_rsqrt_fusion.1, ...), kind=kLoop, calls=%fused_computation.63 | loop fusion | flops 7665088 | bytes 6513664 | tf_op jit(solution)/shard_map/reduce_sum | solution.py:50
  221.5 2.0 shard_map.276
  225.5 1.7 reshape.447
  228.1 1.7 collective-permute-start.28
  229.9 7.9 %collective-permute-done.28 = bf16[2,288,256]{2,1,0:T(8,128)(2,1)S(1)} collective-permute-done((bf16[2,288,256]{2,1,0:T(8,128)(2,1)}, bf16[2,288,256]{2,1,0:T(8,128)(2,1)S(1)}, u32[]{:S(2)}, u32[]{:S(2)}) %collective-permute-start.28) | collective-permute-done | bytes 294944 | tf_op jit(solution)/shard_map/ppermute | solution.py:72
  237.9 2.1 fusion.1
  240.0 1.8 collective-permute-start.31
  243.6 14.9 %shard_map.275.refs_1_ = bf16[1152,768]{1,0:T(8,128)(2,1)S(1)} custom-call(s32[6]{0:T(128)S(1)} %pad_add_fusion.bounds, bf16[1152,768]{1,0:T(8,128)(2,1)S(1)} %copy-done.21, bf16[1152,256]{1,0:T(8,128)(2,1)S(1)} %copy-done.5, bf16[1152,256]{1,0:T(8,128)(2,1)S(1)} %bitcast.247, f32[4,1152]{1,0:T(4,128)S(1)} %get-tuple-element.57.log_ref, ...), custom_call_target="tpu_custom_call" | custom-call | flops 3397386240 | bytes 4718592 | tf_op jit(solution)/shard_map/pallas_call | solution.py:352
  260.4 2.0 convolution_convert_fusion
  262.4 3.5 %shard_map.277 = bf16[1024,768]{1,0:T(8,128)(2,1)S(1)} custom-call(bf16[1152,1024]{1,0:T(8,128)(2,1)S(1)} %bitcast.245, bf16[1152,768]{1,0:T(8,128)(2,1)S(1)} %shard_map.275.refs_1_), custom_call_target="tpu_custom_call" | custom-call | flops 1811939328 | bytes 5701632 | tf_op jit(solution)/shard_map/pallas_call | solution.py:399
  272.0 10.0 %collective-permute-done.38 = bf16[592,256]{1,0:T(8,128)(2,1)S(1)} collective-permute-done((bf16[592,256]{1,0:T(8,128)(2,1)S(1)}, bf16[592,256]{1,0:T(8,128)(2,1)S(1)}, u32[]{:S(2)}, u32[]{:S(2)}) %collective-permute-start.38) | collective-permute-done | bytes 303136 | tf_op jit(solution)/shard_map/ppermute | solution.py:80
  285.1 6.8 %collective-permute-done.37 = bf16[592,256]{1,0:T(8,128)(2,1)S(1)} collective-permute-done((bf16[592,256]{1,0:T(8,128)(2,1)S(1)}, bf16[592,256]{1,0:T(8,128)(2,1)S(1)}, u32[]{:S(2)}, u32[]{:S(2)}) %collective-permute-start.37) | collective-permute-done | bytes 303136 | tf_op jit(solution)/shard_map/ppermute | solution.py:80
  292.9 7.7 %collective-permute-done.36 = bf16[592,256]{1,0:T(8,128)(2,1)S(1)} collective-permute-done((bf16[592,256]{1,0:T(8,128)(2,1)S(1)}, bf16[592,256]{1,0:T(8,128)(2,1)S(1)}, u32[]{:S(2)}, u32[]{:S(2)}) %collective-permute-start.36) | collective-permute-done | bytes 303136 | tf_op jit(solution)/shard_map/ppermute | solution.py:80
  300.6 2.9 collective-permute-done.40
  306.8 13.6 %collective-permute-done.41 = bf16[592,256]{1,0:T(8,128)(2,1)S(1)} collective-permute-done((bf16[592,256]{1,0:T(8,128)(2,1)S(1)}, bf16[592,256]{1,0:T(8,128)(2,1)S(1)}, u32[]{:S(2)}, u32[]{:S(2)}) %collective-permute-start.41) | collective-permute-done | bytes 303136 | tf_op jit(solution)/shard_map/ppermute | solution.py:86
  320.9 3.4 collective-permute-start.42
  325.6 1.8 collective-permute-done.42
  329.0 3.8 %reduce-scatter.2.cloned.1.call-done = bf16[128,2048]{1,0:T(8,128)(2,1)} async-done(((bf16[1024,2048]{1,0:T(8,128)(2,1)}), bf16[128,2048]{1,0:T(8,128)(2,1)}) %reduce-scatter.2.cloned.1.call-update) | async-done | bytes 524304 | tf_op jit(solution)/shard_map/reduce_scatter | solution.py:565
  332.7 1.9 slice_convert_fusion
  334.7 2.8 collective-permute-start.44
  339.0 2.3 collective-permute-done.44
  (405 shorter events, 85.7 us)
Async XLA Ops:
  7.2 111.8 %all-gather.3.cloned.1.call-start = ((), (), s32[]{:S(2)}) async-start(), calls=%async_computation.2 | async-start | bytes 4718592 | tf_op jit(solution)/shard_map/all_gather | solution.py:492
  10.2 11.8 %collective-permute-start.3 = (bf16[2,48,1792]{2,1,0:T(8,128)(2,1)S(1)}, bf16[2,48,1792]{2,1,0:T(8,128)(2,1)S(1)}, u32[]{:S(2)}, u32[]{:S(2)}) collective-permute-start(bf16[2,48,1792]{2,1,0:T(8,128)(2,1)S(1)} %get-tuple-element.124), channel_id=1, source_target_pairs={{0,2},{1,3},{2,0},{3,1},{4,6},{5,7},{6,4},{7,5},{8,10},{9,11},{10,... | collective-permute-start | bytes 1032200 | tf_op jit(solution)/shard_map/ppermute | solution.py:72
  13.2 9.5 %collective-permute-start.5 = (bf16[32,1024]{1,0:T(8,128)(2,1)S(1)}, bf16[32,1024]{1,0:T(8,128)(2,1)S(1)}, u32[]{:S(2)}, u32[]{:S(2)}) collective-permute-start(bf16[32,1024]{1,0:T(8,128)(2,1)S(1)} %copy-done.43), channel_id=1, source_target_pairs={{0,2},{1,3},{2,0},{3,1},{4,6},{5,7},{6,4},{7,5},{8,10},{9,11},{10,... | collective-permute-start | bytes 196616 | tf_op jit(solution)/shard_map/ppermute | solution.py:72
  22.0 1.7 collective-permute-start.4
  24.2 10.0 %collective-permute-start.6 = (bf16[656,256]{1,0:T(8,128)(2,1)S(1)}, bf16[656,256]{1,0:T(8,128)(2,1)S(1)}, u32[]{:S(2)}, u32[]{:S(2)}) collective-permute-start(bf16[656,256]{1,0:T(8,128)(2,1)S(1)} %constant_dynamic-update-slice_fusion.refs_0_), channel_id=1, source_target_pairs={{0,4},{4,0},{8,12},{12,8},{16,20},{20,16},{24,28},{28,24},{1,5},{5... | collective-permute-start | bytes 1007624 | tf_op jit(solution)/shard_map/ppermute | solution.py:80
  26.0 11.5 %collective-permute-start.7 = (bf16[656,256]{1,0:T(8,128)(2,1)S(1)}, bf16[656,256]{1,0:T(8,128)(2,1)S(1)}, u32[]{:S(2)}, u32[]{:S(2)}) collective-permute-start(bf16[656,256]{1,0:T(8,128)(2,1)S(1)} %constant_dynamic-update-slice_fusion.refs_0_), channel_id=1, source_target_pairs={{0,8},{4,12},{8,16},{12,20},{16,24},{20,28},{24,0},{28,4},{1,9},{5... | collective-permute-start | bytes 1007624 | tf_op jit(solution)/shard_map/ppermute | solution.py:86
  38.4 294.3 %reduce-scatter.2.cloned.1.call-start = ((), (), s32[]{:S(2)}) async-start(), calls=%async_computation.1 | async-start | bytes 4718592 | tf_op jit(solution)/shard_map/reduce_scatter | solution.py:565
  38.5 14.4 %collective-permute-start.1 = (bf16[288,1024]{1,0:T(8,128)(2,1)S(1)}, bf16[288,1024]{1,0:T(8,128)(2,1)S(1)}, u32[]{:S(2)}, u32[]{:S(2)}) collective-permute-start(bf16[288,1024]{1,0:T(8,128)(2,1)S(1)} %bitcast.296), channel_id=1, source_target_pairs={{0,2},{1,3},{2,0},{3,1},{4,6},{5,7},{6,4},{7,5},{8,10},{9,11},{10,... | collective-permute-start | bytes 1769480 | tf_op jit(solution)/shard_map/ppermute | solution.py:72
  40.0 18.5 %collective-permute-start = (bf16[288,1024]{1,0:T(8,128)(2,1)S(1)}, bf16[288,1024]{1,0:T(8,128)(2,1)}, u32[]{:S(2)}, u32[]{:S(2)}) collective-permute-start(bf16[288,1024]{1,0:T(8,128)(2,1)S(1)} %bitcast.297), channel_id=1, source_target_pairs={{0,1},{1,0},{2,3},{3,2},{4,5},{5,4},{6,7},{7,6},{8,9},{9,8},{10,11... | collective-permute-start | bytes 1769480 | tf_op jit(solution)/shard_map/ppermute | solution.py:68
  40.5 13.6 %collective-permute-start.8 = (bf16[656,256]{1,0:T(8,128)(2,1)S(1)}, bf16[656,256]{1,0:T(8,128)(2,1)S(1)}, u32[]{:S(2)}, u32[]{:S(2)}) collective-permute-start(bf16[656,256]{1,0:T(8,128)(2,1)S(1)} %collective-permute-done.7.refs_2_), channel_id=1, source_target_pairs={{0,4},{4,0},{8,12},{12,8},{16,20},{20,16},{24,28},{28,24},{1,5},{5... | collective-permute-start | bytes 1007624 | tf_op jit(solution)/shard_map/ppermute | solution.py:80
  41.0 15.4 %collective-permute-start.9 = (bf16[656,256]{1,0:T(8,128)(2,1)S(1)}, bf16[656,256]{1,0:T(8,128)(2,1)S(1)}, u32[]{:S(2)}, u32[]{:S(2)}) collective-permute-start(bf16[656,256]{1,0:T(8,128)(2,1)S(1)} %collective-permute-done.7.refs_2_), channel_id=1, source_target_pairs={{0,8},{4,12},{8,16},{12,20},{16,24},{20,28},{24,0},{28,4},{1,9},{5... | collective-permute-start | bytes 1007624 | tf_op jit(solution)/shard_map/ppermute | solution.py:86
  52.8 24.8 %collective-permute-start.2 = (bf16[288,1024]{1,0:T(8,128)(2,1)S(1)}, bf16[288,1024]{1,0:T(8,128)(2,1)}, u32[]{:S(2)}, u32[]{:S(2)}) collective-permute-start(bf16[288,1024]{1,0:T(8,128)(2,1)S(1)} %collective-permute-done.1), channel_id=1, source_target_pairs={{0,1},{1,0},{2,3},{3,2},{4,5},{5,4},{6,7},{7,6},{8,9},{9,8},{10,11... | collective-permute-start | bytes 1769480 | tf_op jit(solution)/shard_map/ppermute | solution.py:68
  56.4 7.8 %collective-permute-start.10 = (bf16[656,256]{1,0:T(8,128)(2,1)S(1)}, bf16[656,256]{1,0:T(8,128)(2,1)S(1)}, u32[]{:S(2)}, u32[]{:S(2)}) collective-permute-start(bf16[656,256]{1,0:T(8,128)(2,1)S(1)} %collective-permute-done.9.refs_4_), channel_id=1, source_target_pairs={{0,4},{4,0},{8,12},{12,8},{16,20},{20,16},{24,28},{28,24},{1,5},{5... | collective-permute-start | bytes 1007624 | tf_op jit(solution)/shard_map/ppermute | solution.py:80
  58.0 19.0 %collective-permute-start.11 = (bf16[656,256]{1,0:T(8,128)(2,1)S(1)}, bf16[656,256]{1,0:T(8,128)(2,1)S(1)}, u32[]{:S(2)}, u32[]{:S(2)}) collective-permute-start(bf16[656,256]{1,0:T(8,128)(2,1)S(1)} %collective-permute-done.9.refs_4_), channel_id=1, source_target_pairs={{0,8},{4,12},{8,16},{12,20},{16,24},{20,28},{24,0},{28,4},{1,9},{5... | collective-permute-start | bytes 1007624 | tf_op jit(solution)/shard_map/ppermute | solution.py:86
  77.0 11.1 %collective-permute-start.12 = (bf16[656,256]{1,0:T(8,128)(2,1)S(1)}, bf16[656,256]{1,0:T(8,128)(2,1)S(1)}, u32[]{:S(2)}, u32[]{:S(2)}) collective-permute-start(bf16[656,256]{1,0:T(8,128)(2,1)S(1)} %collective-permute-done.11.refs_6_), channel_id=1, source_target_pairs={{0,4},{4,0},{8,12},{12,8},{16,20},{20,16},{24,28},{28,24},{1,5},{5... | collective-permute-start | bytes 1007624 | tf_op jit(solution)/shard_map/ppermute | solution.py:80
  105.2 6.8 %collective-permute-start.13 = (bf16[2,288,256]{2,1,0:T(8,128)(2,1)S(1)}, bf16[2,288,256]{2,1,0:T(8,128)(2,1)S(1)}, u32[]{:S(2)}, u32[]{:S(2)}) collective-permute-start(bf16[2,288,256]{2,1,0:T(8,128)(2,1)S(1)} %get-tuple-element.132), channel_id=1, source_target_pairs={{0,2},{1,3},{2,0},{3,1},{4,6},{5,7},{6,4},{7,5},{8,10},{9,11},{10,... | collective-permute-start | bytes 884744 | tf_op jit(solution)/shard_map/ppermute | solution.py:72
  105.9 8.5 %collective-permute-start.15 = (bf16[16,1,32,1024]{3,2,1,0:T(8,128)(2,1)S(1)}, bf16[16,1,32,1024]{3,2,1,0:T(8,128)(2,1)S(1)}, u32[]{:S(2)}, u32[]{:S(2)}) collective-permute-start(bf16[16,1,32,1024]{3,2,1,0:T(8,128)(2,1)S(1)} %bitcast.240), channel_id=1, source_target_pairs={{0,1},{1,0},{2,3},{3,2},{4,5},{5,4},{6,7},{7,6},{8,9},{9,8},{10,11... | collective-permute-start | bytes 3145736 | tf_op jit(solution)/shard_map/ppermute | solution.py:68
  112.0 1.6 collective-permute-start.14
  117.6 4.1 %collective-permute-start.17 = (bf16[288,1024]{1,0:T(8,128)(2,1)S(1)}, bf16[288,1024]{1,0:T(8,128)(2,1)}, u32[]{:S(2)}, u32[]{:S(2)}) collective-permute-start(bf16[288,1024]{1,0:T(8,128)(2,1)S(1)} %fusion.27), channel_id=1, source_target_pairs={{0,1},{1,0},{2,3},{3,2},{4,5},{5,4},{6,7},{7,6},{8,9},{9,8},{10,11... | collective-permute-start | bytes 1769480 | tf_op jit(solution)/shard_map/ppermute | solution.py:68
  118.0 15.7 %collective-permute-start.16 = (bf16[288,1024]{1,0:T(8,128)(2,1)S(1)}, bf16[288,1024]{1,0:T(8,128)(2,1)}, u32[]{:S(2)}, u32[]{:S(2)}) collective-permute-start(bf16[288,1024]{1,0:T(8,128)(2,1)S(1)} %fusion.27), channel_id=1, source_target_pairs={{0,2},{1,3},{2,0},{3,1},{4,6},{5,7},{6,4},{7,5},{8,10},{9,11},{10,... | collective-permute-start | bytes 1769480 | tf_op jit(solution)/shard_map/ppermute | solution.py:72
  133.7 2.2 collective-permute-start.18
  139.4 2.1 collective-permute-start.19
  141.7 15.4 %collective-permute-start.20 = (bf16[288,1024]{1,0:T(8,128)(2,1)S(1)}, bf16[288,1024]{1,0:T(8,128)(2,1)S(1)}, u32[]{:S(2)}, u32[]{:S(2)}) collective-permute-start(bf16[288,1024]{1,0:T(8,128)(2,1)S(1)} %add_convert_fusion.3), channel_id=1, source_target_pairs={{0,2},{1,3},{2,0},{3,1},{4,6},{5,7},{6,4},{7,5},{8,10},{9,11},{10,... | collective-permute-start | bytes 1769480 | tf_op jit(solution)/shard_map/ppermute | solution.py:72
  143.6 13.6 %collective-permute-start.21 = (bf16[288,1024]{1,0:T(8,128)(2,1)S(1)}, bf16[288,1024]{1,0:T(8,128)(2,1)S(1)}, u32[]{:S(2)}, u32[]{:S(2)}) collective-permute-start(bf16[288,1024]{1,0:T(8,128)(2,1)S(1)} %slice.483), channel_id=1, source_target_pairs={{0,1},{1,0},{2,3},{3,2},{4,5},{5,4},{6,7},{7,6},{8,9},{9,8},{10,11... | collective-permute-start | bytes 1769480 | tf_op jit(solution)/shard_map/ppermute | solution.py:68
  160.3 2.1 collective-permute-start.23
  160.4 15.7 %collective-permute-start.22 = (bf16[288,1024]{1,0:T(8,128)(2,1)S(1)}, bf16[288,1024]{1,0:T(8,128)(2,1)S(1)}, u32[]{:S(2)}, u32[]{:S(2)}) collective-permute-start(bf16[288,1024]{1,0:T(8,128)(2,1)S(1)} %get-tuple-element.79), channel_id=1, source_target_pairs={{0,2},{1,3},{2,0},{3,1},{4,6},{5,7},{6,4},{7,5},{8,10},{9,11},{10,... | collective-permute-start | bytes 1769480 | tf_op jit(solution)/shard_map/ppermute | solution.py:72
  176.2 2.0 collective-permute-start.24
  183.0 2.3 collective-permute-start.25
  187.6 25.8 %collective-permute-start.26 = (bf16[288,1024]{1,0:T(8,128)(2,1)}, bf16[288,1024]{1,0:T(8,128)(2,1)}, u32[]{:S(2)}, u32[]{:S(2)}) collective-permute-start(bf16[288,1024]{1,0:T(8,128)(2,1)} %add_convert_fusion.1), channel_id=1, source_target_pairs={{0,2},{1,3},{2,0},{3,1},{4,6},{5,7},{6,4},{7,5},{8,10},{9,11},{10,... | collective-permute-start | bytes 1769480 | tf_op jit(solution)/shard_map/ppermute | solution.py:72
  192.2 21.3 %collective-permute-start.27 = (bf16[288,1024]{1,0:T(8,128)(2,1)}, bf16[288,1024]{1,0:T(8,128)(2,1)}, u32[]{:S(2)}, u32[]{:S(2)}) collective-permute-start(bf16[288,1024]{1,0:T(8,128)(2,1)} %slice.490), channel_id=1, source_target_pairs={{0,1},{1,0},{2,3},{3,2},{4,5},{5,4},{6,7},{7,6},{8,9},{9,8},{10,11... | collective-permute-start | bytes 1769480 | tf_op jit(solution)/shard_map/ppermute | solution.py:68
  225.5 12.3 %collective-permute-start.30 = (bf16[16,48,1024]{2,1,0:T(8,128)(2,1)}, bf16[16,48,1024]{2,1,0:T(8,128)(2,1)}, u32[]{:S(2)}, u32[]{:S(2)}) collective-permute-start(bf16[16,48,1024]{2,1,0:T(8,128)(2,1)} %fusion.13), channel_id=1, source_target_pairs={{0,1},{1,0},{2,3},{3,2},{4,5},{5,4},{6,7},{7,6},{8,9},{9,8},{10,11... | collective-permute-start | bytes 4718600 | tf_op jit(solution)/shard_map/ppermute | solution.py:68
  228.1 9.6 %collective-permute-start.28 = (bf16[2,288,256]{2,1,0:T(8,128)(2,1)}, bf16[2,288,256]{2,1,0:T(8,128)(2,1)S(1)}, u32[]{:S(2)}, u32[]{:S(2)}) collective-permute-start(bf16[2,288,256]{2,1,0:T(8,128)(2,1)} %get-tuple-element.128), channel_id=1, source_target_pairs={{0,2},{1,3},{2,0},{3,1},{4,6},{5,7},{6,4},{7,5},{8,10},{9,11},{10,... | collective-permute-start | bytes 884744 | tf_op jit(solution)/shard_map/ppermute | solution.py:72
  237.8 4.1 %collective-permute-start.29 = (bf16[2,1,288,256]{3,2,1,0:T(8,128)(2,1)S(1)}, bf16[2,1,288,256]{3,2,1,0:T(8,128)(2,1)S(1)}, u32[]{:S(2)}, u32[]{:S(2)}) collective-permute-start(bf16[2,1,288,256]{3,2,1,0:T(8,128)(2,1)S(1)} %fusion.36), channel_id=1, source_target_pairs={{0,1},{1,0},{2,3},{3,2},{4,5},{5,4},{6,7},{7,6},{8,9},{9,8},{10,11... | collective-permute-start | bytes 884744 | tf_op jit(solution)/shard_map/ppermute | solution.py:68
  240.0 20.0 %collective-permute-start.31 = (bf16[8,48,1024]{2,1,0:T(8,128)(2,1)S(1)}, bf16[8,48,1024]{2,1,0:T(8,128)(2,1)S(1)}, u32[]{:S(2)}, u32[]{:S(2)}) collective-permute-start(bf16[8,48,1024]{2,1,0:T(8,128)(2,1)S(1)} %dynamic-slice_bitcast_fusion), channel_id=1, source_target_pairs={{0,2},{1,3},{2,0},{3,1},{4,6},{5,7},{6,4},{7,5},{8,10},{9,11},{10,... | collective-permute-start | bytes 2359304 | tf_op jit(solution)/shard_map/ppermute | solution.py:72
  266.5 17.2 %collective-permute-start.32 = (bf16[288,1024]{1,0:T(8,128)(2,1)S(1)}, bf16[288,1024]{1,0:T(8,128)(2,1)S(1)}, u32[]{:S(2)}, u32[]{:S(2)}) collective-permute-start(bf16[288,1024]{1,0:T(8,128)(2,1)S(1)} %get-tuple-element.90), channel_id=1, source_target_pairs={{0,1},{1,0},{2,3},{3,2},{4,5},{5,4},{6,7},{7,6},{8,9},{9,8},{10,11... | collective-permute-start | bytes 1769480 | tf_op jit(solution)/shard_map/ppermute | solution.py:68
  267.0 15.0 %collective-permute-start.38 = (bf16[592,256]{1,0:T(8,128)(2,1)S(1)}, bf16[592,256]{1,0:T(8,128)(2,1)S(1)}, u32[]{:S(2)}, u32[]{:S(2)}) collective-permute-start(bf16[592,256]{1,0:T(8,128)(2,1)S(1)} %constant_dynamic-update-slice_fusion.68), channel_id=1, source_target_pairs={{0,4},{4,0},{8,12},{12,8},{16,20},{20,16},{24,28},{28,24},{1,5},{5... | collective-permute-start | bytes 909320 | tf_op jit(solution)/shard_map/ppermute | solution.py:80
  268.5 23.4 %collective-permute-start.37 = (bf16[592,256]{1,0:T(8,128)(2,1)S(1)}, bf16[592,256]{1,0:T(8,128)(2,1)S(1)}, u32[]{:S(2)}, u32[]{:S(2)}) collective-permute-start(bf16[592,256]{1,0:T(8,128)(2,1)S(1)} %constant_dynamic-update-slice_fusion.52), channel_id=1, source_target_pairs={{0,4},{4,0},{8,12},{12,8},{16,20},{20,16},{24,28},{28,24},{1,5},{5... | collective-permute-start | bytes 909320 | tf_op jit(solution)/shard_map/ppermute | solution.py:80
  269.4 31.1 %collective-permute-start.36 = (bf16[592,256]{1,0:T(8,128)(2,1)S(1)}, bf16[592,256]{1,0:T(8,128)(2,1)S(1)}, u32[]{:S(2)}, u32[]{:S(2)}) collective-permute-start(bf16[592,256]{1,0:T(8,128)(2,1)S(1)} %constant_dynamic-update-slice_fusion.36), channel_id=1, source_target_pairs={{0,4},{4,0},{8,12},{12,8},{16,20},{20,16},{24,28},{28,24},{1,5},{5... | collective-permute-start | bytes 909320 | tf_op jit(solution)/shard_map/ppermute | solution.py:80
  270.9 35.9 %collective-permute-start.35 = (bf16[592,256]{1,0:T(8,128)(2,1)S(1)}, bf16[592,256]{1,0:T(8,128)(2,1)S(1)}, u32[]{:S(2)}, u32[]{:S(2)}) collective-permute-start(bf16[592,256]{1,0:T(8,128)(2,1)S(1)} %constant_dynamic-update-slice_fusion.20), channel_id=1, source_target_pairs={{0,4},{4,0},{8,12},{12,8},{16,20},{20,16},{24,28},{28,24},{1,5},{5... | collective-permute-start | bytes 909320 | tf_op jit(solution)/shard_map/ppermute | solution.py:80
  282.1 10.5 %collective-permute-start.39 = (bf16[592,256]{1,0:T(8,128)(2,1)S(1)}, bf16[592,256]{1,0:T(8,128)(2,1)S(1)}, u32[]{:S(2)}, u32[]{:S(2)}) collective-permute-start(bf16[592,256]{1,0:T(8,128)(2,1)S(1)} %add_convert_fusion.5), channel_id=1, source_target_pairs={{0,8},{4,12},{8,16},{12,20},{16,24},{20,28},{24,0},{28,4},{1,9},{5... | collective-permute-start | bytes 909320 | tf_op jit(solution)/shard_map/ppermute | solution.py:86
  283.9 19.8 %collective-permute-start.33 = (bf16[288,1024]{1,0:T(8,128)(2,1)S(1)}, bf16[288,1024]{1,0:T(8,128)(2,1)S(1)}, u32[]{:S(2)}, u32[]{:S(2)}) collective-permute-start(bf16[288,1024]{1,0:T(8,128)(2,1)S(1)} %fusion.26), channel_id=1, source_target_pairs={{0,2},{1,3},{2,0},{3,1},{4,6},{5,7},{6,4},{7,5},{8,10},{9,11},{10,... | collective-permute-start | bytes 1769480 | tf_op jit(solution)/shard_map/ppermute | solution.py:72
  291.9 11.7 %collective-permute-start.34 = (bf16[288,1024]{1,0:T(8,128)(2,1)S(1)}, bf16[288,1024]{1,0:T(8,128)(2,1)S(1)}, u32[]{:S(2)}, u32[]{:S(2)}) collective-permute-start(bf16[288,1024]{1,0:T(8,128)(2,1)S(1)} %slice.381), channel_id=1, source_target_pairs={{0,1},{1,0},{2,3},{3,2},{4,5},{5,4},{6,7},{7,6},{8,9},{9,8},{10,11... | collective-permute-start | bytes 1769480 | tf_op jit(solution)/shard_map/ppermute | solution.py:68
  292.7 10.8 %collective-permute-start.40 = (bf16[592,256]{1,0:T(8,128)(2,1)S(1)}, bf16[592,256]{1,0:T(8,128)(2,1)S(1)}, u32[]{:S(2)}, u32[]{:S(2)}) collective-permute-start(bf16[592,256]{1,0:T(8,128)(2,1)S(1)} %add_convert_fusion.4), channel_id=1, source_target_pairs={{0,8},{4,12},{8,16},{12,20},{16,24},{20,28},{24,0},{28,4},{1,9},{5... | collective-permute-start | bytes 909320 | tf_op jit(solution)/shard_map/ppermute | solution.py:86
  304.9 15.5 %collective-permute-start.41 = (bf16[592,256]{1,0:T(8,128)(2,1)S(1)}, bf16[592,256]{1,0:T(8,128)(2,1)S(1)}, u32[]{:S(2)}, u32[]{:S(2)}) collective-permute-start(bf16[592,256]{1,0:T(8,128)(2,1)S(1)} %convert_add_fusion.4), channel_id=1, source_target_pairs={{0,8},{4,12},{8,16},{12,20},{16,24},{20,28},{24,0},{28,4},{1,9},{5... | collective-permute-start | bytes 909320 | tf_op jit(solution)/shard_map/ppermute | solution.py:86
  320.9 6.5 %collective-permute-start.42 = (bf16[2,48,768]{2,1,0:T(8,128)(2,1)S(1)}, bf16[2,48,768]{2,1,0:T(8,128)(2,1)S(1)}, u32[]{:S(2)}, u32[]{:S(2)}) collective-permute-start(bf16[2,48,768]{2,1,0:T(8,128)(2,1)S(1)} %get-tuple-element.145), channel_id=1, source_target_pairs={{0,2},{1,3},{2,0},{3,1},{4,6},{5,7},{6,4},{7,5},{8,10},{9,11},{10,... | collective-permute-start | bytes 442376 | tf_op jit(solution)/shard_map/ppermute | solution.py:72
  327.4 1.4 collective-permute-start.43
  334.7 6.6 %collective-permute-start.44 = (bf16[2,32,1024]{2,1,0:T(8,128)(2,1)S(1)}, bf16[2,32,1024]{2,1,0:T(8,128)(2,1)S(1)}, u32[]{:S(2)}, u32[]{:S(2)}) collective-permute-start(bf16[2,32,1024]{2,1,0:T(8,128)(2,1)S(1)} %get-tuple-element.149), channel_id=1, source_target_pairs={{0,2},{1,3},{2,0},{3,1},{4,6},{5,7},{6,4},{7,5},{8,10},{9,11},{10,... | collective-permute-start | bytes 393224 | tf_op jit(solution)/shard_map/ppermute | solution.py:72
  341.3 1.4 collective-permute-start.45
  (52 other events, 247.3 us)
Sparse Core Ops, SparseCore 0:
  38.5 80.3 all-gather.2
  230.0 102.6 reduce-scatter.1

commit v5 on v4

--- a/solution.py
+++ b/solution.py
@@ -487,6 +487,8 @@
         attention.settle()
         if step == place.nz - 4:
             early = attention.here
+        if step == place.nz - 3:
+            middle = attention.here
     up_block, down_block, _ = lax.optimization_barrier((up_block, down_weight, early))
     if hidden_own == width:
         later = lax.all_gather(jnp.concatenate([up_block, down_block], axis=0), "dp", axis=0)
@@ -511,7 +513,7 @@
     bias_up = packed_all[:, len(smalls) :].reshape(dp, up_rows, seq, shard)
     bias_up = lax.dynamic_index_in_dim(bias_up, place.s, 2, keepdims=False).reshape(1, hidden_own)
 
-    row_blocks, _ = rows_each(place, rows, lambda k, block: ())
+    row_blocks, _ = rows_each(place, rows, lambda k, block: middle)
     all_rows = jnp.zeros((place.nx, CORES * count, width), BF16)
     for k, both in enumerate(row_blocks):
         mine, other = both[:count], both[count:]

time: 356 us -> 360 us (1.011)
    ppermute x8, waiting for transfers between devices: 46.6 us -> 63 us  [to_y(): lax.ppermute(a, 'dp', [(i, i // n * n + (i % n + k) % n) for i in range(s...]
    ppermute x13, waiting for transfers between devices: 72.9 us -> 61.9 us  [to_x(): lax.ppermute(a, 'seq', [(i, (i // CORES + k) % n * CORES + i % CORES) for...]
  transfers between devices with their start and end apart: 48 -> 48, of which waited for: 36 -> 34; matrix products, arithmetic and copies ran while one was open for 12% -> 12% of each run, Pallas kernels for 12% -> 12%
where the time goes in v5:
time: 360 us; the launch traced here: 356 us
  waiting for transfers between devices  174 us (48%)
  Pallas kernels  43 us (12%)
  local copies, waits for them, and re-layouts  38 us (11%)
  starting transfers between devices  33.3 us (9%)
  other arithmetic  26.5 us (7%)
  matrix products  24.8 us (7%)
  between operations  16.4 us (5%)
    ppermute x8, waiting for transfers between devices, to_y(): lax.ppermute(a, 'dp', [(i, i // n * n + (i % n + k) % n) for i in range(s...  63 us
    ppermute x13, waiting for transfers between devices, to_x(): lax.ppermute(a, 'seq', [(i, (i // CORES + k) % n * CORES + i % CORES) for...  61.9 us
    ppermute x6, waiting for transfers between devices, to_z(): lax.ppermute(a, 'dp', [(i, (i // m + k) % n * m + i % m) for i in range(s...  34.6 us
    unnamed x175, local copies, waits for them, and re-layouts  19.6 us
    ppermute x13, starting transfers between devices, to_x(): lax.ppermute(a, 'seq', [(i, (i // CORES + k) % n * CORES + i % CORES) for...  16.8 us
    pallas_call x1, Pallas kernels, attend_back(): pl.pallas_call(partial(attend_back_kernel, heads), grid_spec=pltpu.Prefet...  14.9 us
    pallas_call x3, Pallas kernels, weight_grads(): pl.pallas_call(partial(grads_kernel, count), grid=(inner // tile,), in_sp...  13.7 us
    dot_general x6, matrix products, right_product(): return lax.dot_general(left, right, DN_T, preferred_element_type=F32)  13.4 us
  transfers between devices with their start and end apart: 48, of which 34 were waited for; matrix products, arithmetic and copies ran while one was open for 12% of the time, Pallas kernels for 12%

profile of v5, /device:TPU:0, one launch (start us, length us, event | category | flops | bytes accessed | tf_op | source)
XLA Modules:
  0.0 356.2 jit_solution(596964926092209962)
XLA Ops:
  10.2 3.0 collective-permute-start.2
  13.9 8.1 %collective-permute-done.2 = bf16[2,48,1792]{2,1,0:T(8,128)(2,1)S(1)} collective-permute-done((bf16[2,48,1792]{2,1,0:T(8,128)(2,1)S(1)}, bf16[2,48,1792]{2,1,0:T(8,128)(2,1)S(1)}, u32[]{:S(2)}, u32[]{:S(2)}) %collective-permute-start.2) | collective-permute-done | bytes 344096 | tf_op jit(solution)/shard_map/ppermute | solution.py:72
  24.2 1.8 collective-permute-start.5
  27.6 6.6 %collective-permute-done.5.refs_1_ = bf16[656,256]{1,0:T(8,128)(2,1)S(1)} collective-permute-done((bf16[656,256]{1,0:T(8,128)(2,1)S(1)}, bf16[656,256]{1,0:T(8,128)(2,1)S(1)}, u32[]{:S(2)}, u32[]{:S(2)}) %collective-permute-start.5) | collective-permute-done | bytes 335904 | tf_op jit(solution)/shard_map/ppermute | solution.py:80
  34.2 3.3 collective-permute-done.6.refs_2_
  41.0 12.5 %collective-permute-done.7.refs_3_ = bf16[656,256]{1,0:T(8,128)(2,1)S(1)} collective-permute-done((bf16[656,256]{1,0:T(8,128)(2,1)S(1)}, bf16[656,256]{1,0:T(8,128)(2,1)S(1)}, u32[]{:S(2)}, u32[]{:S(2)}) %collective-permute-start.7) | collective-permute-done | bytes 335904 | tf_op jit(solution)/shard_map/ppermute | solution.py:80
  53.5 2.3 collective-permute-done.8.refs_4_
  60.0 6.6 %collective-permute-done.10.refs_5_ = bf16[656,256]{1,0:T(8,128)(2,1)S(1)} collective-permute-done((bf16[656,256]{1,0:T(8,128)(2,1)S(1)}, bf16[656,256]{1,0:T(8,128)(2,1)S(1)}, u32[]{:S(2)}, u32[]{:S(2)}) %collective-permute-start.10) | collective-permute-done | bytes 335904 | tf_op jit(solution)/shard_map/ppermute | solution.py:80
  66.6 10.1 %collective-permute-done.11.refs_6_ = bf16[656,256]{1,0:T(8,128)(2,1)S(1)} collective-permute-done((bf16[656,256]{1,0:T(8,128)(2,1)S(1)}, bf16[656,256]{1,0:T(8,128)(2,1)S(1)}, u32[]{:S(2)}, u32[]{:S(2)}) %collective-permute-start.11) | collective-permute-done | bytes 335904 | tf_op jit(solution)/shard_map/ppermute | solution.py:86
  79.5 12.4 %collective-permute-done.12.refs_7_ = bf16[656,256]{1,0:T(8,128)(2,1)S(1)} collective-permute-done((bf16[656,256]{1,0:T(8,128)(2,1)S(1)}, bf16[656,256]{1,0:T(8,128)(2,1)S(1)}, u32[]{:S(2)}, u32[]{:S(2)}) %collective-permute-start.12) | collective-permute-done | bytes 335904 | tf_op jit(solution)/shard_map/ppermute | solution.py:80
  93.8 2.0 fusion.qkv_ref
  95.8 13.1 %shard_map.272 = (bf16[1152,256]{1,0:T(8,128)(2,1)S(1)}, f32[4,1152]{1,0:T(4,128)S(1)}) custom-call(s32[6]{0:T(128)S(1)} %pad_add_fusion.bounds, bf16[1152,768]{1,0:T(8,128)(2,1)S(1)} %fusion.qkv_ref, s32[1,1152]{1,0:T(1,128)S(1)} %copy-done.10, s32[1152,1]{1,0:T(8,128)S(1)} %copy.103.seg_col), custom_call_target="tpu_custom_call" | custom-call | flops 1358954496 | bytes 2359296 | tf_op jit(solution)/shard_map/pallas_call | solution.py:325
  109.8 6.0 %collective-permute-done.13 = bf16[2,288,256]{2,1,0:T(8,128)(2,1)S(1)} collective-permute-done((bf16[2,288,256]{2,1,0:T(8,128)(2,1)S(1)}, bf16[2,288,256]{2,1,0:T(8,128)(2,1)S(1)}, u32[]{:S(2)}, u32[]{:S(2)}) %collective-permute-start.13) | collective-permute-done | bytes 294944 | tf_op jit(solution)/shard_map/ppermute | solution.py:72
  121.9 2.7 fusion.60
  124.6 3.7 %fusion.6 = (bf16[576,1024]{1,0:T(8,128)(2,1)S(1)}, bf16[576,1024]{1,0:T(8,128)(2,1)S(1)}) fusion(f32[1024]{0:T(1024)S(1)} %add.555, bf16[1024,1024]{1,0:T(8,128)(2,1)S(1)} %bitcast.270, bf16[288,1024]{1,0:T(8,128)(2,1)} %collective-permute-done.17, bf16[288,1024]{1,0:T(8,128)(2,1)S(1)} %fusion.27), kind=kOutput, calls=%fused_computation.16 | convolution fusion | flops 1217396736 | bytes 5640192 | tf_op jit(solution)/shard_map/dot_general | solution.py:24
  128.3 9.2 %collective-permute-done.16 = bf16[288,1024]{1,0:T(8,128)(2,1)} collective-permute-done((bf16[288,1024]{1,0:T(8,128)(2,1)S(1)}, bf16[288,1024]{1,0:T(8,128)(2,1)}, u32[]{:S(2)}, u32[]{:S(2)}) %collective-permute-start.16) | collective-permute-done | bytes 589856 | tf_op jit(solution)/shard_map/ppermute | solution.py:72
  139.8 2.0 multiply_convert_fusion.2
  143.5 1.9 collective-permute-done.19
  147.5 13.5 %collective-permute-done.20 = bf16[288,1024]{1,0:T(8,128)(2,1)S(1)} collective-permute-done((bf16[288,1024]{1,0:T(8,128)(2,1)S(1)}, bf16[288,1024]{1,0:T(8,128)(2,1)S(1)}, u32[]{:S(2)}, u32[]{:S(2)}) %collective-permute-start.20) | collective-permute-done | bytes 589856 | tf_op jit(solution)/shard_map/ppermute | solution.py:72
  166.3 2.5 convert_reduce_fusion.2
  168.8 11.2 %collective-permute-done.22 = bf16[288,1024]{1,0:T(8,128)(2,1)S(1)} collective-permute-done((bf16[288,1024]{1,0:T(8,128)(2,1)S(1)}, bf16[288,1024]{1,0:T(8,128)(2,1)S(1)}, u32[]{:S(2)}, u32[]{:S(2)}) %collective-permute-start.22) | collective-permute-done | bytes 589856 | tf_op jit(solution)/shard_map/ppermute | solution.py:72
  180.1 2.0 collective-permute-done.24
  182.1 2.4 convert_reduce_fusion.1
  189.2 2.3 add_convert_fusion.1
  191.8 3.4 convolution_convert_fusion.1
  207.1 8.2 %shard_map.274 = bf16[1024,2048]{1,0:T(8,128)(2,1)S(1)} custom-call(bf16[576,1024]{1,0:T(8,128)(2,1)S(1)} %copy-done.14, bf16[576,1024]{1,0:T(8,128)(2,1)S(1)} %copy-done.16, bf16[576,1024]{1,0:T(8,128)(2,1)S(1)} %copy-done.3, bf16[576,1024]{1,0:T(8,128)(2,1)S(1)} %copy-done.9, bf16[576,1024]{1,0:T(8,128)(2,1)S(1)} %pad_maximum_fusion.1.refs_4_, ...), custom_call_target="tpu_custom_call" | custom-call | flops 4831838208 | bytes 13631488 | tf_op jit(solution)/shard_map/pallas_call | solution.py:399
  215.3 2.0 copy-done
  217.3 4.3 %multiply_reduce_fusion = (bf16[1024]{0:T(1024)(128)(2,1)S(1)}, f32[288]{0:T(512)S(1)}, f32[288]{0:T(512)S(1)}, bf16[1024]{0:T(1024)(128)(2,1)S(1)}, f32[288,1024]{1,0:T(8,128)S(1)}, /*index=5*/bf16[1,288,1024]{2,1,0:T(8,128)(2,1)}) fusion(f32[288,1024]{1,0:T(8,128)} %copy-done.23, f32[288]{0:T(512)S(1)} %add_rsqrt_fusion.1, ...), kind=kLoop, calls=%fused_computation.63 | loop fusion | flops 7665088 | bytes 6513664 | tf_op jit(solution)/shard_map/reduce_sum | solution.py:50
  225.3 2.0 shard_map.276
  233.8 7.9 %collective-permute-done.28 = bf16[2,288,256]{2,1,0:T(8,128)(2,1)S(1)} collective-permute-done((bf16[2,288,256]{2,1,0:T(8,128)(2,1)}, bf16[2,288,256]{2,1,0:T(8,128)(2,1)S(1)}, u32[]{:S(2)}, u32[]{:S(2)}) %collective-permute-start.28) | collective-permute-done | bytes 294944 | tf_op jit(solution)/shard_map/ppermute | solution.py:72
  241.7 2.1 fusion.1
  243.9 1.8 collective-permute-start.31
  247.4 14.9 %shard_map.275.refs_1_ = bf16[1152,768]{1,0:T(8,128)(2,1)S(1)} custom-call(s32[6]{0:T(128)S(1)} %pad_add_fusion.bounds, bf16[1152,768]{1,0:T(8,128)(2,1)S(1)} %copy-done.21, bf16[1152,256]{1,0:T(8,128)(2,1)S(1)} %copy-done.5, bf16[1152,256]{1,0:T(8,128)(2,1)S(1)} %bitcast.247, f32[4,1152]{1,0:T(4,128)S(1)} %get-tuple-element.59.log_ref, ...), custom_call_target="tpu_custom_call" | custom-call | flops 3397386240 | bytes 4718592 | tf_op jit(solution)/shard_map/pallas_call | solution.py:352
  264.2 2.0 convolution_convert_fusion
  266.3 3.5 shard_map.277
  270.8 2.6 collective-permute-start.38
  273.8 2.1 collective-permute-start.36
  276.3 10.0 %collective-permute-done.38 = bf16[592,256]{1,0:T(8,128)(2,1)S(1)} collective-permute-done((bf16[592,256]{1,0:T(8,128)(2,1)S(1)}, bf16[592,256]{1,0:T(8,128)(2,1)S(1)}, u32[]{:S(2)}, u32[]{:S(2)}) %collective-permute-start.38) | collective-permute-done | bytes 303136 | tf_op jit(solution)/shard_map/ppermute | solution.py:80
  289.8 7.0 %collective-permute-done.37 = bf16[592,256]{1,0:T(8,128)(2,1)S(1)} collective-permute-done((bf16[592,256]{1,0:T(8,128)(2,1)S(1)}, bf16[592,256]{1,0:T(8,128)(2,1)S(1)}, u32[]{:S(2)}, u32[]{:S(2)}) %collective-permute-start.37) | collective-permute-done | bytes 303136 | tf_op jit(solution)/shard_map/ppermute | solution.py:80
  298.7 6.3 %collective-permute-done.36 = bf16[592,256]{1,0:T(8,128)(2,1)S(1)} collective-permute-done((bf16[592,256]{1,0:T(8,128)(2,1)S(1)}, bf16[592,256]{1,0:T(8,128)(2,1)S(1)}, u32[]{:S(2)}, u32[]{:S(2)}) %collective-permute-start.36) | collective-permute-done | bytes 303136 | tf_op jit(solution)/shard_map/ppermute | solution.py:80
  305.0 3.5 collective-permute-done.40
  311.3 15.2 %collective-permute-done.41 = bf16[592,256]{1,0:T(8,128)(2,1)S(1)} collective-permute-done((bf16[592,256]{1,0:T(8,128)(2,1)S(1)}, bf16[592,256]{1,0:T(8,128)(2,1)S(1)}, u32[]{:S(2)}, u32[]{:S(2)}) %collective-permute-start.41) | collective-permute-done | bytes 303136 | tf_op jit(solution)/shard_map/ppermute | solution.py:86
  326.9 3.0 collective-permute-start.42
  331.2 1.8 collective-permute-done.42
  334.6 3.5 reduce-scatter.2.cloned.1.call-done
  338.1 1.9 slice_convert_fusion
  340.0 2.4 collective-permute-start.44
  343.9 2.1 collective-permute-done.44
  (405 shorter events, 84.9 us)
Async XLA Ops:
  7.2 114.7 %all-gather.3.cloned.1.call-start = ((), (), s32[]{:S(2)}) async-start(), calls=%async_computation.2 | async-start | bytes 4718592 | tf_op jit(solution)/shard_map/all_gather | solution.py:494
  10.2 11.8 %collective-permute-start.2 = (bf16[2,48,1792]{2,1,0:T(8,128)(2,1)S(1)}, bf16[2,48,1792]{2,1,0:T(8,128)(2,1)S(1)}, u32[]{:S(2)}, u32[]{:S(2)}) collective-permute-start(bf16[2,48,1792]{2,1,0:T(8,128)(2,1)S(1)} %get-tuple-element.126), channel_id=1, source_target_pairs={{0,2},{1,3},{2,0},{3,1},{4,6},{5,7},{6,4},{7,5},{8,10},{9,11},{10,... | collective-permute-start | bytes 1032200 | tf_op jit(solution)/shard_map/ppermute | solution.py:72
  13.2 9.5 %collective-permute-start.4 = (bf16[32,1024]{1,0:T(8,128)(2,1)S(1)}, bf16[32,1024]{1,0:T(8,128)(2,1)S(1)}, u32[]{:S(2)}, u32[]{:S(2)}) collective-permute-start(bf16[32,1024]{1,0:T(8,128)(2,1)S(1)} %copy-done.43), channel_id=1, source_target_pairs={{0,2},{1,3},{2,0},{3,1},{4,6},{5,7},{6,4},{7,5},{8,10},{9,11},{10,... | collective-permute-start | bytes 196616 | tf_op jit(solution)/shard_map/ppermute | solution.py:72
  22.0 1.7 collective-permute-start.3
  24.2 10.0 %collective-permute-start.5 = (bf16[656,256]{1,0:T(8,128)(2,1)S(1)}, bf16[656,256]{1,0:T(8,128)(2,1)S(1)}, u32[]{:S(2)}, u32[]{:S(2)}) collective-permute-start(bf16[656,256]{1,0:T(8,128)(2,1)S(1)} %constant_dynamic-update-slice_fusion.refs_0_), channel_id=1, source_target_pairs={{0,4},{4,0},{8,12},{12,8},{16,20},{20,16},{24,28},{28,24},{1,5},{5... | collective-permute-start | bytes 1007624 | tf_op jit(solution)/shard_map/ppermute | solution.py:80
  26.0 11.5 %collective-permute-start.6 = (bf16[656,256]{1,0:T(8,128)(2,1)S(1)}, bf16[656,256]{1,0:T(8,128)(2,1)S(1)}, u32[]{:S(2)}, u32[]{:S(2)}) collective-permute-start(bf16[656,256]{1,0:T(8,128)(2,1)S(1)} %constant_dynamic-update-slice_fusion.refs_0_), channel_id=1, source_target_pairs={{0,8},{4,12},{8,16},{12,20},{16,24},{20,28},{24,0},{28,4},{1,9},{5... | collective-permute-start | bytes 1007624 | tf_op jit(solution)/shard_map/ppermute | solution.py:86
  38.4 299.7 %reduce-scatter.2.cloned.1.call-start = ((), (), s32[]{:S(2)}) async-start(), calls=%async_computation.1 | async-start | bytes 4718592 | tf_op jit(solution)/shard_map/reduce_scatter | solution.py:567
  38.5 17.4 %collective-permute-start.1 = (bf16[288,1024]{1,0:T(8,128)(2,1)S(1)}, bf16[288,1024]{1,0:T(8,128)(2,1)S(1)}, u32[]{:S(2)}, u32[]{:S(2)}) collective-permute-start(bf16[288,1024]{1,0:T(8,128)(2,1)S(1)} %bitcast.296), channel_id=1, source_target_pairs={{0,2},{1,3},{2,0},{3,1},{4,6},{5,7},{6,4},{7,5},{8,10},{9,11},{10,... | collective-permute-start | bytes 1769480 | tf_op jit(solution)/shard_map/ppermute | solution.py:72
  40.0 18.4 %collective-permute-start = (bf16[288,1024]{1,0:T(8,128)(2,1)S(1)}, bf16[288,1024]{1,0:T(8,128)(2,1)}, u32[]{:S(2)}, u32[]{:S(2)}) collective-permute-start(bf16[288,1024]{1,0:T(8,128)(2,1)S(1)} %bitcast.297), channel_id=1, source_target_pairs={{0,1},{1,0},{2,3},{3,2},{4,5},{5,4},{6,7},{7,6},{8,9},{9,8},{10,11... | collective-permute-start | bytes 1769480 | tf_op jit(solution)/shard_map/ppermute | solution.py:68
  40.2 13.3 %collective-permute-start.7 = (bf16[656,256]{1,0:T(8,128)(2,1)S(1)}, bf16[656,256]{1,0:T(8,128)(2,1)S(1)}, u32[]{:S(2)}, u32[]{:S(2)}) collective-permute-start(bf16[656,256]{1,0:T(8,128)(2,1)S(1)} %collective-permute-done.6.refs_2_), channel_id=1, source_target_pairs={{0,4},{4,0},{8,12},{12,8},{16,20},{20,16},{24,28},{28,24},{1,5},{5... | collective-permute-start | bytes 1007624 | tf_op jit(solution)/shard_map/ppermute | solution.py:80
  40.7 15.1 %collective-permute-start.8 = (bf16[656,256]{1,0:T(8,128)(2,1)S(1)}, bf16[656,256]{1,0:T(8,128)(2,1)S(1)}, u32[]{:S(2)}, u32[]{:S(2)}) collective-permute-start(bf16[656,256]{1,0:T(8,128)(2,1)S(1)} %collective-permute-done.6.refs_2_), channel_id=1, source_target_pairs={{0,8},{4,12},{8,16},{12,20},{16,24},{20,28},{24,0},{28,4},{1,9},{5... | collective-permute-start | bytes 1007624 | tf_op jit(solution)/shard_map/ppermute | solution.py:86
  55.9 22.4 %collective-permute-start.9 = (bf16[288,1024]{1,0:T(8,128)(2,1)S(1)}, bf16[288,1024]{1,0:T(8,128)(2,1)}, u32[]{:S(2)}, u32[]{:S(2)}) collective-permute-start(bf16[288,1024]{1,0:T(8,128)(2,1)S(1)} %collective-permute-done.1), channel_id=1, source_target_pairs={{0,1},{1,0},{2,3},{3,2},{4,5},{5,4},{6,7},{7,6},{8,9},{9,8},{10,11... | collective-permute-start | bytes 1769480 | tf_op jit(solution)/shard_map/ppermute | solution.py:68
  56.3 10.3 %collective-permute-start.10 = (bf16[656,256]{1,0:T(8,128)(2,1)S(1)}, bf16[656,256]{1,0:T(8,128)(2,1)S(1)}, u32[]{:S(2)}, u32[]{:S(2)}) collective-permute-start(bf16[656,256]{1,0:T(8,128)(2,1)S(1)} %collective-permute-done.8.refs_4_), channel_id=1, source_target_pairs={{0,4},{4,0},{8,12},{12,8},{16,20},{20,16},{24,28},{28,24},{1,5},{5... | collective-permute-start | bytes 1007624 | tf_op jit(solution)/shard_map/ppermute | solution.py:80
  57.9 18.8 %collective-permute-start.11 = (bf16[656,256]{1,0:T(8,128)(2,1)S(1)}, bf16[656,256]{1,0:T(8,128)(2,1)S(1)}, u32[]{:S(2)}, u32[]{:S(2)}) collective-permute-start(bf16[656,256]{1,0:T(8,128)(2,1)S(1)} %collective-permute-done.8.refs_4_), channel_id=1, source_target_pairs={{0,8},{4,12},{8,16},{12,20},{16,24},{20,28},{24,0},{28,4},{1,9},{5... | collective-permute-start | bytes 1007624 | tf_op jit(solution)/shard_map/ppermute | solution.py:86
  76.7 15.2 %collective-permute-start.12 = (bf16[656,256]{1,0:T(8,128)(2,1)S(1)}, bf16[656,256]{1,0:T(8,128)(2,1)S(1)}, u32[]{:S(2)}, u32[]{:S(2)}) collective-permute-start(bf16[656,256]{1,0:T(8,128)(2,1)S(1)} %collective-permute-done.11.refs_6_), channel_id=1, source_target_pairs={{0,4},{4,0},{8,12},{12,8},{16,20},{20,16},{24,28},{28,24},{1,5},{5... | collective-permute-start | bytes 1007624 | tf_op jit(solution)/shard_map/ppermute | solution.py:80
  109.0 6.8 %collective-permute-start.13 = (bf16[2,288,256]{2,1,0:T(8,128)(2,1)S(1)}, bf16[2,288,256]{2,1,0:T(8,128)(2,1)S(1)}, u32[]{:S(2)}, u32[]{:S(2)}) collective-permute-start(bf16[2,288,256]{2,1,0:T(8,128)(2,1)S(1)} %get-tuple-element.134), channel_id=1, source_target_pairs={{0,2},{1,3},{2,0},{3,1},{4,6},{5,7},{6,4},{7,5},{8,10},{9,11},{10,... | collective-permute-start | bytes 884744 | tf_op jit(solution)/shard_map/ppermute | solution.py:72
  109.8 8.5 %collective-permute-start.15 = (bf16[16,1,32,1024]{3,2,1,0:T(8,128)(2,1)S(1)}, bf16[16,1,32,1024]{3,2,1,0:T(8,128)(2,1)S(1)}, u32[]{:S(2)}, u32[]{:S(2)}) collective-permute-start(bf16[16,1,32,1024]{3,2,1,0:T(8,128)(2,1)S(1)} %bitcast.240), channel_id=1, source_target_pairs={{0,1},{1,0},{2,3},{3,2},{4,5},{5,4},{6,7},{7,6},{8,9},{9,8},{10,11... | collective-permute-start | bytes 3145736 | tf_op jit(solution)/shard_map/ppermute | solution.py:68
  115.9 1.6 collective-permute-start.14
  121.4 3.2 collective-permute-start.17
  121.8 15.7 %collective-permute-start.16 = (bf16[288,1024]{1,0:T(8,128)(2,1)S(1)}, bf16[288,1024]{1,0:T(8,128)(2,1)}, u32[]{:S(2)}, u32[]{:S(2)}) collective-permute-start(bf16[288,1024]{1,0:T(8,128)(2,1)S(1)} %fusion.27), channel_id=1, source_target_pairs={{0,2},{1,3},{2,0},{3,1},{4,6},{5,7},{6,4},{7,5},{8,10},{9,11},{10,... | collective-permute-start | bytes 1769480 | tf_op jit(solution)/shard_map/ppermute | solution.py:72
  137.5 2.2 collective-permute-start.18
  143.3 2.1 collective-permute-start.19
  145.6 15.4 %collective-permute-start.20 = (bf16[288,1024]{1,0:T(8,128)(2,1)S(1)}, bf16[288,1024]{1,0:T(8,128)(2,1)S(1)}, u32[]{:S(2)}, u32[]{:S(2)}) collective-permute-start(bf16[288,1024]{1,0:T(8,128)(2,1)S(1)} %add_convert_fusion.3), channel_id=1, source_target_pairs={{0,2},{1,3},{2,0},{3,1},{4,6},{5,7},{6,4},{7,5},{8,10},{9,11},{10,... | collective-permute-start | bytes 1769480 | tf_op jit(solution)/shard_map/ppermute | solution.py:72
  147.4 13.6 %collective-permute-start.21 = (bf16[288,1024]{1,0:T(8,128)(2,1)S(1)}, bf16[288,1024]{1,0:T(8,128)(2,1)S(1)}, u32[]{:S(2)}, u32[]{:S(2)}) collective-permute-start(bf16[288,1024]{1,0:T(8,128)(2,1)S(1)} %slice.483), channel_id=1, source_target_pairs={{0,1},{1,0},{2,3},{3,2},{4,5},{5,4},{6,7},{7,6},{8,9},{9,8},{10,11... | collective-permute-start | bytes 1769480 | tf_op jit(solution)/shard_map/ppermute | solution.py:68
  164.2 2.1 collective-permute-start.23
  164.3 15.7 %collective-permute-start.22 = (bf16[288,1024]{1,0:T(8,128)(2,1)S(1)}, bf16[288,1024]{1,0:T(8,128)(2,1)S(1)}, u32[]{:S(2)}, u32[]{:S(2)}) collective-permute-start(bf16[288,1024]{1,0:T(8,128)(2,1)S(1)} %get-tuple-element.81), channel_id=1, source_target_pairs={{0,2},{1,3},{2,0},{3,1},{4,6},{5,7},{6,4},{7,5},{8,10},{9,11},{10,... | collective-permute-start | bytes 1769480 | tf_op jit(solution)/shard_map/ppermute | solution.py:72
  180.0 2.0 collective-permute-start.24
  186.8 2.3 collective-permute-start.25
  191.5 25.8 %collective-permute-start.26 = (bf16[288,1024]{1,0:T(8,128)(2,1)}, bf16[288,1024]{1,0:T(8,128)(2,1)}, u32[]{:S(2)}, u32[]{:S(2)}) collective-permute-start(bf16[288,1024]{1,0:T(8,128)(2,1)} %add_convert_fusion.1), channel_id=1, source_target_pairs={{0,2},{1,3},{2,0},{3,1},{4,6},{5,7},{6,4},{7,5},{8,10},{9,11},{10,... | collective-permute-start | bytes 1769480 | tf_op jit(solution)/shard_map/ppermute | solution.py:72
  196.0 21.3 %collective-permute-start.27 = (bf16[288,1024]{1,0:T(8,128)(2,1)}, bf16[288,1024]{1,0:T(8,128)(2,1)}, u32[]{:S(2)}, u32[]{:S(2)}) collective-permute-start(bf16[288,1024]{1,0:T(8,128)(2,1)} %slice.490), channel_id=1, source_target_pairs={{0,1},{1,0},{2,3},{3,2},{4,5},{5,4},{6,7},{7,6},{8,9},{9,8},{10,11... | collective-permute-start | bytes 1769480 | tf_op jit(solution)/shard_map/ppermute | solution.py:68
  229.4 12.3 %collective-permute-start.30 = (bf16[16,48,1024]{2,1,0:T(8,128)(2,1)}, bf16[16,48,1024]{2,1,0:T(8,128)(2,1)}, u32[]{:S(2)}, u32[]{:S(2)}) collective-permute-start(bf16[16,48,1024]{2,1,0:T(8,128)(2,1)} %fusion.13), channel_id=1, source_target_pairs={{0,1},{1,0},{2,3},{3,2},{4,5},{5,4},{6,7},{7,6},{8,9},{9,8},{10,11... | collective-permute-start | bytes 4718600 | tf_op jit(solution)/shard_map/ppermute | solution.py:68
  232.0 9.6 %collective-permute-start.28 = (bf16[2,288,256]{2,1,0:T(8,128)(2,1)}, bf16[2,288,256]{2,1,0:T(8,128)(2,1)S(1)}, u32[]{:S(2)}, u32[]{:S(2)}) collective-permute-start(bf16[2,288,256]{2,1,0:T(8,128)(2,1)} %get-tuple-element.130), channel_id=1, source_target_pairs={{0,2},{1,3},{2,0},{3,1},{4,6},{5,7},{6,4},{7,5},{8,10},{9,11},{10,... | collective-permute-start | bytes 884744 | tf_op jit(solution)/shard_map/ppermute | solution.py:72
  241.7 4.1 %collective-permute-start.29 = (bf16[2,1,288,256]{3,2,1,0:T(8,128)(2,1)S(1)}, bf16[2,1,288,256]{3,2,1,0:T(8,128)(2,1)S(1)}, u32[]{:S(2)}, u32[]{:S(2)}) collective-permute-start(bf16[2,1,288,256]{3,2,1,0:T(8,128)(2,1)S(1)} %fusion.36), channel_id=1, source_target_pairs={{0,1},{1,0},{2,3},{3,2},{4,5},{5,4},{6,7},{7,6},{8,9},{9,8},{10,11... | collective-permute-start | bytes 884744 | tf_op jit(solution)/shard_map/ppermute | solution.py:68
  243.9 20.0 %collective-permute-start.31 = (bf16[8,48,1024]{2,1,0:T(8,128)(2,1)S(1)}, bf16[8,48,1024]{2,1,0:T(8,128)(2,1)S(1)}, u32[]{:S(2)}, u32[]{:S(2)}) collective-permute-start(bf16[8,48,1024]{2,1,0:T(8,128)(2,1)S(1)} %dynamic-slice_bitcast_fusion), channel_id=1, source_target_pairs={{0,2},{1,3},{2,0},{3,1},{4,6},{5,7},{6,4},{7,5},{8,10},{9,11},{10,... | collective-permute-start | bytes 2359304 | tf_op jit(solution)/shard_map/ppermute | solution.py:72
  270.3 17.8 %collective-permute-start.32 = (bf16[288,1024]{1,0:T(8,128)(2,1)S(1)}, bf16[288,1024]{1,0:T(8,128)(2,1)S(1)}, u32[]{:S(2)}, u32[]{:S(2)}) collective-permute-start(bf16[288,1024]{1,0:T(8,128)(2,1)S(1)} %get-tuple-element.92), channel_id=1, source_target_pairs={{0,1},{1,0},{2,3},{3,2},{4,5},{5,4},{6,7},{7,6},{8,9},{9,8},{10,11... | collective-permute-start | bytes 1769480 | tf_op jit(solution)/shard_map/ppermute | solution.py:68
  270.8 15.5 %collective-permute-start.38 = (bf16[592,256]{1,0:T(8,128)(2,1)S(1)}, bf16[592,256]{1,0:T(8,128)(2,1)S(1)}, u32[]{:S(2)}, u32[]{:S(2)}) collective-permute-start(bf16[592,256]{1,0:T(8,128)(2,1)S(1)} %constant_dynamic-update-slice_fusion.68), channel_id=1, source_target_pairs={{0,4},{4,0},{8,12},{12,8},{16,20},{20,16},{24,28},{28,24},{1,5},{5... | collective-permute-start | bytes 909320 | tf_op jit(solution)/shard_map/ppermute | solution.py:80
  273.6 23.3 %collective-permute-start.37 = (bf16[592,256]{1,0:T(8,128)(2,1)S(1)}, bf16[592,256]{1,0:T(8,128)(2,1)S(1)}, u32[]{:S(2)}, u32[]{:S(2)}) collective-permute-start(bf16[592,256]{1,0:T(8,128)(2,1)S(1)} %constant_dynamic-update-slice_fusion.52), channel_id=1, source_target_pairs={{0,4},{4,0},{8,12},{12,8},{16,20},{20,16},{24,28},{28,24},{1,5},{5... | collective-permute-start | bytes 909320 | tf_op jit(solution)/shard_map/ppermute | solution.py:80
  273.8 31.2 %collective-permute-start.36 = (bf16[592,256]{1,0:T(8,128)(2,1)S(1)}, bf16[592,256]{1,0:T(8,128)(2,1)S(1)}, u32[]{:S(2)}, u32[]{:S(2)}) collective-permute-start(bf16[592,256]{1,0:T(8,128)(2,1)S(1)} %constant_dynamic-update-slice_fusion.36), channel_id=1, source_target_pairs={{0,4},{4,0},{8,12},{12,8},{16,20},{20,16},{24,28},{28,24},{1,5},{5... | collective-permute-start | bytes 909320 | tf_op jit(solution)/shard_map/ppermute | solution.py:80
  276.0 35.3 %collective-permute-start.35 = (bf16[592,256]{1,0:T(8,128)(2,1)S(1)}, bf16[592,256]{1,0:T(8,128)(2,1)S(1)}, u32[]{:S(2)}, u32[]{:S(2)}) collective-permute-start(bf16[592,256]{1,0:T(8,128)(2,1)S(1)} %constant_dynamic-update-slice_fusion.20), channel_id=1, source_target_pairs={{0,4},{4,0},{8,12},{12,8},{16,20},{20,16},{24,28},{28,24},{1,5},{5... | collective-permute-start | bytes 909320 | tf_op jit(solution)/shard_map/ppermute | solution.py:80
  286.5 10.6 %collective-permute-start.39 = (bf16[592,256]{1,0:T(8,128)(2,1)S(1)}, bf16[592,256]{1,0:T(8,128)(2,1)S(1)}, u32[]{:S(2)}, u32[]{:S(2)}) collective-permute-start(bf16[592,256]{1,0:T(8,128)(2,1)S(1)} %add_convert_fusion.5), channel_id=1, source_target_pairs={{0,8},{4,12},{8,16},{12,20},{16,24},{20,28},{24,0},{28,4},{1,9},{5... | collective-permute-start | bytes 909320 | tf_op jit(solution)/shard_map/ppermute | solution.py:86
  288.3 20.2 %collective-permute-start.33 = (bf16[288,1024]{1,0:T(8,128)(2,1)S(1)}, bf16[288,1024]{1,0:T(8,128)(2,1)S(1)}, u32[]{:S(2)}, u32[]{:S(2)}) collective-permute-start(bf16[288,1024]{1,0:T(8,128)(2,1)S(1)} %fusion.26), channel_id=1, source_target_pairs={{0,2},{1,3},{2,0},{3,1},{4,6},{5,7},{6,4},{7,5},{8,10},{9,11},{10,... | collective-permute-start | bytes 1769480 | tf_op jit(solution)/shard_map/ppermute | solution.py:72
  296.8 11.7 %collective-permute-start.34 = (bf16[288,1024]{1,0:T(8,128)(2,1)S(1)}, bf16[288,1024]{1,0:T(8,128)(2,1)S(1)}, u32[]{:S(2)}, u32[]{:S(2)}) collective-permute-start(bf16[288,1024]{1,0:T(8,128)(2,1)S(1)} %slice.381), channel_id=1, source_target_pairs={{0,1},{1,0},{2,3},{3,2},{4,5},{5,4},{6,7},{7,6},{8,9},{9,8},{10,11... | collective-permute-start | bytes 1769480 | tf_op jit(solution)/shard_map/ppermute | solution.py:68
  297.2 11.2 %collective-permute-start.40 = (bf16[592,256]{1,0:T(8,128)(2,1)S(1)}, bf16[592,256]{1,0:T(8,128)(2,1)S(1)}, u32[]{:S(2)}, u32[]{:S(2)}) collective-permute-start(bf16[592,256]{1,0:T(8,128)(2,1)S(1)} %add_convert_fusion.4), channel_id=1, source_target_pairs={{0,8},{4,12},{8,16},{12,20},{16,24},{20,28},{24,0},{28,4},{1,9},{5... | collective-permute-start | bytes 909320 | tf_op jit(solution)/shard_map/ppermute | solution.py:86
  309.8 16.7 %collective-permute-start.41 = (bf16[592,256]{1,0:T(8,128)(2,1)S(1)}, bf16[592,256]{1,0:T(8,128)(2,1)S(1)}, u32[]{:S(2)}, u32[]{:S(2)}) collective-permute-start(bf16[592,256]{1,0:T(8,128)(2,1)S(1)} %convert_add_fusion.4), channel_id=1, source_target_pairs={{0,8},{4,12},{8,16},{12,20},{16,24},{20,28},{24,0},{28,4},{1,9},{5... | collective-permute-start | bytes 909320 | tf_op jit(solution)/shard_map/ppermute | solution.py:86
  326.9 6.1 %collective-permute-start.42 = (bf16[2,48,768]{2,1,0:T(8,128)(2,1)S(1)}, bf16[2,48,768]{2,1,0:T(8,128)(2,1)S(1)}, u32[]{:S(2)}, u32[]{:S(2)}) collective-permute-start(bf16[2,48,768]{2,1,0:T(8,128)(2,1)S(1)} %get-tuple-element.147), channel_id=1, source_target_pairs={{0,2},{1,3},{2,0},{3,1},{4,6},{5,7},{6,4},{7,5},{8,10},{9,11},{10,... | collective-permute-start | bytes 442376 | tf_op jit(solution)/shard_map/ppermute | solution.py:72
  333.1 1.4 collective-permute-start.43
  340.0 6.0 %collective-permute-start.44 = (bf16[2,32,1024]{2,1,0:T(8,128)(2,1)S(1)}, bf16[2,32,1024]{2,1,0:T(8,128)(2,1)S(1)}, u32[]{:S(2)}, u32[]{:S(2)}) collective-permute-start(bf16[2,32,1024]{2,1,0:T(8,128)(2,1)S(1)} %get-tuple-element.151), channel_id=1, source_target_pairs={{0,2},{1,3},{2,0},{3,1},{4,6},{5,7},{6,4},{7,5},{8,10},{9,11},{10,... | collective-permute-start | bytes 393224 | tf_op jit(solution)/shard_map/ppermute | solution.py:72
  346.1 1.4 collective-permute-start.45
  (52 other events, 251.6 us)
Sparse Core Ops, SparseCore 0:
  38.5 82.5 all-gather.2
  233.9 104.1 reduce-scatter.1
